TPU v7x, 32 devices: a whole 2x2x4 slice. The times are simulated.
32 devices in a mesh: gx: 16 (over z, y, x), gy: 2 (over core).
Axes of the slice: x: 2, y: 2, z: 4, core: 2. Of those that a mesh axis runs over, the one named last changes fastest.
Arguments:
- displacement: float32 [3, 32, 128, 256], P(None, None, 'gx', 'gy'), may hold values from -6 to 6
- velocity: float32 [3, 32, 128, 256], P(None, None, 'gx', 'gy'), may hold values from -6 to 6
- slopes: float32 [2, 32, 128, 256], P(None, None, 'gx', 'gy'), may hold values from -0.5 to 0.5
- stretch: float32 [32, 128, 256], P(None, 'gx', 'gy'), may hold values from 0.6 to 1.4
- moduli: float32 [2, 32, 128, 256], P(None, None, 'gx', 'gy'), may hold values from 0.3 to 1
- buoyancy: float32 [32, 128, 256], P(None, 'gx', 'gy'), may hold values from 0.5 to 1.5
- probes: float32 [4, 128, 128], P(None, 'gy'), may hold values from -0.0048828125 to 0.0048828125
Outputs:
- final_displacement: float32 [3, 32, 128, 256], P(None, None, 'gx', 'gy')
- basis: float32 [64, 48, 128], P('gx', 'gy')
- factor: float32 [128, 128], replicated
All inputs are finite; a program needn't handle non-finite values.
Results may differ from a plain program's by a relative error of at most 0.0003.
Values sent between devices are 32-bit elements; how exact they have to be, the bound alone decides.
No kernel may reach another device: no remote copies, remote signals or barrier semaphores. Data moves between devices by JAX's collectives and lax.ppermute only.
A program may use at most 64 MiB of HBM per device.

v0:
```python
import math

import jax
import jax.numpy as jnp
from jax import lax
from jax.sharding import PartitionSpec as P

STEPS = 4


time_step = 0.12


def extended(block, sides, width):
    for axis, dim in sides:
        count = lax.axis_size(axis)
        forward = [(i, i + 1) for i in range(count - 1)]
        backward = [(target, source) for source, target in forward]
        low = lax.ppermute(
            lax.slice_in_dim(block, block.shape[dim] - width, None, axis=dim), axis, forward
        )
        high = lax.ppermute(lax.slice_in_dim(block, 0, width, axis=dim), axis, backward)
        block = jnp.concatenate([low, block, high], axis=dim)
    return block


def fourth(values, dimension):
    length_out = values.shape[dimension] - 4

    def segment(offset):
        return lax.slice_in_dim(values, offset, offset + length_out, axis=dimension)

    return (segment(0) - segment(4) + 8.0 * (segment(3) - segment(1))) / 12.0


def vertical(values):
    padded = jnp.pad(values, ((0, 0), (2, 2), (0, 0), (0, 0)))
    return fourth(padded, 1)


def gradient(padded, slope_x, slope_y, stretch):
    d_x = fourth(padded[:, :, :, 2:-2], 2)
    d_y = fourth(padded[:, :, 2:-2, :], 3)
    d_r = vertical(padded[:, :, 2:-2, 2:-2])
    return jnp.stack([d_x + slope_x * d_r, d_y + slope_y * d_r, stretch * d_r], axis=1)


def stresses(gradients, lame, shear):
    divergence = gradients[0, 0] + gradients[1, 1] + gradients[2, 2]
    pressure = lame * divergence
    return jnp.stack(
        [
            pressure + 2.0 * shear * gradients[0, 0],
            pressure + 2.0 * shear * gradients[1, 1],
            pressure + 2.0 * shear * gradients[2, 2],
            shear * (gradients[0, 1] + gradients[1, 0]),
            shear * (gradients[0, 2] + gradients[2, 0]),
            shear * (gradients[1, 2] + gradients[2, 1]),
        ]
    )


def forces(padded, slope_x, slope_y, stretch):
    d_x = fourth(padded[:, :, :, 2:-2], 2)
    d_y = fourth(padded[:, :, 2:-2, :], 3)
    d_r = vertical(padded[:, :, 2:-2, 2:-2])
    rows_x = (0, 3, 4)
    rows_y = (3, 1, 5)
    rows_z = (4, 5, 2)
    return jnp.stack(
        [
            d_x[rows_x[component]]
            + slope_x * d_r[rows_x[component]]
            + d_y[rows_y[component]]
            + slope_y * d_r[rows_y[component]]
            + stretch * d_r[rows_z[component]]
            for component in range(3)
        ]
    )


def lower_factor(gram):
    order = gram.shape[0]
    positions = jnp.arange(order, dtype=jnp.int32)

    def column_step(column_index, lower):
        picker = (positions == column_index).astype(jnp.float32)
        column = jnp.dot(gram, picker, precision=lax.Precision.HIGHEST)
        row_of = jnp.dot(picker, lower, precision=lax.Precision.HIGHEST)
        column = column - jnp.dot(lower, row_of, precision=lax.Precision.HIGHEST)
        pivot = jnp.sqrt(jnp.sum(column * picker))
        entries = jnp.where(
            positions > column_index,
            column / pivot,
            jnp.where(positions == column_index, pivot, 0.0),
        )
        return lower + entries[:, None] * picker[None, :]

    return lax.fori_loop(0, order, column_step, jnp.zeros_like(gram))


def lower_inverse(lower):
    order = lower.shape[0]
    positions = jnp.arange(order, dtype=jnp.int32)

    def row_step(row_index, inverse):
        picker = (positions == row_index).astype(jnp.float32)
        row_of = jnp.dot(picker, lower, precision=lax.Precision.HIGHEST)
        pivot = jnp.sum(row_of * picker)
        fresh = (picker - jnp.dot(row_of, inverse, precision=lax.Precision.HIGHEST)) / pivot
        return inverse + picker[:, None] * fresh[None, :]

    return lax.fori_loop(0, order, row_step, jnp.zeros_like(lower))


def orthogonalize(tall_block, gram):
    lower = lower_factor(gram)
    inverse = lower_inverse(lower)
    result = jnp.dot(
        tall_block, inverse.T, precision=lax.Precision.HIGHEST, preferred_element_type=jnp.float32
    )
    return (result, lower.T)


def shards(displacement, velocity, slopes, stretch, moduli, buoyancy, probes):
    previous = displacement - time_step * velocity
    current = displacement
    stacked = jnp.concatenate([slopes, stretch[None], moduli], 0)
    near_values = extended(stacked, (("gx", 2), ("gy", 3)), 2)
    for moment in range(STEPS):
        padded = extended(current, (("gx", 2), ("gy", 3)), 4)
        gradients = gradient(padded, near_values[0], near_values[1], near_values[2])
        stress = stresses(gradients, near_values[3], near_values[4])
        pushes = buoyancy * forces(stress, slopes[0], slopes[1], stretch)
        following = 2.0 * current - previous + time_step**2 * pushes
        velocities = (following - previous) / (2.0 * time_step)
        sampled = velocities[:, ::2, ::2, ::2]
        half_x = sampled.shape[2]
        rearranged = jnp.transpose(sampled, (2, 0, 1, 3)).reshape(-1, sampled.shape[3])
        sketch_term = jnp.dot(
            rearranged,
            probes[moment],
            precision=lax.Precision.HIGHEST,
            preferred_element_type=jnp.float32,
        ).reshape(half_x, -1, probes.shape[2])
        reduced = lax.psum_scatter(sketch_term, "gy", scatter_dimension=1, tiled=True)
        sketch = reduced if moment == 0 else sketch + reduced
        previous, current = (current, following)
    tall_block = sketch.reshape(-1, sketch.shape[2])
    rows_total = tall_block.shape[0] * lax.axis_size("gx") * lax.axis_size("gy")
    gram_local = jnp.dot(
        tall_block.T,
        tall_block,
        precision=lax.Precision.HIGHEST,
        preferred_element_type=jnp.float32,
    )
    gram_whole = lax.psum(gram_local, ("gx", "gy"))
    orthonormal, factor = orthogonalize(tall_block, gram_whole)
    basis = (math.sqrt(rows_total) * orthonormal).reshape(sketch.shape)
    return (current, basis, factor)


def solution(mesh):
    in_specs = (
        P(None, None, "gx", "gy"),
        P(None, None, "gx", "gy"),
        P(None, None, "gx", "gy"),
        P(None, "gx", "gy"),
        P(None, None, "gx", "gy"),
        P(None, "gx", "gy"),
        P(None, "gy", None),
    )
    out_specs = (P(None, None, "gx", "gy"), P("gx", "gy", None), P())
    return jax.shard_map(shards, mesh=mesh, in_specs=in_specs, out_specs=out_specs, check_vma=False)
```

profile of v0, /device:TPU:0, one launch (start us, length us, event | category | flops | bytes accessed | tf_op | source)
XLA Modules:
  0.0 986.6 jit_solution(11689234760993657389)
XLA Ops:
  10.5 6.2 collective-permute-start
  19.4 5.5 collective-permute-start.4
  43.4 4.6 pad_maximum_fusion
  54.7 3.8 collective-permute-start.6
  64.2 3.5 fusion.87
  68.5 4.9 fusion.56
  80.6 4.2 collective-permute-start.8
  88.7 5.4 collective-permute-done.9
  108.6 4.5 fusion.50
  123.1 6.4 collective-permute-start.12
  133.0 6.9 slice.1053
  148.5 4.3 collective-permute-start.14
  154.5 6.9 slice.1055
  170.0 3.5 fusion.69
  174.3 4.9 fusion.44
  193.4 6.1 collective-permute-start.16
  201.1 6.9 slice.1057
  224.2 3.5 fusion.60
  228.5 4.9 fusion.38
  241.4 7.0 slice.1059
  250.3 7.7 reduce-scatter.2.cloned.1.call-done
  261.0 123.6 %all-reduce.10.cloned.1.call-done = f32[128,128]{1,0:T(8,128)} async-done(((f32[128,128]{1,0:T(8,128)}), f32[128,128]{1,0:T(8,128)}) %all-reduce.10.cloned.1.call-update) | async-done | bytes 65552 | tf_op jit(solution)/shard_map/psum | solution.py:157
  384.6 363.3 %while.30 = (s32[]{:T(128)}, f32[128,128]{1,0:T(8,128)S(1)}, f32[128,128]{1,0:T(8,128)}, s32[]{:T(128)}, s32[]{:T(128)}) while((s32[]{:T(128)}, f32[128,128]{1,0:T(8,128)S(1)}, f32[128,128]{1,0:T(8,128)}, s32[]{:T(128)}, s32[]{:T(128)}) %tuple.121), condition=%wide.region_7.8_spmd.clone.clone, body=%wide.region_5.7_spmd.clone.clone.sunk | while | flops 673410 | bytes 332917 | solution.py:99
  748.6 230.0 %while.29 = (s32[]{:T(128)}, f32[128,128]{1,0:T(8,128)S(1)}, f32[128,128]{1,0:T(8,128)S(1)}, s32[]{:T(128)}, s32[]{:T(128)}) while((s32[]{:T(128)}, f32[128,128]{1,0:T(8,128)S(1)}, f32[128,128]{1,0:T(8,128)S(1)}, s32[]{:T(128)}, s32[]{:T(128)}) %tuple.124), condition=%wide.region_10.11_spmd.clone, body=%wide.region_8.10_spmd.clone.sunk | while | flops 460034 | bytes 265316 | solution.py:113
  (1557 shorter events, 637.4 us)
Async XLA Ops:
  7.2 250.8 %reduce-scatter.2.cloned.1.call-start = ((), (), s32[]{:S(2)}) async-start(), calls=%async_computation.2 | async-start | bytes 147456 | tf_op jit(solution)/shard_map/reduce_scatter | solution.py:146
  9.2 18.5 %collective-permute-start.1 = (f32[5,32,2,128]{3,1,2,0:T(8,128)}, f32[5,32,2,128]{3,1,2,0:T(8,128)}, u32[]{:S(2)}, u32[]{:S(2)}) collective-permute-start(f32[5,32,2,128]{3,1,2,0:T(8,128)} %copy.382), channel_id=1, source_target_pairs={{2,0},{4,2},{6,4},{8,6},{10,8},{12,10},{14,12},{16,14},{18,16},{20... | collective-permute-start | bytes 491528 | tf_op jit(solution)/shard_map/ppermute | solution.py:22
  10.5 15.8 %collective-permute-start = (f32[5,32,2,128]{3,1,2,0:T(8,128)S(1)}, f32[5,32,2,128]{3,1,2,0:T(8,128)}, u32[]{:S(2)}, u32[]{:S(2)}) collective-permute-start(f32[5,32,2,128]{3,1,2,0:T(8,128)S(1)} %copy.381), channel_id=1, source_target_pairs={{0,2},{2,4},{4,6},{6,8},{8,10},{10,12},{12,14},{14,16},{16,18},{18... | collective-permute-start | bytes 491528 | tf_op jit(solution)/shard_map/ppermute | solution.py:19
  17.4 32.7 %collective-permute-start.5 = (f32[3,32,4,128]{3,1,2,0:T(8,128)}, f32[3,32,4,128]{3,1,2,0:T(8,128)}, u32[]{:S(2)}, u32[]{:S(2)}) collective-permute-start(f32[3,32,4,128]{3,1,2,0:T(8,128)} %copy.384), channel_id=1, source_target_pairs={{2,0},{4,2},{6,4},{8,6},{10,8},{12,10},{14,12},{16,14},{18,16},{20... | collective-permute-start | bytes 589832 | tf_op jit(solution)/shard_map/ppermute | solution.py:22
  19.4 28.6 %collective-permute-start.4 = (f32[3,32,4,128]{3,1,2,0:T(8,128)}, f32[3,32,4,128]{3,1,2,0:T(8,128)}, u32[]{:S(2)}, u32[]{:S(2)}) collective-permute-start(f32[3,32,4,128]{3,1,2,0:T(8,128)} %copy.383), channel_id=1, source_target_pairs={{0,2},{2,4},{4,6},{6,8},{8,10},{10,12},{12,14},{14,16},{16,18},{18... | collective-permute-start | bytes 589832 | tf_op jit(solution)/shard_map/ppermute | solution.py:19
  31.5 11.9 %collective-permute-start.2 = (f32[5,32,12,2]{1,3,2,0:T(2,128)}, f32[5,32,12,2]{1,3,2,0:T(2,128)}, u32[]{:S(2)}, u32[]{:S(2)}) collective-permute-start(f32[5,32,12,2]{1,3,2,0:T(2,128)} %get-tuple-element.285), channel_id=1, source_target_pairs={{0,1},{2,3},{4,5},{6,7},{8,9},{10,11},{12,13},{14,15},{16,17},{18,... | collective-permute-start | bytes 46088 | tf_op jit(solution)/shard_map/ppermute | solution.py:19
  33.4 10.0 %collective-permute-start.3 = (f32[5,32,12,2]{1,3,2,0:T(2,128)}, f32[5,32,12,2]{1,3,2,0:T(2,128)}, u32[]{:S(2)}, u32[]{:S(2)}) collective-permute-start(f32[5,32,12,2]{1,3,2,0:T(2,128)} %get-tuple-element.286), channel_id=1, source_target_pairs={{1,0},{3,2},{5,4},{7,6},{9,8},{11,10},{13,12},{15,14},{17,16},{19,... | collective-permute-start | bytes 46088 | tf_op jit(solution)/shard_map/ppermute | solution.py:22
  36.6 40.2 %copy-start.25 = (f32[32,8,128]{0,2,1:T(8,128)}, f32[32,8,128]{0,2,1:T(8,128)S(1)}, u32[]{:S(2)}) copy-start(f32[32,8,128]{0,2,1:T(8,128)S(1)} %copy.331) | copy-start | bytes 393220
  53.2 7.2 collective-permute-start.7
  54.7 5.8 collective-permute-start.6
  80.6 7.9 collective-permute-start.8
  85.0 9.1 collective-permute-start.9
  94.4 4.4 collective-permute-start.11
  95.7 4.0 collective-permute-start.10
  123.1 17.7 %collective-permute-start.12 = (f32[3,32,4,128]{3,1,2,0:T(8,128)}, f32[3,32,4,128]{3,1,2,0:T(8,128)}, u32[]{:S(2)}, u32[]{:S(2)}) collective-permute-start(f32[3,32,4,128]{3,1,2,0:T(8,128)} %copy.348), channel_id=1, source_target_pairs={{0,2},{2,4},{4,6},{6,8},{8,10},{10,12},{12,14},{14,16},{16,18},{18... | collective-permute-start | bytes 589832 | tf_op jit(solution)/shard_map/ppermute | solution.py:19
  131.6 11.3 %collective-permute-start.13 = (f32[3,32,4,128]{3,1,2,0:T(8,128)}, f32[3,32,4,128]{3,1,2,0:T(8,128)}, u32[]{:S(2)}, u32[]{:S(2)}) collective-permute-start(f32[3,32,4,128]{3,1,2,0:T(8,128)} %copy.349), channel_id=1, source_target_pairs={{2,0},{4,2},{6,4},{8,6},{10,8},{12,10},{14,12},{16,14},{18,16},{20... | collective-permute-start | bytes 589832 | tf_op jit(solution)/shard_map/ppermute | solution.py:22
  147.3 15.0 %collective-permute-start.15 = (f32[3,32,16,4]{1,2,3,0:T(8,128)}, f32[3,32,16,4]{1,2,3,0:T(8,128)}, u32[]{:S(2)}, u32[]{:S(2)}) collective-permute-start(f32[3,32,16,4]{1,2,3,0:T(8,128)} %copy.353), channel_id=1, source_target_pairs={{1,0},{3,2},{5,4},{7,6},{9,8},{11,10},{13,12},{15,14},{17,16},{19,... | collective-permute-start | bytes 73736 | tf_op jit(solution)/shard_map/ppermute | solution.py:22
  148.5 14.6 %collective-permute-start.14 = (f32[3,32,16,4]{1,2,3,0:T(8,128)}, f32[3,32,16,4]{1,2,3,0:T(8,128)}, u32[]{:S(2)}, u32[]{:S(2)}) collective-permute-start(f32[3,32,16,4]{1,2,3,0:T(8,128)} %copy.352), channel_id=1, source_target_pairs={{0,1},{2,3},{4,5},{6,7},{8,9},{10,11},{12,13},{14,15},{16,17},{18,... | collective-permute-start | bytes 73736 | tf_op jit(solution)/shard_map/ppermute | solution.py:19
  192.1 18.8 %collective-permute-start.17 = (f32[3,32,4,128]{3,1,2,0:T(8,128)}, f32[3,32,4,128]{3,1,2,0:T(8,128)}, u32[]{:S(2)}, u32[]{:S(2)}) collective-permute-start(f32[3,32,4,128]{3,1,2,0:T(8,128)} %copy.362), channel_id=1, source_target_pairs={{2,0},{4,2},{6,4},{8,6},{10,8},{12,10},{14,12},{16,14},{18,16},{20... | collective-permute-start | bytes 589832 | tf_op jit(solution)/shard_map/ppermute | solution.py:22
  193.4 15.4 %collective-permute-start.16 = (f32[3,32,4,128]{3,1,2,0:T(8,128)}, f32[3,32,4,128]{3,1,2,0:T(8,128)}, u32[]{:S(2)}, u32[]{:S(2)}) collective-permute-start(f32[3,32,4,128]{3,1,2,0:T(8,128)} %copy.361), channel_id=1, source_target_pairs={{0,2},{2,4},{4,6},{6,8},{8,10},{10,12},{12,14},{14,16},{16,18},{18... | collective-permute-start | bytes 589832 | tf_op jit(solution)/shard_map/ppermute | solution.py:19
  214.2 5.4 collective-permute-start.19
  215.5 4.1 collective-permute-start.18
  250.2 134.4 %all-reduce.10.cloned.1.call-start = ((), (), s32[]{:S(2)}) async-start(), calls=%async_computation.1 | async-start | bytes 131072 | tf_op jit(solution)/shard_map/psum | solution.py:157
  259.8 718.9 %copy-start.55 = (f32[4,24,128]{2,1,0:T(8,128)S(1)}, f32[4,24,128]{2,1,0:T(8,128)}, u32[]{:S(2)}) copy-start(f32[4,24,128]{2,1,0:T(8,128)} %reduce-scatter.2.cloned.1.call-done) | copy-start | bytes 147460
  (59 other events, 376.0 us)
Sparse Core Ops, SparseCore 0:
  250.3 7.5 reduce-scatter.1
  264.1 120.4 all-reduce.9
where the time goes:
time: 1000 us; the launch traced here: 987 us
  matrix products  478 us (48%)
  waiting for transfers between devices  139 us (14%)
  other arithmetic  116 us (12%)
  loops' own time  98.3 us (10%)
  local copies, waits for them, and re-layouts  81.5 us (8%)
  starting transfers between devices  58 us (6%)
  between operations  15.7 us (2%)
    dot_general x128, matrix products, column_step(): column = jnp.dot(gram, picker, precision=lax.Precision.HIGHEST)  124 us
    psum x1, waiting for transfers between devices, shards(): gram_whole = lax.psum(gram_local, ('gx', 'gy'))  124 us
    dot_general x128, matrix products, column_step(): column = column - jnp.dot(lower, row_of, precision=lax.Precision.HIGHEST)  108 us
    dot_general x128, matrix products, row_step(): jnp.dot(row_of, inverse, precision=lax.Precision.HIGHEST)  107 us
    dot_general x128, matrix products, row_step(): row_of = jnp.dot(picker, lower, precision=lax.Precision.HIGHEST)  105 us
    another operation x1, loops' own time, lower_factor(): return lax.fori_loop(0, order, column_step, jnp.zeros_like(gram))  94 us
    ppermute x10, starting transfers between devices, extended(): lax.ppermute(lax.slice_in_dim(block, block.shape[dim] - width, None, axis...  44.4 us
    div x8, other arithmetic, fourth(): return (segment(0) - segment(4) + 8.0 * (segment(3) - segment(1))) / 12.0  32.5 us
  transfers between devices with their start and end apart: 22, of which 5 were waited for; matrix products, arithmetic and copies ran while one was open for 6% of the time, Pallas kernels for 0%

commit v1 on v0

v1 whole, which is shorter than its diff:
```python
import math

import jax
import jax.numpy as jnp
from jax import lax
from jax.experimental import pallas as pl
from jax.experimental.pallas import tpu as pltpu
from jax.sharding import PartitionSpec as P

STEPS = 4
SUB = 8

time_step = 0.12


def roll(value, shift, axis=-1):
    axis = axis % value.ndim
    shift = shift % value.shape[axis]
    return value if shift == 0 else pltpu.roll(value, shift, axis)


def lanes_of(shape):
    return lax.broadcasted_iota(jnp.int32, shape, len(shape) - 1)


def layer_derivative(value):
    groups = value.shape[0] // SUB
    parts = [value[SUB * v : SUB * (v + 1)] for v in range(groups)]
    sub = lax.broadcasted_iota(jnp.int32, parts[0].shape, 0)
    shifted = {}

    def at(v):
        if 0 <= v < groups:
            return parts[v]
        if v not in shifted:
            if v >= groups:
                shifted[v] = jnp.where(sub < SUB - 1, roll(parts[v - groups], -1, 0), 0.0)
            else:
                shifted[v] = jnp.where(sub > 0, roll(parts[v + groups], 1, 0), 0.0)
        return shifted[v]

    return jnp.concatenate(
        [at(v - 2) - at(v + 2) + 8.0 * (at(v + 1) - at(v - 1)) for v in range(groups)], 0
    )


def band_matrix(count):
    row = lax.broadcasted_iota(jnp.int32, (count, count), 0)
    col = lax.broadcasted_iota(jnp.int32, (count, count), 1)
    away = row - col
    band = jnp.where(
        away == -2,
        1.0,
        jnp.where(away == 2, -1.0, jnp.where(away == 1, 8.0, jnp.where(away == -1, -8.0, 0.0))),
    )
    return band.astype(jnp.bfloat16)


def banded(value, band):
    high = value.astype(jnp.bfloat16)
    low = (value - high.astype(jnp.float32)).astype(jnp.bfloat16)
    return jnp.dot(high, band, preferred_element_type=jnp.float32) + jnp.dot(
        low, band, preferred_element_type=jnp.float32
    )


def edge_terms(edge, window):
    w = lanes_of(edge.shape) % window
    up_2, up_3 = roll(edge, 2), roll(edge, 3)
    down_2, down_3 = roll(edge, -2), roll(edge, -3)
    right = jnp.where(w == 7, 8.0 * up_3, 0.0) - up_2
    left = down_2 - jnp.where(w == 8, 8.0 * down_3, 0.0)
    return jnp.where((w == 6) | (w == 7), right, left)


def edge_spread(terms, place, window):
    count = terms.shape[-1]
    lane = lanes_of(terms.shape)
    return jnp.where((lane < 2) | (lane >= count - 2), roll(terms, count - 2 - window * place - 6), 0.0)


def edge_message(load, x_count, rows, y_count):
    window = y_count // x_count
    place = lanes_of((rows, y_count)) // window
    message = None
    for x in range(x_count):
        moved = roll(load(x), window * x + 4)
        message = moved if message is None else jnp.where(place == x, moved, message)
    return message


def corner_message(messages, first, window):
    place = lanes_of(messages[0].shape) // (2 * window)
    packed = None
    for c, message in enumerate(messages):
        moved = roll(message, 2 * window * c - window * first)
        packed = moved if packed is None else jnp.where(place == c, moved, packed)
    return packed


def edge_tile(own, from_left, from_right, has_left, has_right, window):
    w = lanes_of(own.shape) % window
    halo = jnp.where(w < 8, from_right * has_right, roll(from_left, 8) * has_left)
    mine = jnp.where(w < 4, own, roll(own, 8))
    return jnp.where((w >= 4) & (w < 12), halo, mine)


def begin_kernel(u_ref, low_ref, high_ref, edge_ref, up_ref, down_ref):
    comps, half, rows, y_count = low_ref.shape
    x_count = 2 * half
    window = y_count // x_count
    groups = rows // SUB
    messages = []
    for c in range(comps):

        def load(x):
            return jnp.concatenate(
                [
                    u_ref[c, pl.ds(x_count * v + x, SUB, stride=groups * x_count), :]
                    for v in range(groups)
                ],
                0,
            )

        slabs = [load(x) for x in range(x_count)]
        for x in range(x_count):
            (low_ref if x < half else high_ref)[c, x % half] = slabs[x]
        message = edge_message(lambda x: slabs[x], x_count, rows, y_count)
        edge_ref[c] = message
        messages.append(message)
    up_ref[...] = corner_message(messages, x_count - 2, window)
    down_ref[...] = corner_message(messages, 0, window)


def metric_kernel(
    u_ref, v_ref, slope_ref, stretch_ref, moduli_ref, buoyancy_ref,
    before_low, before_high, metric_ref, first_ref, last_ref, edge_ref, push_ref,
):
    comps, half, rows, y_count = before_low.shape
    x_count = 2 * half
    groups = rows // SUB

    def load(ref, *index):
        def at(x):
            return jnp.concatenate(
                [
                    ref[(*index, pl.ds(x_count * v + x, SUB, stride=groups * x_count), slice(None))]
                    for v in range(groups)
                ],
                0,
            )

        return at

    fields = [
        (load(slope_ref, 0), 1.0),
        (load(slope_ref, 1), 1.0),
        (load(stretch_ref), 1.0),
        (load(moduli_ref, 0), 1.0 / 12.0),
        (load(moduli_ref, 1), 1.0 / 12.0),
    ]
    for m, (at, scale) in enumerate(fields):
        slabs = [at(x) * scale if scale != 1.0 else at(x) for x in range(x_count)]
        for x in range(x_count):
            metric_ref[m, x] = slabs[x]
        for k in range(2):
            first_ref[m, k] = slabs[k]
            last_ref[m, k] = slabs[x_count - 2 + k]
        edge_ref[m] = edge_message(lambda x: slabs[x], x_count, rows, y_count)
    at = load(buoyancy_ref)
    for x in range(x_count):
        push_ref[x] = at(x) * (time_step**2 / 12.0)
    for c in range(comps):
        at, rate = load(u_ref, c), load(v_ref, c)
        for x in range(x_count):
            (before_low if x < half else before_high)[c, x % half] = at(x) - time_step * rate(x)


def all_stresses(grads, lame, shear):
    pressure = lame * (grads[0][0] + grads[1][1] + grads[2][2])
    twice = shear + shear
    return (
        pressure + twice * grads[0][0],
        pressure + twice * grads[1][1],
        pressure + twice * grads[2][2],
        shear * (grads[0][1] + grads[1][0]),
        shear * (grads[0][2] + grads[2][0]),
        shear * (grads[1][2] + grads[2][1]),
    )


def make_step(sides, first_step, last_step):
    def kernel(*refs):
        refs = list(refs)

        def take(count):
            out = refs[:count]
            del refs[:count]
            return out

        (side_ref,) = take(1)
        low_ref, high_ref, below_ref, above_ref = take(4)
        before_low, before_high = take(2)
        metric_ref, push_ref, metric_below, metric_above = take(4)
        (edge_ref,) = take(1)
        edge_in = take(sides)
        up_in = take(sides)
        down_in = take(sides)
        (metric_edge,) = take(1)
        metric_edge_in = take(sides)
        (probe_ref,) = take(1)
        sketch_in = None if first_step else take(1)[0]
        if last_step:
            out_ref, sketch_ref = take(2)
        else:
            out_low, out_high, out_edge, out_up, out_down, sketch_ref = take(6)
        ext, dyu, s_x, s_o, dys, rates, spread_probe = take(7)

        comps, half, rows, y_count = low_ref.shape
        x_count = 2 * half
        window = y_count // x_count
        groups = rows // SUB
        has_left, has_right = side_ref[0], side_ref[1]
        band = band_matrix(y_count)
        edge_shape = (rows, y_count)
        lane = lanes_of(edge_shape)
        w = lane % window
        place = lane // window

        for c in range(comps):
            for k in range(half):
                ext[c, k] = below_ref[c, k]
                ext[c, half + k] = low_ref[c, k]
                ext[c, 2 * half + k] = high_ref[c, k]
                ext[c, 3 * half + k] = above_ref[c, k]

        edges, corners = [], []
        for c in range(comps):
            edge = edge_tile(edge_ref[c], edge_in[0][c], edge_in[-1][c], has_left, has_right, window)
            size = 2 * window

            def beside(which):
                return jnp.where(
                    place >= x_count - 2,
                    roll(up_in[which][...], (x_count - 2) * window - size * c),
                    roll(down_in[which][...], -size * c),
                )

            corner = jnp.where(
                w < 8, beside(-1) * has_right, roll(beside(0), 8) * has_left
            )
            edges.append(edge)
            corners.append(corner)
            edge_add = edge_terms(edge, window)
            corner_add = edge_terms(corner, window)
            first, count = (half - 2, x_count + 4) if c < 2 else (half, x_count)
            flat = ext[c, first : first + count].reshape(count * rows, y_count)
            result = banded(flat, band)
            for k in range(count):
                x = first + k - half
                terms = edge_add if 0 <= x < x_count else corner_add
                dyu[c, first + k] = result[k * rows : (k + 1) * rows] + edge_spread(
                    terms, x % x_count, window
                )

        def gradients(at, metric, full):
            slope_x, slope_y, stretch = metric[:3]
            grads = []
            for c in range(comps):
                dr = layer_derivative(ext[c, at])
                dx = ext[c, at - 2] - ext[c, at + 2] + 8.0 * (ext[c, at + 1] - ext[c, at - 1])
                row = [dx + slope_x * dr, None, stretch * dr]
                if full or c < 2:
                    row[1] = dyu[c, at] + slope_y * dr
                else:
                    row[1] = dr
                grads.append(row)
            return grads

        def tile_row(x, carry):
            metric = [metric_ref[m, x] for m in range(5)]
            grads = gradients(x + half, metric, True)
            s11, s22, s33, s12, s13, s23 = all_stresses(grads, metric[3], metric[4])
            s_x[0, x + 2] = s11
            s_x[1, x + 2] = s12
            s_x[2, x + 2] = s13
            s_o[0, x] = s22
            s_o[1, x] = s23
            s_o[2, x] = s33
            return carry

        for k in range(2):
            for source, at in ((metric_below, half - 2 + k), (metric_above, half + x_count + k)):
                metric = [source[m, k] for m in range(5)]
                grads = gradients(at, metric, False)
                s11, _, _, s12, s13, _ = all_stresses(grads, metric[3], metric[4])
                s_x[0, at - half + 2] = s11
                s_x[1, at - half + 2] = s12
                s_x[2, at - half + 2] = s13
        lax.fori_loop(0, x_count, tile_row, 0)

        metric = [
            edge_tile(
                metric_edge[m], metric_edge_in[0][m], metric_edge_in[-1][m],
                has_left, has_right, window,
            )
            for m in range(5)
        ]
        grads = []
        for c in range(comps):
            edge, corner = edges[c], corners[c]

            def along(k):
                inside = (place + k < x_count) if k > 0 else (place + k >= 0)
                return jnp.where(inside, roll(edge, -window * k), roll(corner, -window * k))

            dr = layer_derivative(edge)
            if c < 2:
                dx = along(-2) - along(2) + 8.0 * (along(1) - along(-1))
            else:
                dx = dr
            dy = roll(edge, 2) - roll(edge, -2) + 8.0 * (roll(edge, -1) - roll(edge, 1))
            grads.append([dx + metric[0] * dr, dy + metric[1] * dr, metric[2] * dr])
        _, e22, _, e12, _, e23 = all_stresses(grads, metric[3], metric[4])

        for i, (edge, source) in enumerate(((e12, None), (e22, 0), (e23, 1))):
            value = s_x[1, 2 : 2 + x_count] if source is None else s_o[source]
            result = banded(value.reshape(x_count * rows, y_count), band)
            terms = edge_terms(edge, window)
            for x in range(x_count):
                dys[i, x] = result[x * rows : (x + 1) * rows] + edge_spread(terms, x, window)

        def update(x, keep):
            slope_x, slope_y, stretch = metric_ref[0, x], metric_ref[1, x], metric_ref[2, x]
            push = push_ref[x]
            r11, r12, r13 = (layer_derivative(s_x[k, x + 2]) for k in range(3))
            r22, r23, r33 = (layer_derivative(s_o[k, x]) for k in range(3))
            layers = ((r11, r12, r13), (r12, r22, r23), (r13, r23, r33))
            for c in range(comps):
                force = s_x[c, x] - s_x[c, x + 4] + 8.0 * (s_x[c, x + 3] - s_x[c, x + 1])
                force = force + slope_x * layers[c][0] + dys[c, x]
                force = force + slope_y * layers[c][1] + stretch * layers[c][2]
                keep(c, force * push)

        picked = groups // 2
        messages = [None] * comps
        for x in range(x_count):
            before = before_low if x < half else before_high

            def keep(c, change):
                past = before[c, x % half]
                following = 2.0 * ext[c, half + x] - past + change
                if last_step:
                    for v in range(groups):
                        out_ref[c, pl.ds(x_count * v + x, SUB, stride=groups * x_count), :] = (
                            following[SUB * v : SUB * (v + 1)]
                        )
                else:
                    (out_low if x < half else out_high)[c, x % half] = following
                    moved = roll(following, window * x + 4)
                    messages[c] = moved if x == 0 else jnp.where(place == x, moved, messages[c])
                if x % 2 == 0:
                    rate = (following - past) * (0.5 / time_step)
                    for v in range(0, groups, 2):
                        start = ((x // 2 * comps + c) * picked + v // 2) * SUB
                        rates[start : start + SUB] = rate[SUB * v : SUB * (v + 1)]

            update(x, keep)

        if not last_step:
            for c in range(comps):
                out_edge[c] = messages[c]
            out_up[...] = corner_message(messages, x_count - 2, window)
            out_down[...] = corner_message(messages, 0, window)

        spread_probe[...] = jnp.zeros_like(spread_probe)
        spread_probe[pl.ds(0, y_count // 2, stride=2), :] = probe_ref[...]
        sketch = jnp.dot(
            rates[...],
            spread_probe[...],
            precision=lax.Precision.HIGHEST,
            preferred_element_type=jnp.float32,
        )
        if sketch_in is not None:
            sketch = sketch + sketch_in[...]
        if last_step:
            for k in range(x_count // 2 * comps):
                for v in range(picked):
                    start = (k * picked + v) * SUB
                    sketch_ref[pl.ds(k * picked * SUB + v, SUB, stride=picked), :] = sketch[
                        start : start + SUB
                    ]
        else:
            sketch_ref[...] = sketch

    return kernel


def gram_kernel(first_ref, second_ref, sum_ref, gram_ref):
    total = first_ref[...] + second_ref[...]
    sum_ref[...] = total
    gram_ref[...] = lax.dot_general(
        total,
        total,
        (((0,), (0,)), ((), ())),
        precision=lax.Precision.HIGHEST,
        preferred_element_type=jnp.float32,
    )


def factor_kernel(scale):
    def kernel(side_ref, gram_ref, tall_ref, basis_ref, factor_ref):
        order = gram_ref.shape[0]
        blocks = order // SUB
        shape = (SUB, order)
        sub = lax.broadcasted_iota(jnp.int32, shape, 0)
        lane = lanes_of(shape)
        work = [gram_ref[SUB * q : SUB * (q + 1), :] for q in range(blocks)]
        other = [jnp.where(lane == sub + SUB * q, 1.0, 0.0) for q in range(blocks)]
        for j in range(order):
            p, k = divmod(j, SUB)
            columns = [jnp.broadcast_to(work[q][:, j : j + 1], shape) for q in range(p, blocks)]
            pivot = jnp.broadcast_to(columns[0][k : k + 1, :], shape)
            inverse = 1.0 / pivot
            row = jnp.broadcast_to(work[p][k : k + 1, :], shape) * inverse
            row_other = jnp.broadcast_to(other[p][k : k + 1, :], shape) * inverse
            for q in range(p, blocks):
                column = columns[q - p]
                if q == p:
                    column = jnp.where(sub > k, column, 0.0)
                work[q] = work[q] - column * row
                other[q] = other[q] - column * row_other
            root = lax.rsqrt(pivot)
            work[p] = jnp.where(sub == k, work[p] * root, work[p])
            other[p] = jnp.where(sub == k, other[p] * root, other[p])
        for q in range(blocks):
            factor_ref[SUB * q : SUB * (q + 1), :] = jnp.where(
                lane >= sub + SUB * q, work[q], 0.0
            )
        inverse_lower = jnp.concatenate(other, 0) * scale
        count, kept = basis_ref.shape[0], basis_ref.shape[1]
        start = pl.multiple_of(side_ref[0] * kept, SUB)
        for k in range(count):
            basis_ref[k] = lax.dot_general(
                tall_ref[k, pl.ds(start, kept), :],
                inverse_lower,
                (((1,), (1,)), ((), ())),
                precision=lax.Precision.HIGHEST,
                preferred_element_type=jnp.float32,
            )

    return kernel


def f32(*shape):
    return jax.ShapeDtypeStruct(shape, jnp.float32)


VMEM = pl.BlockSpec(memory_space=pltpu.MemorySpace.VMEM)
SMEM = pl.BlockSpec(memory_space=pltpu.MemorySpace.SMEM)


def call(kernel, outs, name, ins, scalars=0, scratch=(), flops=0):
    size = sum(math.prod(x.shape) * 4 for x in (*ins, *outs))
    return pl.pallas_call(
        kernel,
        out_shape=outs,
        in_specs=[SMEM] * scalars + [VMEM] * (len(ins) - scalars),
        out_specs=[VMEM] * len(outs),
        scratch_shapes=list(scratch),
        cost_estimate=pl.CostEstimate(flops=flops, bytes_accessed=size, transcendentals=0),
        name=name,
    )(*ins)


def butterfly(value, axis, last=False):
    count = lax.axis_size(axis)
    if count & (count - 1):
        total = lax.psum(value, axis)
        return (total, jnp.zeros_like(total)) if last else total
    bit = 1
    while bit < count:
        other = lax.ppermute(value, axis, [(i, i ^ bit) for i in range(count)])
        if last and 2 * bit == count:
            return value, other
        value = value + other
        bit *= 2
    return (value, jnp.zeros_like(value)) if last else value


def shards(displacement, velocity, slopes, stretch, moduli, buoyancy, probes):
    comps, layers, x_count, y_count = displacement.shape
    width = probes.shape[2]
    half = x_count // 2
    n_x, n_y = lax.axis_size("gx"), lax.axis_size("gy")
    side = lax.axis_index("gy")
    has = jnp.stack([side > 0, side < n_y - 1]).astype(jnp.float32)
    sides = 1 if n_y == 2 else 2

    def flat(array):
        return array.reshape(array.shape[:-3] + (layers * x_count, y_count))

    def along_x(value, step):
        pairs = [(i, i + step) for i in range(n_x) if 0 <= i + step < n_x]
        return lax.ppermute(value, "gx", pairs)

    def along_y(value):
        if sides == 1:
            return [lax.ppermute(value, "gy", [(0, 1), (1, 0)])]
        return [
            lax.ppermute(value, "gy", [(i, i + s) for i in range(n_y) if 0 <= i + s < n_y])
            for s in (1, -1)
        ]

    def diagonal(value, step):
        def pairs(moves):
            return [
                (i * n_y + k, (i + step) * n_y + k + s)
                for s in moves
                for i in range(n_x)
                for k in range(n_y)
                if 0 <= i + step < n_x and 0 <= k + s < n_y
            ]

        groups = [(1, -1)] if sides == 1 else [(1,), (-1,)]
        return [lax.ppermute(value, ("gx", "gy"), pairs(moves)) for moves in groups]

    u_flat = flat(displacement)
    part = f32(comps, half, layers, y_count)
    packed = f32(comps, layers, y_count)
    corner = f32(layers, y_count)
    low, high, edge, up, down = call(
        begin_kernel, [part, part, packed, corner, corner], "begin", [u_flat]
    )
    metric_rows = f32(5, 2, layers, y_count)
    before_low, before_high, metric, m_first, m_last, m_edge, push = call(
        metric_kernel,
        [
            part, part, f32(5, x_count, layers, y_count), metric_rows, metric_rows,
            f32(5, layers, y_count), f32(x_count, layers, y_count),
        ],
        "metrics",
        [u_flat, flat(velocity), flat(slopes), flat(stretch), flat(moduli), flat(buoyancy)],
    )
    m_below = along_x(m_last, 1)
    m_above = along_x(m_first, -1)
    m_edge_in = along_y(m_edge)

    sketch_rows = x_count // 2 * comps * (layers // 2)
    slab = (x_count, layers, y_count)
    scratch = [
        pltpu.VMEM((comps, 2 * x_count, layers, y_count), jnp.float32),
        pltpu.VMEM((comps, 2 * x_count, layers, y_count), jnp.float32),
        pltpu.VMEM((comps, x_count + 4, layers, y_count), jnp.float32),
        pltpu.VMEM((comps, *slab), jnp.float32),
        pltpu.VMEM((comps, *slab), jnp.float32),
        pltpu.VMEM((sketch_rows, y_count), jnp.float32),
        pltpu.VMEM((y_count, width), jnp.float32),
    ]
    sketch = []
    for moment in range(STEPS):
        last = moment == STEPS - 1
        below = along_x(high, 1)
        above = along_x(low, -1)
        edge_in = along_y(edge)
        up_in = diagonal(up, 1)
        down_in = diagonal(down, -1)
        outs = [f32(comps, layers * x_count, y_count)] if last else [part, part, packed, corner, corner]
        outs = outs + [f32(sketch_rows, width)]
        results = call(
            make_step(sides, moment == 0, last),
            outs,
            f"step_{moment}",
            [
                has, low, high, below, above, before_low, before_high, metric, push, m_below,
                m_above, edge, *edge_in, *up_in, *down_in, m_edge, *m_edge_in, probes[moment],
                *sketch,
            ],
            scalars=1,
            scratch=scratch,
            flops=30_000_000,
        )
        sketch = [results[-1]]
        if not last:
            before_low, before_high = low, high
            low, high, edge, up, down = results[:-1]
    final = results[0].reshape(displacement.shape)

    mine, theirs = butterfly(sketch[0], "gy", last=True)
    tall, gram = call(
        gram_kernel, [f32(sketch_rows, width), f32(width, width)], "gram", [mine, theirs]
    )
    gram = butterfly(gram, "gx")
    depth = comps * (layers // 2)
    rows_total = sketch_rows * n_x
    basis, factor = call(
        factor_kernel(math.sqrt(rows_total)),
        [f32(x_count // 2, depth // n_y, width), f32(width, width)],
        "factor",
        [side.reshape(1).astype(jnp.int32), gram, tall.reshape(x_count // 2, depth, width)],
        scalars=1,
    )
    return (final, basis, factor)


def solution(mesh):
    in_specs = (
        P(None, None, "gx", "gy"),
        P(None, None, "gx", "gy"),
        P(None, None, "gx", "gy"),
        P(None, "gx", "gy"),
        P(None, None, "gx", "gy"),
        P(None, "gx", "gy"),
        P(None, "gy", None),
    )
    out_specs = (P(None, None, "gx", "gy"), P("gx", "gy", None), P())
    return jax.shard_map(shards, mesh=mesh, in_specs=in_specs, out_specs=out_specs, check_vma=False)
```

time: 1000 us -> 148 us (0.15); the launches traced: 987 us -> 147 us
  matrix products: 478 us -> 0 us
  other arithmetic: 116 us -> 2.15 us
  waiting for transfers between devices: 139 us -> 29.8 us
  loops' own time: 98.3 us -> 0 us
  local copies, waits for them, and re-layouts: 81.5 us -> 4.26 us
  Pallas kernels: 0 us -> 43.4 us
  between operations: 15.7 us -> 1.04 us
    dot_general x646 -> x0, matrix products: 478 us -> none  [the longest x128 124 us: column_step(): column = jnp.dot(gram, picker, precision=lax.Precision.HIGHEST)]
    psum x1 -> x0, waiting for transfers between devices: 124 us -> none  [shards(): gram_whole = lax.psum(gram_local, ('gx', 'gy'))]
    another operation x2 -> x0, loops' own time: 98.3 us -> none  [the longest x1 94 us: lower_factor(): return lax.fori_loop(0, order, column_step, jnp.zeros_like(gram))]
    add x264 -> x4, other arithmetic: 49.7 us -> 1.5 us  [butterfly(): value = value + other]
    pallas_call x0 -> x8, Pallas kernels: none -> 43.4 us  [call(): pl.pallas_call(kernel, out_shape=outs, in_specs=[SMEM] * scalars + [VMEM]...]
    slice x28 -> x0, local copies, waits for them, and re-layouts: 40.9 us -> none  [the longest x4 27.8 us: shards(): sampled = velocities[:, ::2, ::2, ::2]]
    div x12 -> x0, other arithmetic: 40.1 us -> none  [the longest x8 32.5 us: fourth(): return (segment(0) - segment(4) + 8.0 * (segment(3) - segment(1))) / 12.0]
    ppermute x20 -> x28, waiting for transfers between devices: 8.01 us -> 29.8 us  [the longest x5 11.7 us: butterfly(): other = lax.ppermute(value, axis, [(i, i ^ bit) for i in range(count)])]
  transfers between devices with their start and end apart: 22 -> 28, of which waited for: 5 -> 14; matrix products, arithmetic and copies ran while one was open for 6% -> 1% of each run, Pallas kernels for 0% -> 2%
where the time goes in v1:
time: 148 us; the launch traced here: 147 us
  starting transfers between devices  66.4 us (45%)
  Pallas kernels  43.4 us (29%)
  waiting for transfers between devices  29.8 us (20%)
  local copies, waits for them, and re-layouts  4.26 us (3%)
  other arithmetic  2.15 us (1%)
    pallas_call x8, Pallas kernels, call(): pl.pallas_call(kernel, out_shape=outs, in_specs=[SMEM] * scalars + [VMEM]...  43.4 us
    ppermute x10, starting transfers between devices, along_x(): return lax.ppermute(value, 'gx', pairs)  31.3 us
    ppermute x8, starting transfers between devices, diagonal(): return [lax.ppermute(value, ('gx', 'gy'), pairs(moves)) for moves in groups]  24 us
    ppermute x5, waiting for transfers between devices, butterfly(): other = lax.ppermute(value, axis, [(i, i ^ bit) for i in range(count)])  11.7 us
    ppermute x8, waiting for transfers between devices, diagonal(): return [lax.ppermute(value, ('gx', 'gy'), pairs(moves)) for moves in groups]  11.7 us
    ppermute x5, starting transfers between devices, butterfly(): other = lax.ppermute(value, axis, [(i, i ^ bit) for i in range(count)])  9.67 us
    ppermute x10, waiting for transfers between devices, along_x(): return lax.ppermute(value, 'gx', pairs)  5.71 us
    unnamed x52, local copies, waits for them, and re-layouts  3.6 us
  transfers between devices with their start and end apart: 28, of which 14 were waited for; matrix products, arithmetic and copies ran while one was open for 1% of the time, Pallas kernels for 2%

profile of v1, /device:TPU:0, one launch (start us, length us, event | category | flops | bytes accessed | tf_op | source)
XLA Modules:
  0.0 147.0 jit_solution(8703723802168142052)
XLA Ops:
  2.6 4.3 %collective-permute-start.5 = (f32[32,128]{1,0:T(8,128)}, f32[32,128]{1,0:T(8,128)S(1)}, u32[]{:S(2)}, u32[]{:S(2)}) collective-permute-start(f32[32,128]{1,0:T(8,128)} %get-tuple-element.48), channel_id=1, source_target_pairs={{0,3},{2,5},{4,7},{6,9},{8,11},{10,13},{12,15},{14,17},{16,19},{18... | collective-permute-start | bytes 49160 | tf_op jit(solution)/shard_map/ppermute | solution.py:526
  10.2 4.8 %collective-permute-start = (f32[3,4,32,128]{3,2,1,0:T(8,128)}, f32[3,4,32,128]{3,2,1,0:T(8,128)S(1)}, u32[]{:S(2)}, u32[]{:S(2)}) collective-permute-start(f32[3,4,32,128]{3,2,1,0:T(8,128)} %get-tuple-element.40.refs_2_.refs_6_), channel_id=1, source_target_pairs={{0,2},{2,4},{4,6},{6,8},{8,10},{10,12},{12,14},{14,16},{16,18},{18... | collective-permute-start | bytes 589832 | tf_op jit(solution)/shard_map/ppermute | solution.py:505
  15.1 3.1 %metrics.1 = (f32[3,4,32,128]{3,2,1,0:T(8,128)}, f32[3,4,32,128]{3,2,1,0:T(8,128)}, f32[5,8,32,128]{3,2,1,0:T(8,128)}, f32[5,2,32,128]{3,2,1,0:T(8,128)}, f32[5,...) custom-call(f32[3,256,128]{2,1,0:T(8,128)} %bitcast.20, f32[3,256,128]{2,1,0:T(8,128)} %bitcast.21, ...), custom_call_target="tpu_custom_call" | custom-call | bytes 3162112 | tf_op jit(solution)/shard_map/metrics/pallas_call | solution.py:465
  18.2 4.8 %collective-permute-start.2 = (f32[5,2,32,128]{3,2,1,0:T(8,128)}, f32[5,2,32,128]{3,2,1,0:T(8,128)S(1)}, u32[]{:S(2)}, u32[]{:S(2)}) collective-permute-start(f32[5,2,32,128]{3,2,1,0:T(8,128)} %get-tuple-element.45), channel_id=1, source_target_pairs={{0,2},{2,4},{4,6},{6,8},{8,10},{10,12},{12,14},{14,16},{16,18},{18... | collective-permute-start | bytes 491528 | tf_op jit(solution)/shard_map/ppermute | solution.py:505
  27.8 4.4 %collective-permute-done.3.refs_10_ = f32[5,2,32,128]{3,2,1,0:T(8,128)S(1)} collective-permute-done((f32[5,2,32,128]{3,2,1,0:T(8,128)}, f32[5,2,32,128]{3,2,1,0:T(8,128)S(1)}, u32[]{:S(2)}, u32[]{:S(2)}) %collective-permute-start.3) | collective-permute-done | bytes 163872 | tf_op jit(solution)/shard_map/ppermute | solution.py:505
  33.0 4.2 %step_0.1 = (f32[3,4,32,128]{3,2,1,0:T(8,128)}, f32[3,4,32,128]{3,2,1,0:T(8,128)}, f32[3,32,128]{2,1,0:T(8,128)}, f32[32,128]{1,0:T(8,128)}, f32[32,128]{1,0:T(8,128)}, /*index=5*/f32[192,128]{1,0:T(8,128)}) custom-call(f32[2]{0:T(128)} %add_convert_fusion.refs_0_, f32[3,4,32,128]{3,2,1,0:T(8,128)} %get-tuple-element.39.refs_1_.refs_5_, ...), custom_call_target="tpu_custom_call" | custom-call | flops 30000000 | bytes 3194888 | tf_op jit(solution)/shard_map/step_0/pallas_call | solution.py:465
  38.5 4.9 %collective-permute-start.8 = (f32[3,4,32,128]{3,2,1,0:T(8,128)}, f32[3,4,32,128]{3,2,1,0:T(8,128)S(1)}, u32[]{:S(2)}, u32[]{:S(2)}) collective-permute-start(f32[3,4,32,128]{3,2,1,0:T(8,128)} %get-tuple-element.52.refs_2_.refs_6_), channel_id=1, source_target_pairs={{0,2},{2,4},{4,6},{6,8},{8,10},{10,12},{12,14},{14,16},{16,18},{18... | collective-permute-start | bytes 589832 | tf_op jit(solution)/shard_map/ppermute | solution.py:505
  43.5 4.9 %collective-permute-start.11 = (f32[32,128]{1,0:T(8,128)}, f32[32,128]{1,0:T(8,128)S(1)}, u32[]{:S(2)}, u32[]{:S(2)}) collective-permute-start(f32[32,128]{1,0:T(8,128)} %get-tuple-element.54), channel_id=1, source_target_pairs={{0,3},{2,5},{4,7},{6,9},{8,11},{10,13},{12,15},{14,17},{16,19},{18... | collective-permute-start | bytes 49160 | tf_op jit(solution)/shard_map/ppermute | solution.py:526
  54.5 4.2 %step_1.1 = (f32[3,4,32,128]{3,2,1,0:T(8,128)}, f32[3,4,32,128]{3,2,1,0:T(8,128)}, f32[3,32,128]{2,1,0:T(8,128)}, f32[32,128]{1,0:T(8,128)}, f32[32,128]{1,0:T(8,128)}, /*index=5*/f32[192,128]{1,0:T(8,128)}) custom-call(f32[2]{0:T(128)} %add_convert_fusion.refs_0_, f32[3,4,32,128]{3,2,1,0:T(8,128)} %get-tuple-element.51.refs_1_.refs_5_, ...), custom_call_target="tpu_custom_call" | custom-call | flops 30000000 | bytes 3293192 | tf_op jit(solution)/shard_map/step_1/pallas_call | solution.py:465
  60.0 4.9 %collective-permute-start.13 = (f32[3,4,32,128]{3,2,1,0:T(8,128)}, f32[3,4,32,128]{3,2,1,0:T(8,128)S(1)}, u32[]{:S(2)}, u32[]{:S(2)}) collective-permute-start(f32[3,4,32,128]{3,2,1,0:T(8,128)} %get-tuple-element.58.refs_2_.refs_6_), channel_id=1, source_target_pairs={{0,2},{2,4},{4,6},{6,8},{8,10},{10,12},{12,14},{14,16},{16,18},{18... | collective-permute-start | bytes 589832 | tf_op jit(solution)/shard_map/ppermute | solution.py:505
  65.3 4.7 %collective-permute-start.16 = (f32[32,128]{1,0:T(8,128)}, f32[32,128]{1,0:T(8,128)S(1)}, u32[]{:S(2)}, u32[]{:S(2)}) collective-permute-start(f32[32,128]{1,0:T(8,128)} %get-tuple-element.60), channel_id=1, source_target_pairs={{0,3},{2,5},{4,7},{6,9},{8,11},{10,13},{12,15},{14,17},{16,19},{18... | collective-permute-start | bytes 49160 | tf_op jit(solution)/shard_map/ppermute | solution.py:526
  71.3 3.3 %collective-permute-done.16.refs_13_ = f32[32,128]{1,0:T(8,128)S(1)} collective-permute-done((f32[32,128]{1,0:T(8,128)}, f32[32,128]{1,0:T(8,128)S(1)}, u32[]{:S(2)}, u32[]{:S(2)}) %collective-permute-start.16) | collective-permute-done | bytes 16416 | tf_op jit(solution)/shard_map/ppermute | solution.py:526
  76.0 4.3 %step_2.1 = (f32[3,4,32,128]{3,2,1,0:T(8,128)}, f32[3,4,32,128]{3,2,1,0:T(8,128)}, f32[3,32,128]{2,1,0:T(8,128)}, f32[32,128]{1,0:T(8,128)}, f32[32,128]{1,0:T(8,128)}, /*index=5*/f32[192,128]{1,0:T(8,128)}) custom-call(f32[2]{0:T(128)} %add_convert_fusion.refs_0_, f32[3,4,32,128]{3,2,1,0:T(8,128)} %get-tuple-element.57.refs_1_.refs_5_, ...), custom_call_target="tpu_custom_call" | custom-call | flops 30000000 | bytes 3293192 | tf_op jit(solution)/shard_map/step_2/pallas_call | solution.py:465
  81.6 5.3 %collective-permute-start.18 = (f32[3,4,32,128]{3,2,1,0:T(8,128)}, f32[3,4,32,128]{3,2,1,0:T(8,128)S(1)}, u32[]{:S(2)}, u32[]{:S(2)}) collective-permute-start(f32[3,4,32,128]{3,2,1,0:T(8,128)} %get-tuple-element.64.refs_2_), channel_id=1, source_target_pairs={{0,2},{2,4},{4,6},{6,8},{8,10},{10,12},{12,14},{14,16},{16,18},{18... | collective-permute-start | bytes 589832 | tf_op jit(solution)/shard_map/ppermute | solution.py:505
  87.1 4.7 %collective-permute-start.21 = (f32[32,128]{1,0:T(8,128)}, f32[32,128]{1,0:T(8,128)S(1)}, u32[]{:S(2)}, u32[]{:S(2)}) collective-permute-start(f32[32,128]{1,0:T(8,128)} %get-tuple-element.66), channel_id=1, source_target_pairs={{0,3},{2,5},{4,7},{6,9},{8,11},{10,13},{12,15},{14,17},{16,19},{18... | collective-permute-start | bytes 49160 | tf_op jit(solution)/shard_map/ppermute | solution.py:526
  93.3 3.1 %collective-permute-done.21.refs_13_ = f32[32,128]{1,0:T(8,128)S(1)} collective-permute-done((f32[32,128]{1,0:T(8,128)}, f32[32,128]{1,0:T(8,128)S(1)}, u32[]{:S(2)}, u32[]{:S(2)}) %collective-permute-start.21) | collective-permute-done | bytes 16416 | tf_op jit(solution)/shard_map/ppermute | solution.py:526
  97.9 4.3 %step_3.1 = (f32[3,256,128]{2,1,0:T(8,128)}, f32[192,128]{1,0:T(8,128)}) custom-call(f32[2]{0:T(128)} %add_convert_fusion.refs_0_, f32[3,4,32,128]{3,2,1,0:T(8,128)} %get-tuple-element.63.refs_1_, f32[3,4,32,128]{3,2,1,0:T(8,128)} %get-tuple-element.64.refs_2_, f32[3,4,32,128]{3,2,1,0:T(8,128)} %copy-done.7, f32[3,4,32,128]{3,2,1,0:T(8,128)} %copy-done.6, ...), custom_call_target="tpu_custom_call" | custom-call | flops 30000000 | bytes 3211272 | tf_op jit(solution)/shard_map/step_3/pallas_call | solution.py:465
  106.2 2.8 %collective-permute-start.24 = (f32[128,128]{1,0:T(8,128)}, f32[128,128]{1,0:T(8,128)S(1)}, u32[]{:S(2)}, u32[]{:S(2)}) collective-permute-start(f32[128,128]{1,0:T(8,128)} %get-tuple-element.71), channel_id=1, source_target_pairs={{0,2},{2,0},{4,6},{6,4},{8,10},{10,8},{12,14},{14,12},{16,18},{18,... | collective-permute-start | bytes 196616 | tf_op jit(solution)/shard_map/ppermute | solution.py:483
  109.1 2.8 %collective-permute-done.24 = f32[128,128]{1,0:T(8,128)S(1)} collective-permute-done((f32[128,128]{1,0:T(8,128)}, f32[128,128]{1,0:T(8,128)S(1)}, u32[]{:S(2)}, u32[]{:S(2)}) %collective-permute-start.24) | collective-permute-done | bytes 65568 | tf_op jit(solution)/shard_map/ppermute | solution.py:483
  112.7 2.4 %collective-permute-start.25 = (f32[128,128]{1,0:T(8,128)S(1)}, f32[128,128]{1,0:T(8,128)S(1)}, u32[]{:S(2)}, u32[]{:S(2)}) collective-permute-start(f32[128,128]{1,0:T(8,128)S(1)} %add.12), channel_id=1, source_target_pairs={{0,4},{2,6},{4,0},{6,2},{8,12},{10,14},{12,8},{14,10},{16,20},{18,... | collective-permute-start | bytes 196616 | tf_op jit(solution)/shard_map/ppermute | solution.py:483
  119.1 2.7 %collective-permute-done.26 = f32[128,128]{1,0:T(8,128)S(1)} collective-permute-done((f32[128,128]{1,0:T(8,128)S(1)}, f32[128,128]{1,0:T(8,128)S(1)}, u32[]{:S(2)}, u32[]{:S(2)}) %collective-permute-start.26) | collective-permute-done | bytes 65568 | tf_op jit(solution)/shard_map/ppermute | solution.py:483
  121.8 2.7 %collective-permute-start.27 = (f32[128,128]{1,0:T(8,128)S(1)}, f32[128,128]{1,0:T(8,128)S(1)}, u32[]{:S(2)}, u32[]{:S(2)}) collective-permute-start(f32[128,128]{1,0:T(8,128)S(1)} %add.14), channel_id=1, source_target_pairs={{0,16},{2,18},{4,20},{6,22},{8,24},{10,26},{12,28},{14,30},{16,0},... | collective-permute-start | bytes 196616 | tf_op jit(solution)/shard_map/ppermute | solution.py:483
  124.4 2.6 %collective-permute-done.27 = f32[128,128]{1,0:T(8,128)S(1)} collective-permute-done((f32[128,128]{1,0:T(8,128)S(1)}, f32[128,128]{1,0:T(8,128)S(1)}, u32[]{:S(2)}, u32[]{:S(2)}) %collective-permute-start.27) | collective-permute-done | bytes 65568 | tf_op jit(solution)/shard_map/ppermute | solution.py:483
  127.6 19.4 %factor.1 = (f32[4,24,128]{2,1,0:T(8,128)}, f32[128,128]{1,0:T(8,128)}) custom-call(s32[1]{0:T(128)} %bitcast.13.side_ref, f32[128,128]{1,0:T(8,128)} %add.15.gram_ref, f32[4,48,128]{2,1,0:T(8,128)} %bitcast.26), custom_call_target="tpu_custom_call" | custom-call | bytes 278532 | tf_op jit(solution)/shard_map/factor/pallas_call | solution.py:465
  (98 shorter events, 36.3 us)
Async XLA Ops:
  2.6 15.6 %collective-permute-start.5 = (f32[32,128]{1,0:T(8,128)}, f32[32,128]{1,0:T(8,128)S(1)}, u32[]{:S(2)}, u32[]{:S(2)}) collective-permute-start(f32[32,128]{1,0:T(8,128)} %get-tuple-element.48), channel_id=1, source_target_pairs={{0,3},{2,5},{4,7},{6,9},{8,11},{10,13},{12,15},{14,17},{16,19},{18... | collective-permute-start | bytes 49160 | tf_op jit(solution)/shard_map/ppermute | solution.py:526
  6.9 16.1 %collective-permute-start.6 = (f32[32,128]{1,0:T(8,128)}, f32[32,128]{1,0:T(8,128)S(1)}, u32[]{:S(2)}, u32[]{:S(2)}) collective-permute-start(f32[32,128]{1,0:T(8,128)} %get-tuple-element.49), channel_id=1, source_target_pairs={{2,1},{4,3},{6,5},{8,7},{10,9},{12,11},{14,13},{16,15},{18,17},{20... | collective-permute-start | bytes 49160 | tf_op jit(solution)/shard_map/ppermute | solution.py:526
  8.2 16.9 %collective-permute-start.4 = (f32[3,32,128]{2,1,0:T(8,128)}, f32[3,32,128]{2,1,0:T(8,128)S(1)}, u32[]{:S(2)}, u32[]{:S(2)}) collective-permute-start(f32[3,32,128]{2,1,0:T(8,128)} %get-tuple-element.47.refs_11_), channel_id=1, source_target_pairs={{0,1},{1,0},{2,3},{3,2},{4,5},{5,4},{6,7},{7,6},{8,9},{9,8},{10,11... | collective-permute-start | bytes 147464 | tf_op jit(solution)/shard_map/ppermute | solution.py:509
  9.0 23.3 %collective-permute-start.1 = (f32[3,4,32,128]{3,2,1,0:T(8,128)}, f32[3,4,32,128]{3,2,1,0:T(8,128)S(1)}, u32[]{:S(2)}, u32[]{:S(2)}) collective-permute-start(f32[3,4,32,128]{3,2,1,0:T(8,128)} %get-tuple-element.39.refs_1_.refs_5_), channel_id=1, source_target_pairs={{2,0},{4,2},{6,4},{8,6},{10,8},{12,10},{14,12},{16,14},{18,16},{20... | collective-permute-start | bytes 589832 | tf_op jit(solution)/shard_map/ppermute | solution.py:505
  10.2 22.0 %collective-permute-start = (f32[3,4,32,128]{3,2,1,0:T(8,128)}, f32[3,4,32,128]{3,2,1,0:T(8,128)S(1)}, u32[]{:S(2)}, u32[]{:S(2)}) collective-permute-start(f32[3,4,32,128]{3,2,1,0:T(8,128)} %get-tuple-element.40.refs_2_.refs_6_), channel_id=1, source_target_pairs={{0,2},{2,4},{4,6},{6,8},{8,10},{10,12},{12,14},{14,16},{16,18},{18... | collective-permute-start | bytes 589832 | tf_op jit(solution)/shard_map/ppermute | solution.py:505
  18.2 9.6 %collective-permute-start.2 = (f32[5,2,32,128]{3,2,1,0:T(8,128)}, f32[5,2,32,128]{3,2,1,0:T(8,128)S(1)}, u32[]{:S(2)}, u32[]{:S(2)}) collective-permute-start(f32[5,2,32,128]{3,2,1,0:T(8,128)} %get-tuple-element.45), channel_id=1, source_target_pairs={{0,2},{2,4},{4,6},{6,8},{8,10},{10,12},{12,14},{14,16},{16,18},{18... | collective-permute-start | bytes 491528 | tf_op jit(solution)/shard_map/ppermute | solution.py:505
  23.0 9.2 %collective-permute-start.3 = (f32[5,2,32,128]{3,2,1,0:T(8,128)}, f32[5,2,32,128]{3,2,1,0:T(8,128)S(1)}, u32[]{:S(2)}, u32[]{:S(2)}) collective-permute-start(f32[5,2,32,128]{3,2,1,0:T(8,128)} %get-tuple-element.46), channel_id=1, source_target_pairs={{2,0},{4,2},{6,4},{8,6},{10,8},{12,10},{14,12},{16,14},{18,16},{20... | collective-permute-start | bytes 491528 | tf_op jit(solution)/shard_map/ppermute | solution.py:505
  37.2 16.5 %collective-permute-start.9 = (f32[3,4,32,128]{3,2,1,0:T(8,128)}, f32[3,4,32,128]{3,2,1,0:T(8,128)S(1)}, u32[]{:S(2)}, u32[]{:S(2)}) collective-permute-start(f32[3,4,32,128]{3,2,1,0:T(8,128)} %get-tuple-element.51.refs_1_.refs_5_), channel_id=1, source_target_pairs={{2,0},{4,2},{6,4},{8,6},{10,8},{12,10},{14,12},{16,14},{18,16},{20... | collective-permute-start | bytes 589832 | tf_op jit(solution)/shard_map/ppermute | solution.py:505
  38.5 15.2 %collective-permute-start.8 = (f32[3,4,32,128]{3,2,1,0:T(8,128)}, f32[3,4,32,128]{3,2,1,0:T(8,128)S(1)}, u32[]{:S(2)}, u32[]{:S(2)}) collective-permute-start(f32[3,4,32,128]{3,2,1,0:T(8,128)} %get-tuple-element.52.refs_2_.refs_6_), channel_id=1, source_target_pairs={{0,2},{2,4},{4,6},{6,8},{8,10},{10,12},{12,14},{14,16},{16,18},{18... | collective-permute-start | bytes 589832 | tf_op jit(solution)/shard_map/ppermute | solution.py:505
  43.5 10.3 %collective-permute-start.10 = (f32[3,32,128]{2,1,0:T(8,128)}, f32[3,32,128]{2,1,0:T(8,128)S(1)}, u32[]{:S(2)}, u32[]{:S(2)}) collective-permute-start(f32[3,32,128]{2,1,0:T(8,128)} %get-tuple-element.53.refs_11_), channel_id=1, source_target_pairs={{0,1},{1,0},{2,3},{3,2},{4,5},{5,4},{6,7},{7,6},{8,9},{9,8},{10,11... | collective-permute-start | bytes 147464 | tf_op jit(solution)/shard_map/ppermute | solution.py:509
  43.5 8.1 %collective-permute-start.11 = (f32[32,128]{1,0:T(8,128)}, f32[32,128]{1,0:T(8,128)S(1)}, u32[]{:S(2)}, u32[]{:S(2)}) collective-permute-start(f32[32,128]{1,0:T(8,128)} %get-tuple-element.54), channel_id=1, source_target_pairs={{0,3},{2,5},{4,7},{6,9},{8,11},{10,13},{12,15},{14,17},{16,19},{18... | collective-permute-start | bytes 49160 | tf_op jit(solution)/shard_map/ppermute | solution.py:526
  48.5 5.3 %collective-permute-start.12 = (f32[32,128]{1,0:T(8,128)}, f32[32,128]{1,0:T(8,128)S(1)}, u32[]{:S(2)}, u32[]{:S(2)}) collective-permute-start(f32[32,128]{1,0:T(8,128)} %get-tuple-element.55), channel_id=1, source_target_pairs={{2,1},{4,3},{6,5},{8,7},{10,9},{12,11},{14,13},{16,15},{18,17},{20... | collective-permute-start | bytes 49160 | tf_op jit(solution)/shard_map/ppermute | solution.py:526
  58.7 16.5 %collective-permute-start.14 = (f32[3,4,32,128]{3,2,1,0:T(8,128)}, f32[3,4,32,128]{3,2,1,0:T(8,128)S(1)}, u32[]{:S(2)}, u32[]{:S(2)}) collective-permute-start(f32[3,4,32,128]{3,2,1,0:T(8,128)} %get-tuple-element.57.refs_1_.refs_5_), channel_id=1, source_target_pairs={{2,0},{4,2},{6,4},{8,6},{10,8},{12,10},{14,12},{16,14},{18,16},{20... | collective-permute-start | bytes 589832 | tf_op jit(solution)/shard_map/ppermute | solution.py:505
  60.0 15.2 %collective-permute-start.13 = (f32[3,4,32,128]{3,2,1,0:T(8,128)}, f32[3,4,32,128]{3,2,1,0:T(8,128)S(1)}, u32[]{:S(2)}, u32[]{:S(2)}) collective-permute-start(f32[3,4,32,128]{3,2,1,0:T(8,128)} %get-tuple-element.58.refs_2_.refs_6_), channel_id=1, source_target_pairs={{0,2},{2,4},{4,6},{6,8},{8,10},{10,12},{12,14},{14,16},{16,18},{18... | collective-permute-start | bytes 589832 | tf_op jit(solution)/shard_map/ppermute | solution.py:505
  65.0 10.3 %collective-permute-start.15 = (f32[3,32,128]{2,1,0:T(8,128)}, f32[3,32,128]{2,1,0:T(8,128)S(1)}, u32[]{:S(2)}, u32[]{:S(2)}) collective-permute-start(f32[3,32,128]{2,1,0:T(8,128)} %get-tuple-element.59.refs_11_), channel_id=1, source_target_pairs={{0,1},{1,0},{2,3},{3,2},{4,5},{5,4},{6,7},{7,6},{8,9},{9,8},{10,11... | collective-permute-start | bytes 147464 | tf_op jit(solution)/shard_map/ppermute | solution.py:509
  65.3 9.3 %collective-permute-start.16 = (f32[32,128]{1,0:T(8,128)}, f32[32,128]{1,0:T(8,128)S(1)}, u32[]{:S(2)}, u32[]{:S(2)}) collective-permute-start(f32[32,128]{1,0:T(8,128)} %get-tuple-element.60), channel_id=1, source_target_pairs={{0,3},{2,5},{4,7},{6,9},{8,11},{10,13},{12,15},{14,17},{16,19},{18... | collective-permute-start | bytes 49160 | tf_op jit(solution)/shard_map/ppermute | solution.py:526
  70.0 5.3 %collective-permute-start.17 = (f32[32,128]{1,0:T(8,128)}, f32[32,128]{1,0:T(8,128)S(1)}, u32[]{:S(2)}, u32[]{:S(2)}) collective-permute-start(f32[32,128]{1,0:T(8,128)} %get-tuple-element.61), channel_id=1, source_target_pairs={{2,1},{4,3},{6,5},{8,7},{10,9},{12,11},{14,13},{16,15},{18,17},{20... | collective-permute-start | bytes 49160 | tf_op jit(solution)/shard_map/ppermute | solution.py:526
  80.3 16.8 %collective-permute-start.19 = (f32[3,4,32,128]{3,2,1,0:T(8,128)}, f32[3,4,32,128]{3,2,1,0:T(8,128)S(1)}, u32[]{:S(2)}, u32[]{:S(2)}) collective-permute-start(f32[3,4,32,128]{3,2,1,0:T(8,128)} %get-tuple-element.63.refs_1_), channel_id=1, source_target_pairs={{2,0},{4,2},{6,4},{8,6},{10,8},{12,10},{14,12},{16,14},{18,16},{20... | collective-permute-start | bytes 589832 | tf_op jit(solution)/shard_map/ppermute | solution.py:505
  81.6 15.5 %collective-permute-start.18 = (f32[3,4,32,128]{3,2,1,0:T(8,128)}, f32[3,4,32,128]{3,2,1,0:T(8,128)S(1)}, u32[]{:S(2)}, u32[]{:S(2)}) collective-permute-start(f32[3,4,32,128]{3,2,1,0:T(8,128)} %get-tuple-element.64.refs_2_), channel_id=1, source_target_pairs={{0,2},{2,4},{4,6},{6,8},{8,10},{10,12},{12,14},{14,16},{16,18},{18... | collective-permute-start | bytes 589832 | tf_op jit(solution)/shard_map/ppermute | solution.py:505
  86.9 10.3 %collective-permute-start.20 = (f32[3,32,128]{2,1,0:T(8,128)}, f32[3,32,128]{2,1,0:T(8,128)S(1)}, u32[]{:S(2)}, u32[]{:S(2)}) collective-permute-start(f32[3,32,128]{2,1,0:T(8,128)} %get-tuple-element.65.refs_11_), channel_id=1, source_target_pairs={{0,1},{1,0},{2,3},{3,2},{4,5},{5,4},{6,7},{7,6},{8,9},{9,8},{10,11... | collective-permute-start | bytes 147464 | tf_op jit(solution)/shard_map/ppermute | solution.py:509
  87.1 9.3 %collective-permute-start.21 = (f32[32,128]{1,0:T(8,128)}, f32[32,128]{1,0:T(8,128)S(1)}, u32[]{:S(2)}, u32[]{:S(2)}) collective-permute-start(f32[32,128]{1,0:T(8,128)} %get-tuple-element.66), channel_id=1, source_target_pairs={{0,3},{2,5},{4,7},{6,9},{8,11},{10,13},{12,15},{14,17},{16,19},{18... | collective-permute-start | bytes 49160 | tf_op jit(solution)/shard_map/ppermute | solution.py:526
  91.9 5.3 %collective-permute-start.22 = (f32[32,128]{1,0:T(8,128)}, f32[32,128]{1,0:T(8,128)S(1)}, u32[]{:S(2)}, u32[]{:S(2)}) collective-permute-start(f32[32,128]{1,0:T(8,128)} %get-tuple-element.67), channel_id=1, source_target_pairs={{2,1},{4,3},{6,5},{8,7},{10,9},{12,11},{14,13},{16,15},{18,17},{20... | collective-permute-start | bytes 49160 | tf_op jit(solution)/shard_map/ppermute | solution.py:526
  106.2 5.7 %collective-permute-start.24 = (f32[128,128]{1,0:T(8,128)}, f32[128,128]{1,0:T(8,128)S(1)}, u32[]{:S(2)}, u32[]{:S(2)}) collective-permute-start(f32[128,128]{1,0:T(8,128)} %get-tuple-element.71), channel_id=1, source_target_pairs={{0,2},{2,0},{4,6},{6,4},{8,10},{10,8},{12,14},{14,12},{16,18},{18,... | collective-permute-start | bytes 196616 | tf_op jit(solution)/shard_map/ppermute | solution.py:483
  121.8 5.2 %collective-permute-start.27 = (f32[128,128]{1,0:T(8,128)S(1)}, f32[128,128]{1,0:T(8,128)S(1)}, u32[]{:S(2)}, u32[]{:S(2)}) collective-permute-start(f32[128,128]{1,0:T(8,128)S(1)} %add.14), channel_id=1, source_target_pairs={{0,16},{2,18},{4,20},{6,22},{8,24},{10,26},{12,28},{14,30},{16,0},... | collective-permute-start | bytes 196616 | tf_op jit(solution)/shard_map/ppermute | solution.py:483
  (30 other events, 64.1 us)

commit v2 on v1

--- a/solution.py
+++ b/solution.py
@@ -79,23 +79,14 @@
     return jnp.where((lane < 2) | (lane >= count - 2), roll(terms, count - 2 - window * place - 6), 0.0)
 
 
-def edge_message(load, x_count, rows, y_count):
+def edge_message(load, x_count, rows, y_count, which=None):
     window = y_count // x_count
     place = lanes_of((rows, y_count)) // window
     message = None
-    for x in range(x_count):
+    for x in which or range(x_count):
         moved = roll(load(x), window * x + 4)
         message = moved if message is None else jnp.where(place == x, moved, message)
     return message
-
-
-def corner_message(messages, first, window):
-    place = lanes_of(messages[0].shape) // (2 * window)
-    packed = None
-    for c, message in enumerate(messages):
-        moved = roll(message, 2 * window * c - window * first)
-        packed = moved if packed is None else jnp.where(place == c, moved, packed)
-    return packed
 
 
 def edge_tile(own, from_left, from_right, has_left, has_right, window):
@@ -105,12 +96,11 @@
     return jnp.where((w >= 4) & (w < 12), halo, mine)
 
 
-def begin_kernel(u_ref, low_ref, high_ref, edge_ref, up_ref, down_ref):
+def begin_kernel(u_ref, low_ref, high_ref, edge_ref):
     comps, half, rows, y_count = low_ref.shape
     x_count = 2 * half
     window = y_count // x_count
     groups = rows // SUB
-    messages = []
     for c in range(comps):
 
         def load(x):
@@ -125,11 +115,18 @@
         slabs = [load(x) for x in range(x_count)]
         for x in range(x_count):
             (low_ref if x < half else high_ref)[c, x % half] = slabs[x]
-        message = edge_message(lambda x: slabs[x], x_count, rows, y_count)
-        edge_ref[c] = message
-        messages.append(message)
-    up_ref[...] = corner_message(messages, x_count - 2, window)
-    down_ref[...] = corner_message(messages, 0, window)
+        edge_ref[c] = edge_message(lambda x: slabs[x], x_count, rows, y_count)
+
+
+def corner_kernel(below_ref, above_ref, corner_ref):
+    half, rows, y_count = below_ref.shape[1:]
+    x_count = 2 * half
+    for c in range(corner_ref.shape[0]):
+
+        def load(x):
+            return below_ref[c, x - half] if x >= half else above_ref[c, x]
+
+        corner_ref[c] = edge_message(load, x_count, rows, y_count, (0, 1, x_count - 2, x_count - 1))
 
 
 def metric_kernel(
@@ -204,8 +201,7 @@
         metric_ref, push_ref, metric_below, metric_above = take(4)
         (edge_ref,) = take(1)
         edge_in = take(sides)
-        up_in = take(sides)
-        down_in = take(sides)
+        corner_in = take(sides)
         (metric_edge,) = take(1)
         metric_edge_in = take(sides)
         (probe_ref,) = take(1)
@@ -213,7 +209,7 @@
         if last_step:
             out_ref, sketch_ref = take(2)
         else:
-            out_low, out_high, out_edge, out_up, out_down, sketch_ref = take(6)
+            out_low, out_high, out_edge, sketch_ref = take(4)
         ext, dyu, s_x, s_o, dys, rates, spread_probe = take(7)
 
         comps, half, rows, y_count = low_ref.shape
@@ -237,22 +233,16 @@
         edges, corners = [], []
         for c in range(comps):
             edge = edge_tile(edge_ref[c], edge_in[0][c], edge_in[-1][c], has_left, has_right, window)
-            size = 2 * window
-
-            def beside(which):
-                return jnp.where(
-                    place >= x_count - 2,
-                    roll(up_in[which][...], (x_count - 2) * window - size * c),
-                    roll(down_in[which][...], -size * c),
+            if c < 2:
+                corner = jnp.where(
+                    w < 8, corner_in[-1][c] * has_right, roll(corner_in[0][c], 8) * has_left
                 )
-
-            corner = jnp.where(
-                w < 8, beside(-1) * has_right, roll(beside(0), 8) * has_left
-            )
+                corner_add = edge_terms(corner, window)
+            else:
+                corner = corner_add = None
             edges.append(edge)
             corners.append(corner)
             edge_add = edge_terms(edge, window)
-            corner_add = edge_terms(corner, window)
             first, count = (half - 2, x_count + 4) if c < 2 else (half, x_count)
             flat = ext[c, first : first + count].reshape(count * rows, y_count)
             result = banded(flat, band)
@@ -370,8 +360,6 @@
         if not last_step:
             for c in range(comps):
                 out_edge[c] = messages[c]
-            out_up[...] = corner_message(messages, x_count - 2, window)
-            out_down[...] = corner_message(messages, 0, window)
 
         spread_probe[...] = jnp.zeros_like(spread_probe)
         spread_probe[pl.ds(0, y_count // 2, stride=2), :] = probe_ref[...]
@@ -468,6 +456,7 @@
         in_specs=[SMEM] * scalars + [VMEM] * (len(ins) - scalars),
         out_specs=[VMEM] * len(outs),
         scratch_shapes=list(scratch),
+        compiler_params=pltpu.CompilerParams(vmem_limit_bytes=24 * 2**20),
         cost_estimate=pl.CostEstimate(flops=flops, bytes_accessed=size, transcendentals=0),
         name=name,
     )(*ins)
@@ -512,26 +501,10 @@
             for s in (1, -1)
         ]
 
-    def diagonal(value, step):
-        def pairs(moves):
-            return [
-                (i * n_y + k, (i + step) * n_y + k + s)
-                for s in moves
-                for i in range(n_x)
-                for k in range(n_y)
-                if 0 <= i + step < n_x and 0 <= k + s < n_y
-            ]
-
-        groups = [(1, -1)] if sides == 1 else [(1,), (-1,)]
-        return [lax.ppermute(value, ("gx", "gy"), pairs(moves)) for moves in groups]
-
     u_flat = flat(displacement)
     part = f32(comps, half, layers, y_count)
     packed = f32(comps, layers, y_count)
-    corner = f32(layers, y_count)
-    low, high, edge, up, down = call(
-        begin_kernel, [part, part, packed, corner, corner], "begin", [u_flat]
-    )
+    low, high, edge = call(begin_kernel, [part, part, packed], "begin", [u_flat])
     metric_rows = f32(5, 2, layers, y_count)
     before_low, before_high, metric, m_first, m_last, m_edge, push = call(
         metric_kernel,
@@ -563,9 +536,11 @@
         below = along_x(high, 1)
         above = along_x(low, -1)
         edge_in = along_y(edge)
-        up_in = diagonal(up, 1)
-        down_in = diagonal(down, -1)
-        outs = [f32(comps, layers * x_count, y_count)] if last else [part, part, packed, corner, corner]
+        (corner,) = call(
+            corner_kernel, [f32(2, layers, y_count)], f"corner_{moment}", [below, above]
+        )
+        corner_in = along_y(corner)
+        outs = [f32(comps, layers * x_count, y_count)] if last else [part, part, packed]
         outs = outs + [f32(sketch_rows, width)]
         results = call(
             make_step(sides, moment == 0, last),
@@ -573,7 +548,7 @@
             f"step_{moment}",
             [
                 has, low, high, below, above, before_low, before_high, metric, push, m_below,
-                m_above, edge, *edge_in, *up_in, *down_in, m_edge, *m_edge_in, probes[moment],
+                m_above, edge, *edge_in, *corner_in, m_edge, *m_edge_in, probes[moment],
                 *sketch,
             ],
             scalars=1,
@@ -583,7 +558,7 @@
         sketch = [results[-1]]
         if not last:
             before_low, before_high = low, high
-            low, high, edge, up, down = results[:-1]
+            low, high, edge = results[:-1]
     final = results[0].reshape(displacement.shape)
 
     mine, theirs = butterfly(sketch[0], "gy", last=True)

time: 148 us -> 122 us (0.82)
  starting transfers between devices: 66.4 us -> 42.4 us
  waiting for transfers between devices: 29.8 us -> 43.3 us
  Pallas kernels: 43.4 us -> 30.3 us
  other arithmetic: 2.15 us -> 0.11 us
    ppermute x8 -> x0, starting transfers between devices: 24 us -> none  [diagonal(): return [lax.ppermute(value, ('gx', 'gy'), pairs(moves)) for moves in groups]]
    ppermute x10, waiting for transfers between devices: 5.71 us -> 27 us  [along_x(): return lax.ppermute(value, 'gx', pairs)]
    pallas_call x8 -> x12, Pallas kernels: 43.4 us -> 30.3 us  [call(): pl.pallas_call(kernel, out_shape=outs, in_specs=[SMEM] * scalars + [VMEM]...]
    ppermute x8 -> x0, waiting for transfers between devices: 11.7 us -> none  [diagonal(): return [lax.ppermute(value, ('gx', 'gy'), pairs(moves)) for moves in groups]]
    ppermute x5 -> x9, waiting for transfers between devices: 0.62 us -> 4.07 us  [along_y(): return [lax.ppermute(value, 'gy', [(0, 1), (1, 0)])]]
    unnamed x52 -> x14, local copies, waits for them, and re-layouts: 3.6 us -> 4.7 us
  transfers between devices with their start and end apart: 28 -> 24, of which waited for: 14 -> 17; matrix products, arithmetic and copies ran while one was open for 1% -> 0% of each run, Pallas kernels for 2% -> 1%
where the time goes in v2:
time: 122 us
  waiting for transfers between devices  43.3 us (35%)
  starting transfers between devices  42.4 us (35%)
  Pallas kernels  30.3 us (25%)
  local copies, waits for them, and re-layouts  4.71 us (4%)
    ppermute x10, starting transfers between devices, along_x(): return lax.ppermute(value, 'gx', pairs)  32.4 us
    pallas_call x12, Pallas kernels, call(): pl.pallas_call(kernel, out_shape=outs, in_specs=[SMEM] * scalars + [VMEM]...  30.3 us
    ppermute x10, waiting for transfers between devices, along_x(): return lax.ppermute(value, 'gx', pairs)  27 us
    ppermute x5, waiting for transfers between devices, butterfly(): other = lax.ppermute(value, axis, [(i, i ^ bit) for i in range(count)])  12.2 us
    ppermute x5, starting transfers between devices, butterfly(): other = lax.ppermute(value, axis, [(i, i ^ bit) for i in range(count)])  8.36 us
    unnamed x14, local copies, waits for them, and re-layouts  4.7 us
    ppermute x9, waiting for transfers between devices, along_y(): return [lax.ppermute(value, 'gy', [(0, 1), (1, 0)])]  4.07 us
  transfers between devices with their start and end apart: 24, of which 17 were waited for; matrix products, arithmetic and copies ran while one was open for 0% of the time, Pallas kernels for 1%

profile of v2, /device:TPU:0, one launch (start us, length us, event | category | flops | bytes accessed | tf_op | source)
XLA Modules:
  0.0 121.7 jit_solution(7888505926098703272)
XLA Ops:
  3.8 5.0 %collective-permute-start = (f32[3,4,32,128]{3,2,1,0:T(8,128)S(1)}, f32[3,4,32,128]{3,2,1,0:T(8,128)S(1)}, u32[]{:S(2)}, u32[]{:S(2)}) collective-permute-start(f32[3,4,32,128]{3,2,1,0:T(8,128)S(1)} %get-tuple-element.32.refs_2_.refs_6_), channel_id=1, source_target_pairs={{0,2},{2,4},{4,6},{6,8},{8,10},{10,12},{12,14},{14,16},{16,18},{18... | collective-permute-start | bytes 589832 | tf_op jit(solution)/shard_map/ppermute | solution.py:494
  13.5 4.8 %collective-permute-start.2 = (f32[5,2,32,128]{3,2,1,0:T(8,128)S(1)}, f32[5,2,32,128]{3,2,1,0:T(8,128)S(1)}, u32[]{:S(2)}, u32[]{:S(2)}) collective-permute-start(f32[5,2,32,128]{3,2,1,0:T(8,128)S(1)} %get-tuple-element.37), channel_id=1, source_target_pairs={{0,2},{2,4},{4,6},{6,8},{8,10},{10,12},{12,14},{14,16},{16,18},{18... | collective-permute-start | bytes 491528 | tf_op jit(solution)/shard_map/ppermute | solution.py:494
  21.8 4.6 %collective-permute-done.3.refs_10_ = f32[5,2,32,128]{3,2,1,0:T(8,128)S(1)} collective-permute-done((f32[5,2,32,128]{3,2,1,0:T(8,128)S(1)}, f32[5,2,32,128]{3,2,1,0:T(8,128)S(1)}, u32[]{:S(2)}, u32[]{:S(2)}) %collective-permute-start.3) | collective-permute-done | bytes 163872 | tf_op jit(solution)/shard_map/ppermute | solution.py:494
  26.4 2.3 %step_0.1 = (f32[3,4,32,128]{3,2,1,0:T(8,128)S(1)}, f32[3,4,32,128]{3,2,1,0:T(8,128)S(1)}, f32[3,32,128]{2,1,0:T(8,128)S(1)}, f32[192,128]{1,0:T(8,128)S(1)}) custom-call(f32[2]{0:T(128)S(1)} %add_convert_fusion.refs_0_, f32[3,4,32,128]{3,2,1,0:T(8,128)S(1)} %get-tuple-element.31.refs_1_.refs_5_, f32[3,4,32,128]{3,2,1,0:T(8,128)S(1)} %get-tuple-element.32.refs_2_.refs_6_, ...), custom_call_target="tpu_custom_call" | custom-call | flops 30000000 | bytes 3162120 | tf_op jit(solution)/shard_map/step_0/pallas_call | solution.py:453
  30.0 5.8 %collective-permute-start.7 = (f32[3,4,32,128]{3,2,1,0:T(8,128)S(1)}, f32[3,4,32,128]{3,2,1,0:T(8,128)S(1)}, u32[]{:S(2)}, u32[]{:S(2)}) collective-permute-start(f32[3,4,32,128]{3,2,1,0:T(8,128)S(1)} %get-tuple-element.42.refs_2_.refs_6_), channel_id=1, source_target_pairs={{0,2},{2,4},{4,6},{6,8},{8,10},{10,12},{12,14},{14,16},{16,18},{18... | collective-permute-start | bytes 589832 | tf_op jit(solution)/shard_map/ppermute | solution.py:494
  35.9 2.1 %collective-permute-done.8.above_ref.refs_4_ = f32[3,4,32,128]{3,2,1,0:T(8,128)S(1)} collective-permute-done((f32[3,4,32,128]{3,2,1,0:T(8,128)S(1)}, f32[3,4,32,128]{3,2,1,0:T(8,128)S(1)}, u32[]{:S(2)}, u32[]{:S(2)}) %collective-permute-start.8) | collective-permute-done | bytes 196640 | tf_op jit(solution)/shard_map/ppermute | solution.py:494
  38.0 4.6 %collective-permute-done.7.below_ref.refs_3_ = f32[3,4,32,128]{3,2,1,0:T(8,128)S(1)} collective-permute-done((f32[3,4,32,128]{3,2,1,0:T(8,128)S(1)}, f32[3,4,32,128]{3,2,1,0:T(8,128)S(1)}, u32[]{:S(2)}, u32[]{:S(2)}) %collective-permute-start.7) | collective-permute-done | bytes 196640 | tf_op jit(solution)/shard_map/ppermute | solution.py:494
  44.0 2.3 %step_1.1 = (f32[3,4,32,128]{3,2,1,0:T(8,128)S(1)}, f32[3,4,32,128]{3,2,1,0:T(8,128)S(1)}, f32[3,32,128]{2,1,0:T(8,128)S(1)}, f32[192,128]{1,0:T(8,128)S(1)}) custom-call(f32[2]{0:T(128)S(1)} %add_convert_fusion.refs_0_, f32[3,4,32,128]{3,2,1,0:T(8,128)S(1)} %get-tuple-element.41.refs_1_.refs_5_, f32[3,4,32,128]{3,2,1,0:T(8,128)S(1)} %get-tuple-element.42.refs_2_.refs_6_, ...), custom_call_target="tpu_custom_call" | custom-call | flops 30000000 | bytes 3260424 | tf_op jit(solution)/shard_map/step_1/pallas_call | solution.py:453
  47.6 5.0 %collective-permute-start.11 = (f32[3,4,32,128]{3,2,1,0:T(8,128)S(1)}, f32[3,4,32,128]{3,2,1,0:T(8,128)S(1)}, u32[]{:S(2)}, u32[]{:S(2)}) collective-permute-start(f32[3,4,32,128]{3,2,1,0:T(8,128)S(1)} %get-tuple-element.46.refs_2_.refs_6_), channel_id=1, source_target_pairs={{0,2},{2,4},{4,6},{6,8},{8,10},{10,12},{12,14},{14,16},{16,18},{18... | collective-permute-start | bytes 589832 | tf_op jit(solution)/shard_map/ppermute | solution.py:494
  52.7 3.2 %collective-permute-done.12.above_ref.refs_4_ = f32[3,4,32,128]{3,2,1,0:T(8,128)S(1)} collective-permute-done((f32[3,4,32,128]{3,2,1,0:T(8,128)S(1)}, f32[3,4,32,128]{3,2,1,0:T(8,128)S(1)}, u32[]{:S(2)}, u32[]{:S(2)}) %collective-permute-start.12) | collective-permute-done | bytes 196640 | tf_op jit(solution)/shard_map/ppermute | solution.py:494
  55.9 4.2 %collective-permute-done.11.below_ref.refs_3_ = f32[3,4,32,128]{3,2,1,0:T(8,128)S(1)} collective-permute-done((f32[3,4,32,128]{3,2,1,0:T(8,128)S(1)}, f32[3,4,32,128]{3,2,1,0:T(8,128)S(1)}, u32[]{:S(2)}, u32[]{:S(2)}) %collective-permute-start.11) | collective-permute-done | bytes 196640 | tf_op jit(solution)/shard_map/ppermute | solution.py:494
  61.4 2.3 %step_2.1 = (f32[3,4,32,128]{3,2,1,0:T(8,128)S(1)}, f32[3,4,32,128]{3,2,1,0:T(8,128)S(1)}, f32[3,32,128]{2,1,0:T(8,128)S(1)}, f32[192,128]{1,0:T(8,128)S(1)}) custom-call(f32[2]{0:T(128)S(1)} %add_convert_fusion.refs_0_, f32[3,4,32,128]{3,2,1,0:T(8,128)S(1)} %get-tuple-element.45.refs_1_.refs_5_, f32[3,4,32,128]{3,2,1,0:T(8,128)S(1)} %get-tuple-element.46.refs_2_.refs_6_, ...), custom_call_target="tpu_custom_call" | custom-call | flops 30000000 | bytes 3260424 | tf_op jit(solution)/shard_map/step_2/pallas_call | solution.py:453
  65.0 5.2 %collective-permute-start.15 = (f32[3,4,32,128]{3,2,1,0:T(8,128)S(1)}, f32[3,4,32,128]{3,2,1,0:T(8,128)S(1)}, u32[]{:S(2)}, u32[]{:S(2)}) collective-permute-start(f32[3,4,32,128]{3,2,1,0:T(8,128)S(1)} %get-tuple-element.50.refs_2_), channel_id=1, source_target_pairs={{0,2},{2,4},{4,6},{6,8},{8,10},{10,12},{12,14},{14,16},{16,18},{18... | collective-permute-start | bytes 589832 | tf_op jit(solution)/shard_map/ppermute | solution.py:494
  70.3 3.0 %collective-permute-done.16.above_ref.refs_4_ = f32[3,4,32,128]{3,2,1,0:T(8,128)S(1)} collective-permute-done((f32[3,4,32,128]{3,2,1,0:T(8,128)S(1)}, f32[3,4,32,128]{3,2,1,0:T(8,128)S(1)}, u32[]{:S(2)}, u32[]{:S(2)}) %collective-permute-start.16) | collective-permute-done | bytes 196640 | tf_op jit(solution)/shard_map/ppermute | solution.py:494
  73.3 4.6 %collective-permute-done.15.below_ref.refs_3_ = f32[3,4,32,128]{3,2,1,0:T(8,128)S(1)} collective-permute-done((f32[3,4,32,128]{3,2,1,0:T(8,128)S(1)}, f32[3,4,32,128]{3,2,1,0:T(8,128)S(1)}, u32[]{:S(2)}, u32[]{:S(2)}) %collective-permute-start.15) | collective-permute-done | bytes 196640 | tf_op jit(solution)/shard_map/ppermute | solution.py:494
  79.3 3.1 %step_3.1 = (f32[3,256,128]{2,1,0:T(8,128)}, f32[192,128]{1,0:T(8,128)S(1)}) custom-call(f32[2]{0:T(128)S(1)} %add_convert_fusion.refs_0_, f32[3,4,32,128]{3,2,1,0:T(8,128)S(1)} %get-tuple-element.49.refs_1_, f32[3,4,32,128]{3,2,1,0:T(8,128)S(1)} %get-tuple-element.50.refs_2_, f32[3,4,32,128]{3,2,1,0:T(8,128)S(1)} %collective-permute-done.15.below_ref.refs_3_, ...), custom_call_target="tpu_custom_call" | custom-call | flops 30000000 | bytes 3211272 | tf_op jit(solution)/shard_map/step_3/pallas_call | solution.py:453
  84.0 2.5 %collective-permute-start.20 = (f32[128,128]{1,0:T(8,128)S(1)}, f32[128,128]{1,0:T(8,128)S(1)}, u32[]{:S(2)}, u32[]{:S(2)}) collective-permute-start(f32[128,128]{1,0:T(8,128)S(1)} %get-tuple-element.55), channel_id=1, source_target_pairs={{0,2},{2,0},{4,6},{6,4},{8,10},{10,8},{12,14},{14,12},{16,18},{18,... | collective-permute-start | bytes 196616 | tf_op jit(solution)/shard_map/ppermute | solution.py:472
  86.5 2.4 %collective-permute-done.20 = f32[128,128]{1,0:T(8,128)S(1)} collective-permute-done((f32[128,128]{1,0:T(8,128)S(1)}, f32[128,128]{1,0:T(8,128)S(1)}, u32[]{:S(2)}, u32[]{:S(2)}) %collective-permute-start.20) | collective-permute-done | bytes 65568 | tf_op jit(solution)/shard_map/ppermute | solution.py:472
  89.5 3.7 %collective-permute-done.21 = f32[128,128]{1,0:T(8,128)S(1)} collective-permute-done((f32[128,128]{1,0:T(8,128)S(1)}, f32[128,128]{1,0:T(8,128)S(1)}, u32[]{:S(2)}, u32[]{:S(2)}) %collective-permute-start.21) | collective-permute-done | bytes 65568 | tf_op jit(solution)/shard_map/ppermute | solution.py:472
  93.3 1.7 %collective-permute-start.22 = (f32[128,128]{1,0:T(8,128)S(1)}, f32[128,128]{1,0:T(8,128)S(1)}, u32[]{:S(2)}, u32[]{:S(2)}) collective-permute-start(f32[128,128]{1,0:T(8,128)S(1)} %add.13), channel_id=1, source_target_pairs={{0,8},{2,10},{4,12},{6,14},{8,0},{10,2},{12,4},{14,6},{16,24},{18,... | collective-permute-start | bytes 196616 | tf_op jit(solution)/shard_map/ppermute | solution.py:472
  95.0 2.6 %collective-permute-done.22 = f32[128,128]{1,0:T(8,128)S(1)} collective-permute-done((f32[128,128]{1,0:T(8,128)S(1)}, f32[128,128]{1,0:T(8,128)S(1)}, u32[]{:S(2)}, u32[]{:S(2)}) %collective-permute-start.22) | collective-permute-done | bytes 65568 | tf_op jit(solution)/shard_map/ppermute | solution.py:472
  97.6 3.4 %collective-permute-start.23 = (f32[128,128]{1,0:T(8,128)S(1)}, f32[128,128]{1,0:T(8,128)S(1)}, u32[]{:S(2)}, u32[]{:S(2)}) collective-permute-start(f32[128,128]{1,0:T(8,128)S(1)} %add.14), channel_id=1, source_target_pairs={{0,16},{2,18},{4,20},{6,22},{8,24},{10,26},{12,28},{14,30},{16,0},... | collective-permute-start | bytes 196616 | tf_op jit(solution)/shard_map/ppermute | solution.py:472
  101.0 2.3 %collective-permute-done.23 = f32[128,128]{1,0:T(8,128)S(1)} collective-permute-done((f32[128,128]{1,0:T(8,128)S(1)}, f32[128,128]{1,0:T(8,128)S(1)}, u32[]{:S(2)}, u32[]{:S(2)}) %collective-permute-start.23) | collective-permute-done | bytes 65568 | tf_op jit(solution)/shard_map/ppermute | solution.py:472
  103.3 18.5 %factor.1 = (f32[4,24,128]{2,1,0:T(8,128)}, f32[128,128]{1,0:T(8,128)}) custom-call(s32[1]{0:T(128)} %bitcast.13.side_ref, f32[128,128]{1,0:T(8,128)S(1)} %add.15.gram_ref, f32[4,48,128]{2,1,0:T(8,128)S(1)} %bitcast.26), custom_call_target="tpu_custom_call" | custom-call | bytes 278532 | tf_op jit(solution)/shard_map/factor/pallas_call | solution.py:453
  (56 shorter events, 21.6 us)
Async XLA Ops:
  1.9 18.6 %collective-permute-start.4 = (f32[3,32,128]{2,1,0:T(8,128)S(1)}, f32[3,32,128]{2,1,0:T(8,128)S(1)}, u32[]{:S(2)}, u32[]{:S(2)}) collective-permute-start(f32[3,32,128]{2,1,0:T(8,128)S(1)} %get-tuple-element.39.refs_11_), channel_id=1, source_target_pairs={{0,1},{1,0},{2,3},{3,2},{4,5},{5,4},{6,7},{7,6},{8,9},{9,8},{10,11... | collective-permute-start | bytes 147464 | tf_op jit(solution)/shard_map/ppermute | solution.py:498
  2.5 17.2 %collective-permute-start.1 = (f32[3,4,32,128]{3,2,1,0:T(8,128)S(1)}, f32[3,4,32,128]{3,2,1,0:T(8,128)S(1)}, u32[]{:S(2)}, u32[]{:S(2)}) collective-permute-start(f32[3,4,32,128]{3,2,1,0:T(8,128)S(1)} %get-tuple-element.31.refs_1_.refs_5_), channel_id=1, source_target_pairs={{2,0},{4,2},{6,4},{8,6},{10,8},{12,10},{14,12},{16,14},{18,16},{20... | collective-permute-start | bytes 589832 | tf_op jit(solution)/shard_map/ppermute | solution.py:494
  3.8 16.0 %collective-permute-start = (f32[3,4,32,128]{3,2,1,0:T(8,128)S(1)}, f32[3,4,32,128]{3,2,1,0:T(8,128)S(1)}, u32[]{:S(2)}, u32[]{:S(2)}) collective-permute-start(f32[3,4,32,128]{3,2,1,0:T(8,128)S(1)} %get-tuple-element.32.refs_2_.refs_6_), channel_id=1, source_target_pairs={{0,2},{2,4},{4,6},{6,8},{8,10},{10,12},{12,14},{14,16},{16,18},{18... | collective-permute-start | bytes 589832 | tf_op jit(solution)/shard_map/ppermute | solution.py:494
  13.5 8.3 %collective-permute-start.2 = (f32[5,2,32,128]{3,2,1,0:T(8,128)S(1)}, f32[5,2,32,128]{3,2,1,0:T(8,128)S(1)}, u32[]{:S(2)}, u32[]{:S(2)}) collective-permute-start(f32[5,2,32,128]{3,2,1,0:T(8,128)S(1)} %get-tuple-element.37), channel_id=1, source_target_pairs={{0,2},{2,4},{4,6},{6,8},{8,10},{10,12},{12,14},{14,16},{16,18},{18... | collective-permute-start | bytes 491528 | tf_op jit(solution)/shard_map/ppermute | solution.py:494
  18.3 8.1 %collective-permute-start.3 = (f32[5,2,32,128]{3,2,1,0:T(8,128)S(1)}, f32[5,2,32,128]{3,2,1,0:T(8,128)S(1)}, u32[]{:S(2)}, u32[]{:S(2)}) collective-permute-start(f32[5,2,32,128]{3,2,1,0:T(8,128)S(1)} %get-tuple-element.38), channel_id=1, source_target_pairs={{2,0},{4,2},{6,4},{8,6},{10,8},{12,10},{14,12},{16,14},{18,16},{20... | collective-permute-start | bytes 491528 | tf_op jit(solution)/shard_map/ppermute | solution.py:494
  19.7 1.3 %collective-permute-start.6 = (f32[5,32,128]{2,1,0:T(8,128)S(1)}, f32[5,32,128]{2,1,0:T(8,128)S(1)}, u32[]{:S(2)}, u32[]{:S(2)}) collective-permute-start(f32[5,32,128]{2,1,0:T(8,128)S(1)} %get-tuple-element.40.refs_14_), channel_id=1, source_target_pairs={{0,1},{1,0},{2,3},{3,2},{4,5},{5,4},{6,7},{7,6},{8,9},{9,8},{10,11... | collective-permute-start | bytes 245768 | tf_op jit(solution)/shard_map/ppermute | solution.py:498
  19.9 6.5 %collective-permute-start.5 = (f32[2,32,128]{2,1,0:T(8,128)S(1)}, f32[2,32,128]{2,1,0:T(8,128)S(1)}, u32[]{:S(2)}, u32[]{:S(2)}) collective-permute-start(f32[2,32,128]{2,1,0:T(8,128)S(1)} %corner_0.1), channel_id=1, source_target_pairs={{0,1},{1,0},{2,3},{3,2},{4,5},{5,4},{6,7},{7,6},{8,9},{9,8},{10,11... | collective-permute-start | bytes 98312 | tf_op jit(solution)/shard_map/ppermute | solution.py:498
  28.7 9.3 %collective-permute-start.8 = (f32[3,4,32,128]{3,2,1,0:T(8,128)S(1)}, f32[3,4,32,128]{3,2,1,0:T(8,128)S(1)}, u32[]{:S(2)}, u32[]{:S(2)}) collective-permute-start(f32[3,4,32,128]{3,2,1,0:T(8,128)S(1)} %get-tuple-element.41.refs_1_.refs_5_), channel_id=1, source_target_pairs={{2,0},{4,2},{6,4},{8,6},{10,8},{12,10},{14,12},{16,14},{18,16},{20... | collective-permute-start | bytes 589832 | tf_op jit(solution)/shard_map/ppermute | solution.py:494
  30.0 12.6 %collective-permute-start.7 = (f32[3,4,32,128]{3,2,1,0:T(8,128)S(1)}, f32[3,4,32,128]{3,2,1,0:T(8,128)S(1)}, u32[]{:S(2)}, u32[]{:S(2)}) collective-permute-start(f32[3,4,32,128]{3,2,1,0:T(8,128)S(1)} %get-tuple-element.42.refs_2_.refs_6_), channel_id=1, source_target_pairs={{0,2},{2,4},{4,6},{6,8},{8,10},{10,12},{12,14},{14,16},{16,18},{18... | collective-permute-start | bytes 589832 | tf_op jit(solution)/shard_map/ppermute | solution.py:494
  35.8 6.9 %collective-permute-start.9 = (f32[3,32,128]{2,1,0:T(8,128)S(1)}, f32[3,32,128]{2,1,0:T(8,128)S(1)}, u32[]{:S(2)}, u32[]{:S(2)}) collective-permute-start(f32[3,32,128]{2,1,0:T(8,128)S(1)} %get-tuple-element.43.refs_11_), channel_id=1, source_target_pairs={{0,1},{1,0},{2,3},{3,2},{4,5},{5,4},{6,7},{7,6},{8,9},{9,8},{10,11... | collective-permute-start | bytes 147464 | tf_op jit(solution)/shard_map/ppermute | solution.py:498
  42.7 1.3 %collective-permute-start.10 = (f32[2,32,128]{2,1,0:T(8,128)S(1)}, f32[2,32,128]{2,1,0:T(8,128)S(1)}, u32[]{:S(2)}, u32[]{:S(2)}) collective-permute-start(f32[2,32,128]{2,1,0:T(8,128)S(1)} %corner_1.1), channel_id=1, source_target_pairs={{0,1},{1,0},{2,3},{3,2},{4,5},{5,4},{6,7},{7,6},{8,9},{9,8},{10,11... | collective-permute-start | bytes 98312 | tf_op jit(solution)/shard_map/ppermute | solution.py:498
  46.3 9.6 %collective-permute-start.12 = (f32[3,4,32,128]{3,2,1,0:T(8,128)S(1)}, f32[3,4,32,128]{3,2,1,0:T(8,128)S(1)}, u32[]{:S(2)}, u32[]{:S(2)}) collective-permute-start(f32[3,4,32,128]{3,2,1,0:T(8,128)S(1)} %get-tuple-element.45.refs_1_.refs_5_), channel_id=1, source_target_pairs={{2,0},{4,2},{6,4},{8,6},{10,8},{12,10},{14,12},{16,14},{18,16},{20... | collective-permute-start | bytes 589832 | tf_op jit(solution)/shard_map/ppermute | solution.py:494
  47.6 12.5 %collective-permute-start.11 = (f32[3,4,32,128]{3,2,1,0:T(8,128)S(1)}, f32[3,4,32,128]{3,2,1,0:T(8,128)S(1)}, u32[]{:S(2)}, u32[]{:S(2)}) collective-permute-start(f32[3,4,32,128]{3,2,1,0:T(8,128)S(1)} %get-tuple-element.46.refs_2_.refs_6_), channel_id=1, source_target_pairs={{0,2},{2,4},{4,6},{6,8},{8,10},{10,12},{12,14},{14,16},{16,18},{18... | collective-permute-start | bytes 589832 | tf_op jit(solution)/shard_map/ppermute | solution.py:494
  52.6 7.6 %collective-permute-start.13 = (f32[3,32,128]{2,1,0:T(8,128)S(1)}, f32[3,32,128]{2,1,0:T(8,128)S(1)}, u32[]{:S(2)}, u32[]{:S(2)}) collective-permute-start(f32[3,32,128]{2,1,0:T(8,128)S(1)} %get-tuple-element.47.refs_11_), channel_id=1, source_target_pairs={{0,1},{1,0},{2,3},{3,2},{4,5},{5,4},{6,7},{7,6},{8,9},{9,8},{10,11... | collective-permute-start | bytes 147464 | tf_op jit(solution)/shard_map/ppermute | solution.py:498
  60.1 1.3 %collective-permute-start.14 = (f32[2,32,128]{2,1,0:T(8,128)S(1)}, f32[2,32,128]{2,1,0:T(8,128)S(1)}, u32[]{:S(2)}, u32[]{:S(2)}) collective-permute-start(f32[2,32,128]{2,1,0:T(8,128)S(1)} %corner_2.1), channel_id=1, source_target_pairs={{0,1},{1,0},{2,3},{3,2},{4,5},{5,4},{6,7},{7,6},{8,9},{9,8},{10,11... | collective-permute-start | bytes 98312 | tf_op jit(solution)/shard_map/ppermute | solution.py:498
  63.7 9.6 %collective-permute-start.16 = (f32[3,4,32,128]{3,2,1,0:T(8,128)S(1)}, f32[3,4,32,128]{3,2,1,0:T(8,128)S(1)}, u32[]{:S(2)}, u32[]{:S(2)}) collective-permute-start(f32[3,4,32,128]{3,2,1,0:T(8,128)S(1)} %get-tuple-element.49.refs_1_), channel_id=1, source_target_pairs={{2,0},{4,2},{6,4},{8,6},{10,8},{12,10},{14,12},{16,14},{18,16},{20... | collective-permute-start | bytes 589832 | tf_op jit(solution)/shard_map/ppermute | solution.py:494
  65.0 12.9 %collective-permute-start.15 = (f32[3,4,32,128]{3,2,1,0:T(8,128)S(1)}, f32[3,4,32,128]{3,2,1,0:T(8,128)S(1)}, u32[]{:S(2)}, u32[]{:S(2)}) collective-permute-start(f32[3,4,32,128]{3,2,1,0:T(8,128)S(1)} %get-tuple-element.50.refs_2_), channel_id=1, source_target_pairs={{0,2},{2,4},{4,6},{6,8},{8,10},{10,12},{12,14},{14,16},{16,18},{18... | collective-permute-start | bytes 589832 | tf_op jit(solution)/shard_map/ppermute | solution.py:494
  70.2 7.9 %collective-permute-start.17 = (f32[3,32,128]{2,1,0:T(8,128)S(1)}, f32[3,32,128]{2,1,0:T(8,128)S(1)}, u32[]{:S(2)}, u32[]{:S(2)}) collective-permute-start(f32[3,32,128]{2,1,0:T(8,128)S(1)} %get-tuple-element.51.refs_11_), channel_id=1, source_target_pairs={{0,1},{1,0},{2,3},{3,2},{4,5},{5,4},{6,7},{7,6},{8,9},{9,8},{10,11... | collective-permute-start | bytes 147464 | tf_op jit(solution)/shard_map/ppermute | solution.py:498
  78.0 1.3 %collective-permute-start.18 = (f32[2,32,128]{2,1,0:T(8,128)S(1)}, f32[2,32,128]{2,1,0:T(8,128)S(1)}, u32[]{:S(2)}, u32[]{:S(2)}) collective-permute-start(f32[2,32,128]{2,1,0:T(8,128)S(1)} %corner_3.1), channel_id=1, source_target_pairs={{0,1},{1,0},{2,3},{3,2},{4,5},{5,4},{6,7},{7,6},{8,9},{9,8},{10,11... | collective-permute-start | bytes 98312 | tf_op jit(solution)/shard_map/ppermute | solution.py:498
  82.4 1.3 %collective-permute-start.19 = (f32[192,128]{1,0:T(8,128)S(1)}, f32[192,128]{1,0:T(8,128)S(1)}, u32[]{:S(2)}, u32[]{:S(2)}) collective-permute-start(f32[192,128]{1,0:T(8,128)S(1)} %get-tuple-element.54.first_ref), channel_id=1, source_target_pairs={{0,1},{1,0},{2,3},{3,2},{4,5},{5,4},{6,7},{7,6},{8,9},{9,8},{10,11... | collective-permute-start | bytes 294920 | tf_op jit(solution)/shard_map/ppermute | solution.py:472
  84.0 5.0 %collective-permute-start.20 = (f32[128,128]{1,0:T(8,128)S(1)}, f32[128,128]{1,0:T(8,128)S(1)}, u32[]{:S(2)}, u32[]{:S(2)}) collective-permute-start(f32[128,128]{1,0:T(8,128)S(1)} %get-tuple-element.55), channel_id=1, source_target_pairs={{0,2},{2,0},{4,6},{6,4},{8,10},{10,8},{12,14},{14,12},{16,18},{18,... | collective-permute-start | bytes 196616 | tf_op jit(solution)/shard_map/ppermute | solution.py:472
  88.9 4.3 %collective-permute-start.21 = (f32[128,128]{1,0:T(8,128)S(1)}, f32[128,128]{1,0:T(8,128)S(1)}, u32[]{:S(2)}, u32[]{:S(2)}) collective-permute-start(f32[128,128]{1,0:T(8,128)S(1)} %add.12), channel_id=1, source_target_pairs={{0,4},{2,6},{4,0},{6,2},{8,12},{10,14},{12,8},{14,10},{16,20},{18,... | collective-permute-start | bytes 196616 | tf_op jit(solution)/shard_map/ppermute | solution.py:472
  93.3 4.3 %collective-permute-start.22 = (f32[128,128]{1,0:T(8,128)S(1)}, f32[128,128]{1,0:T(8,128)S(1)}, u32[]{:S(2)}, u32[]{:S(2)}) collective-permute-start(f32[128,128]{1,0:T(8,128)S(1)} %add.13), channel_id=1, source_target_pairs={{0,8},{2,10},{4,12},{6,14},{8,0},{10,2},{12,4},{14,6},{16,24},{18,... | collective-permute-start | bytes 196616 | tf_op jit(solution)/shard_map/ppermute | solution.py:472
  97.6 5.6 %collective-permute-start.23 = (f32[128,128]{1,0:T(8,128)S(1)}, f32[128,128]{1,0:T(8,128)S(1)}, u32[]{:S(2)}, u32[]{:S(2)}) collective-permute-start(f32[128,128]{1,0:T(8,128)S(1)} %add.14), channel_id=1, source_target_pairs={{0,16},{2,18},{4,20},{6,22},{8,24},{10,26},{12,28},{14,30},{16,0},... | collective-permute-start | bytes 196616 | tf_op jit(solution)/shard_map/ppermute | solution.py:472
  (7 other events, 19.0 us)

commit v3 on v0

v3 whole, which is shorter than its diff:
```python
import math
from functools import partial

import jax
import jax.numpy as jnp
from jax import lax
from jax.experimental import pallas as pl
from jax.experimental.pallas import tpu as pltpu
from jax.sharding import PartitionSpec as P

STEPS = 4
SUB = 8

time_step = 0.12


def roll(value, shift, axis=-1):
    axis = axis % value.ndim
    shift = shift % value.shape[axis]
    return value if shift == 0 else pltpu.roll(value, shift, axis)


def lanes_of(shape):
    return lax.broadcasted_iota(jnp.int32, shape, len(shape) - 1)


def layer_derivative(value):
    groups = value.shape[0] // SUB
    parts = [value[SUB * v : SUB * (v + 1)] for v in range(groups)]
    sub = lax.broadcasted_iota(jnp.int32, parts[0].shape, 0)
    shifted = {}

    def at(v):
        if 0 <= v < groups:
            return parts[v]
        if v not in shifted:
            if v >= groups:
                shifted[v] = jnp.where(sub < SUB - 1, roll(parts[v - groups], -1, 0), 0.0)
            else:
                shifted[v] = jnp.where(sub > 0, roll(parts[v + groups], 1, 0), 0.0)
        return shifted[v]

    return jnp.concatenate(
        [at(v - 2) - at(v + 2) + 8.0 * (at(v + 1) - at(v - 1)) for v in range(groups)], 0
    )


def band_matrix(count):
    row = lax.broadcasted_iota(jnp.int32, (count, count), 0)
    col = lax.broadcasted_iota(jnp.int32, (count, count), 1)
    away = row - col
    band = jnp.where(
        away == -2,
        1.0,
        jnp.where(away == 2, -1.0, jnp.where(away == 1, 8.0, jnp.where(away == -1, -8.0, 0.0))),
    )
    return band.astype(jnp.bfloat16)


def banded(value, band):
    high = value.astype(jnp.bfloat16)
    low = (value - high.astype(jnp.float32)).astype(jnp.bfloat16)
    return jnp.dot(high, band, preferred_element_type=jnp.float32) + jnp.dot(
        low, band, preferred_element_type=jnp.float32
    )


def edge_terms(edge, window):
    w = lanes_of(edge.shape) % window
    up_2, up_3 = roll(edge, 2), roll(edge, 3)
    down_2, down_3 = roll(edge, -2), roll(edge, -3)
    right = jnp.where(w == 7, 8.0 * up_3, 0.0) - up_2
    left = down_2 - jnp.where(w == 8, 8.0 * down_3, 0.0)
    return jnp.where((w == 6) | (w == 7), right, left)


def edge_spread(terms, place, window):
    count = terms.shape[-1]
    lane = lanes_of(terms.shape)
    return jnp.where((lane < 2) | (lane >= count - 2), roll(terms, count - 2 - window * place - 6), 0.0)


def edge_message(load, x_count, rows, y_count, which=None):
    window = y_count // x_count
    place = lanes_of((rows, y_count)) // window
    message = None
    for x in which or range(x_count):
        moved = roll(load(x), window * x + 4)
        message = moved if message is None else jnp.where(place == x, moved, message)
    return message


def neighbours():
    at = lax.axis_index("gy")
    return (at > 0).astype(jnp.float32), (at < lax.axis_size("gy") - 1).astype(jnp.float32)


def edge_tile(own, from_left, from_right, has_left, has_right, window):
    w = lanes_of(own.shape) % window
    halo = jnp.where(w < 8, from_right * has_right, roll(from_left, 8) * has_left)
    mine = jnp.where(w < 4, own, roll(own, 8))
    return jnp.where((w >= 4) & (w < 12), halo, mine)


def strided(ref, x_count, rows, index=()):
    groups = rows // SUB

    def at(x):
        return jnp.concatenate(
            [
                ref[(*index, pl.ds(x_count * v + x, SUB, stride=groups * x_count), slice(None))]
                for v in range(groups)
            ],
            0,
        )

    return at


def central(far_low, near_low, near_high, far_high):
    def minus(first, second):
        if second is None:
            return first
        return -second if first is None else first - second

    near, far = minus(near_high, near_low), minus(far_low, far_high)
    if near is None:
        return far
    return 8.0 * near if far is None else far + 8.0 * near


def halves(low_ref, high_ref, half):
    def at(c, x):
        return low_ref[c * half + x] if x < half else high_ref[c * half + x - half]

    return at


def begin_kernel(*refs):
    sources, (down_ref, up_ref, edge_ref, metric_ref) = refs[:4], refs[4:8]
    u_ref, slope_ref, stretch_ref, moduli_ref = refs[8:12]
    sems = refs[12]
    copies = [
        pltpu.make_async_copy(source, target, sems.at[i])
        for i, (source, target) in enumerate(zip(sources, refs[8:12]))
    ]
    for copy in copies:
        copy.start()
    copies[0].wait()
    x_count, rows, y_count = metric_ref.shape[1:]
    half = x_count // 2
    comps = u_ref.shape[0]
    for c in range(comps):
        at = strided(u_ref, x_count, rows, (c,))
        slabs = [at(x) for x in range(x_count)]
        for k in range(half):
            down_ref[c * half + k] = slabs[k]
            up_ref[c * half + k] = slabs[half + k]
        edge_ref[c] = edge_message(lambda x: slabs[x], x_count, rows, y_count)
    for copy in copies[1:]:
        copy.wait()
    fields = [
        (strided(slope_ref, x_count, rows, (0,)), None),
        (strided(slope_ref, x_count, rows, (1,)), None),
        (strided(stretch_ref, x_count, rows), None),
        (strided(moduli_ref, x_count, rows, (0,)), 1.0 / 12.0),
        (strided(moduli_ref, x_count, rows, (1,)), 1.0 / 12.0),
    ]
    for m, (at, scale) in enumerate(fields):
        slabs = [at(x) if scale is None else at(x) * scale for x in range(x_count)]
        for x in range(x_count):
            metric_ref[m, x] = slabs[x]
        for k in range(2):
            down_ref[comps * half + 2 * m + k] = slabs[k]
            up_ref[comps * half + 2 * m + k] = slabs[x_count - 2 + k]
        edge_ref[comps + m] = edge_message(lambda x: slabs[x], x_count, rows, y_count)


def rest_kernel(u_ref, v_ref, buoyancy_ref, before_low, before_high, push_ref):
    x_count, rows, _ = push_ref.shape
    half = x_count // 2
    at = strided(buoyancy_ref, x_count, rows)
    for x in range(x_count):
        push_ref[x] = at(x) * (time_step**2 / 12.0)
    for c in range(u_ref.shape[0]):
        at, rate = strided(u_ref, x_count, rows, (c,)), strided(v_ref, x_count, rows, (c,))
        for x in range(x_count):
            (before_low if x < half else before_high)[c * half + x % half] = (
                at(x) - time_step * rate(x)
            )


def corner_kernel(half, below_ref, above_ref, *refs):
    corner_ref = refs[-1]
    rows, y_count = below_ref.shape[1:]
    x_count = 2 * half
    for c in range(corner_ref.shape[0]):

        def load(x):
            return below_ref[c * half + x - half] if x >= half else above_ref[c * half + x]

        corner_ref[c] = edge_message(load, x_count, rows, y_count, (0, 1, x_count - 2, x_count - 1))


def all_stresses(grads, lame, shear):
    pressure = lame * (grads[0][0] + grads[1][1] + grads[2][2])
    twice = shear + shear
    return (
        pressure + twice * grads[0][0],
        pressure + twice * grads[1][1],
        pressure + twice * grads[2][2],
        shear * (grads[0][1] + grads[1][0]),
        shear * (grads[0][2] + grads[2][0]),
        shear * (grads[1][2] + grads[2][1]),
    )


def tile_kernel(sides, comps, *refs):
    low_ref, high_ref, edge_ref = refs[:3]
    edge_in = refs[3 : 3 + sides]
    metric_ref, first_edge = refs[3 + sides : 5 + sides]
    first_edge_in = refs[5 + sides : 5 + 2 * sides]
    s_x, s_o, e_s = refs[5 + 2 * sides :]
    x_count, rows, y_count = metric_ref.shape[1:]
    half, window = x_count // 2, y_count // x_count
    has_left, has_right = neighbours()
    place = lanes_of((rows, y_count)) // window
    u = halves(low_ref, high_ref, half)
    band = band_matrix(y_count)

    edges, across = [], []
    for c in range(comps):
        edge = edge_tile(edge_ref[c], edge_in[0][c], edge_in[-1][c], has_left, has_right, window)
        terms = edge_terms(edge, window)
        result = banded(jnp.concatenate([u(c, x) for x in range(x_count)], 0), band)
        edges.append(edge)
        across.append(
            [
                result[x * rows : (x + 1) * rows] + edge_spread(terms, x, window)
                for x in range(x_count)
            ]
        )

    def gradients(along, beside, layers, metric):
        return [
            [
                along[c] + metric[0] * layers[c],
                beside[c] + metric[1] * layers[c],
                metric[2] * layers[c],
            ]
            for c in range(comps)
        ]

    for x in range(x_count):
        metric = [metric_ref[m, x] for m in range(5)]

        def near(c, k):
            return u(c, x + k) if 0 <= x + k < x_count else None

        along = [central(*(near(c, k) for k in (-2, -1, 1, 2))) for c in range(comps)]
        layers = [layer_derivative(u(c, x)) for c in range(comps)]
        grads = gradients(along, [across[c][x] for c in range(comps)], layers, metric)
        s11, s22, s33, s12, s13, s23 = all_stresses(grads, metric[3], metric[4])
        s_x[0, x], s_x[1, x], s_x[2, x] = s11, s12, s13
        s_o[0, x], s_o[1, x], s_o[2, x] = s22, s23, s33

    metric = [
        edge_tile(
            first_edge[comps + m], first_edge_in[0][comps + m], first_edge_in[-1][comps + m],
            has_left, has_right, window,
        )
        for m in range(5)
    ]
    along, beside = [], []
    for edge in edges:

        def near(k):
            inside = (place + k < x_count) if k > 0 else (place + k >= 0)
            return jnp.where(inside, roll(edge, -window * k), 0.0)

        along.append(central(*(near(k) for k in (-2, -1, 1, 2))))
        beside.append(central(*(roll(edge, -k) for k in (-2, -1, 1, 2))))
    grads = gradients(along, beside, [layer_derivative(edge) for edge in edges], metric)
    _, e22, _, e12, _, e23 = all_stresses(grads, metric[3], metric[4])
    e_s[0], e_s[1], e_s[2], e_s[3], e_s[4] = e12, e22, e23, metric[3], metric[4]


def wide_kernel(
    low_ref, high_ref, below_ref, above_ref, before_low, before_high, metric_ref, push_ref,
    first_below, first_above, s_x, s_o, e_s, out_low, out_high, out_edge,
):
    x_count, rows, y_count = metric_ref.shape[1:]
    half, window = x_count // 2, y_count // x_count
    comps = s_x.shape[0]
    inner = halves(low_ref, high_ref, half)
    past = halves(before_low, before_high, half)
    band = band_matrix(y_count)

    def u(c, x):
        if x < 0:
            return below_ref[c * half + half + x]
        return above_ref[c * half + x - x_count] if x >= x_count else inner(c, x)

    along_x, others = {}, {}
    for x in range(x_count):
        near = {k: x + k for k in (-2, -1, 1, 2) if not 0 <= x + k < x_count}
        values = [s_x[i, x] for i in range(3)]
        rest = [s_o[i, x] for i in range(3)]
        if near:
            add = [
                central(*(u(c, near[k]) if k in near else None for k in (-2, -1, 1, 2)))
                for c in range(comps)
            ]
            lame, shear = metric_ref[3, x], metric_ref[4, x]
            pressure = lame * add[0]
            values[0] = values[0] + pressure + (shear + shear) * add[0]
            values[1] = values[1] + shear * add[1]
            values[2] = values[2] + shear * add[2]
            rest[0] = rest[0] + pressure
            rest[2] = rest[2] + pressure
        along_x[x], others[x] = values, rest

    outside = (-2, -1, x_count, x_count + 1)
    across = [
        banded(jnp.concatenate([u(c, x) for x in outside], 0), band) for c in range(2)
    ]
    for place, x in enumerate(outside):
        source, k = (first_below, place) if x < 0 else (first_above, place - 2)
        slope_x, slope_y, stretch, lame, shear = (
            source[comps * half + 2 * m + k] for m in range(5)
        )
        dr = [layer_derivative(u(c, x)) for c in range(comps)]
        dx = [central(*(u(c, x + j) for j in (-2, -1, 1, 2))) for c in range(comps)]
        dy = [across[c][place * rows : (place + 1) * rows] for c in range(2)]
        g11 = dx[0] + slope_x * dr[0]
        pressure = lame * (g11 + dy[1] + slope_y * dr[1] + stretch * dr[2])
        along_x[x] = [
            pressure + (shear + shear) * g11,
            shear * (dy[0] + slope_y * dr[0] + dx[1] + slope_x * dr[1]),
            shear * (stretch * dr[0] + dx[2] + slope_x * dr[2]),
        ]

    def across_of(i, x):
        return along_x[x][1] if i == 0 else others[x][i - 1]

    beside = []
    for i in range(comps):
        result = banded(jnp.concatenate([across_of(i, x) for x in range(x_count)], 0), band)
        terms = edge_terms(e_s[i], window)
        beside.append(
            [
                result[x * rows : (x + 1) * rows] + edge_spread(terms, x, window)
                for x in range(x_count)
            ]
        )

    place = lanes_of((rows, y_count)) // window
    messages = [None] * comps
    for x in range(x_count):
        slope_x, slope_y, stretch = (metric_ref[m, x] for m in range(3))
        r11, r12, r13 = (layer_derivative(value) for value in along_x[x])
        r22, r23, r33 = (layer_derivative(value) for value in others[x])
        layers = ((r11, r12, r13), (r12, r22, r23), (r13, r23, r33))
        for c in range(comps):
            force = central(*(along_x[x + k][c] for k in (-2, -1, 1, 2))) + beside[c][x]
            force = force + slope_x * layers[c][0] + slope_y * layers[c][1]
            force = force + stretch * layers[c][2]
            following = 2.0 * u(c, x) - past(c, x) + force * push_ref[x]
            (out_low if x < half else out_high)[c * half + x % half] = following
            moved = roll(following, window * x + 4)
            messages[c] = moved if x == 0 else jnp.where(place == x, moved, messages[c])
    for c in range(comps):
        out_edge[c] = messages[c]


def fix_kernel(sides, *refs):
    corner_in = refs[:sides]
    first_below, first_above, e_s, push_ref, low_ref, high_ref, edge_ref = refs[sides : 7 + sides]
    out_low, out_high, *out_edge = refs[7 + sides :]
    x_count, rows, y_count = push_ref.shape
    half, window = x_count // 2, y_count // x_count
    comps = edge_ref.shape[0]
    has_left, has_right = neighbours()
    lane = lanes_of((rows, y_count))
    place, w = lane // window, lane % window
    lame, shear = 3, 4

    corners = [
        jnp.where(w < 8, corner_in[-1][c] * has_right, roll(corner_in[0][c], 8) * has_left)
        for c in range(2)
    ]
    terms = [edge_terms(corner, window) for corner in corners]

    def edge_change(corner):
        def near(k):
            inside = (place + k < x_count) if k > 0 else (place + k >= 0)
            return jnp.where(inside, 0.0, roll(corner, -window * k))

        return central(*(near(k) for k in (-2, -1, 1, 2)))

    beside = [
        edge_terms(e_s[shear] * edge_change(corners[1]), window),
        edge_terms(e_s[lame] * edge_change(corners[0]), window),
    ]

    def stress_change(c, x):
        source, k = (first_below, x + 2) if x < 0 else (first_above, x - x_count)
        modulus = source[comps * half + 2 * (lame if c == 0 else shear) + k]
        return modulus * edge_spread(terms[1 - c], x % x_count, window)

    for c in range(comps):
        changes = {}
        if c < 2:
            changes = {x: stress_change(c, x) for x in (-2, -1, x_count, x_count + 1)}
        message = edge_ref[c]
        for x in range(x_count):
            at = c * half + x % half
            value = (low_ref if x < half else high_ref)[at]
            near = [changes.get(x + k) for k in (-2, -1, 1, 2)]
            if any(item is not None for item in near):
                change = central(*near) + edge_spread(beside[c], x, window)
                value = value + change * push_ref[x]
                message = jnp.where(place == x, roll(value, window * x + 4), message)
            (out_low if x < half else out_high)[at] = value
        if out_edge:
            out_edge[0][c] = message


def sketch_kernel(moment, last, shape, *refs):
    comps, half, rows, y_count = shape
    low_ref, high_ref, before_low, before_high, probe_ref = refs[:5]
    sketch_in = None if moment == 0 else refs[5]
    sketch_ref, spread = refs[-2:]
    x_count = 2 * half
    groups = rows // SUB
    picked = groups // 2
    now = halves(low_ref, high_ref, half)
    past = halves(before_low, before_high, half)
    spread[...] = jnp.zeros_like(spread)
    spread[pl.ds(0, y_count // 2, stride=2), :] = probe_ref[moment]
    rates = []
    for x in range(0, x_count, 2):
        for c in range(comps):
            rate = (now(c, x) - past(c, x)) * (0.5 / time_step)
            rates += [rate[SUB * v : SUB * (v + 1)] for v in range(0, groups, 2)]
    sketch = jnp.dot(
        jnp.concatenate(rates, 0),
        spread[...],
        precision=lax.Precision.HIGHEST,
        preferred_element_type=jnp.float32,
    )
    if sketch_in is not None:
        sketch = sketch + sketch_in[...]
    if last:
        for k in range(half * comps):
            for v in range(picked):
                start = (k * picked + v) * SUB
                sketch_ref[pl.ds(k * picked * SUB + v, SUB, stride=picked), :] = sketch[
                    start : start + SUB
                ]
    else:
        sketch_ref[...] = sketch


def finish_kernel(half, rows, low_ref, high_ref, out_ref):
    x_count, groups = 2 * half, rows // SUB
    now = halves(low_ref, high_ref, half)
    for c in range(out_ref.shape[0]):
        for x in range(x_count):
            value = now(c, x)
            for v in range(groups):
                out_ref[c, pl.ds(x_count * v + x, SUB, stride=groups * x_count), :] = value[
                    SUB * v : SUB * (v + 1)
                ]


def gram_kernel(first_ref, second_ref, sum_ref, packed_ref):
    total = first_ref[...] + second_ref[...]
    sum_ref[...] = total
    gram = lax.dot_general(
        total,
        total,
        (((0,), (0,)), ((), ())),
        precision=lax.Precision.HIGHEST,
        preferred_element_type=jnp.float32,
    )
    order = gram.shape[0]
    mid = order // 2
    top, bottom = gram[:mid], gram[mid:]
    row = lax.broadcasted_iota(jnp.int32, (mid, order), 0)
    column = lanes_of((mid, order)) - mid
    packed_ref[:mid] = jnp.where((column >= 0) & (row >= column), roll(top, mid), bottom)
    diagonal = jnp.sum(jnp.where(row == column, bottom, 0.0), 0, keepdims=True)
    packed_ref[mid:] = jnp.broadcast_to(diagonal, (packed_ref.shape[0] - mid, order))


def unpacked(packed):
    order = packed.shape[1]
    mid = order // 2
    row = lax.broadcasted_iota(jnp.int32, (mid, order), 0)
    lane = lanes_of((mid, order))
    column = lane - mid
    main = packed[:mid]
    diagonal = jnp.broadcast_to(packed[mid : mid + 1], (mid, order))
    moved = roll(main, mid)
    top = jnp.where(row > lane, moved, jnp.where(row == lane, 0.5 * moved, 0.0))
    bottom = jnp.where(
        (column < 0) | (row < column), main, jnp.where(row == column, 0.5 * diagonal, 0.0)
    )
    part = jnp.concatenate([top, bottom], 0)
    return part + part.T


def factor_kernel(scale, first_ref, second_ref, tall_ref, basis_ref, factor_ref):
    gram = unpacked(first_ref[...] + second_ref[...])
    order = gram.shape[0]
    blocks = order // SUB
    shape = (SUB, order)
    sub = lax.broadcasted_iota(jnp.int32, shape, 0)
    lane = lanes_of(shape)
    work = [gram[SUB * q : SUB * (q + 1)] for q in range(blocks)]
    other = [jnp.where(lane == sub + SUB * q, 1.0, 0.0) for q in range(blocks)]
    inverse_rows = []

    def row_of(value, k):
        return jnp.broadcast_to(value[k : k + 1, :], value.shape)

    def column_of(value, j):
        return jnp.broadcast_to(value[:, j : j + 1], value.shape)

    for p in range(blocks):
        columns = [column_of(work[p], SUB * p + k) for k in range(SUB)]
        ahead = [column_of(work[p + 1], SUB * p + k) for k in range(SUB)] if p + 1 < blocks else []
        upper = solved = work[p]
        lower = solved_other = other[p]
        pivots = inverses = columns[0]
        for k in range(SUB):
            pivot = row_of(columns[k], k)
            inverse = 1.0 / pivot
            every = jnp.where(sub != k, columns[k] * inverse, 0.0)
            after = jnp.where(sub > k, every, 0.0)
            for m in range(k + 1, SUB):
                columns[m] = columns[m] - every * row_of(columns[m], k)
            upper = upper - after * row_of(upper, k)
            lower = lower - after * row_of(lower, k)
            solved = solved - every * row_of(solved, k)
            solved_other = solved_other - every * row_of(solved_other, k)
            pivots = jnp.where(sub == k, pivot, pivots)
            inverses = jnp.where(sub == k, inverse, inverses)
        root = lax.rsqrt(pivots)
        factor_ref[SUB * p : SUB * (p + 1), :] = jnp.where(lane >= sub + SUB * p, upper * root, 0.0)
        inverse_rows.append(lower * root * scale)
        solved, solved_other = solved * inverses, solved_other * inverses
        for k, column in enumerate(ahead):
            work[p + 1] = work[p + 1] - column * row_of(solved, k)
            other[p + 1] = other[p + 1] - column * row_of(solved_other, k)
        if p + 2 < blocks:
            both = jnp.concatenate([solved, solved_other], 1)
            parts = [jnp.zeros((SUB * p, 2 * order), jnp.float32)] if p else []
            parts += [both, jnp.zeros((order - SUB * (p + 1), 2 * order), jnp.float32)]
            change = jnp.dot(
                jnp.concatenate(work[p + 2 :], 0),
                jnp.concatenate(parts, 0),
                precision=lax.Precision.HIGHEST,
                preferred_element_type=jnp.float32,
            )
            for i, q in enumerate(range(p + 2, blocks)):
                work[q] = work[q] - change[SUB * i : SUB * (i + 1), :order]
                other[q] = other[q] - change[SUB * i : SUB * (i + 1), order:]

    inverse_lower = jnp.concatenate(inverse_rows, 0)
    count, kept = basis_ref.shape[0], basis_ref.shape[1]
    start = pl.multiple_of(lax.axis_index("gy") * kept, SUB)
    tall = jnp.concatenate([tall_ref[k, pl.ds(start, kept), :] for k in range(count)], 0)
    basis = lax.dot_general(
        tall,
        inverse_lower,
        (((1,), (1,)), ((), ())),
        precision=lax.Precision.HIGHEST,
        preferred_element_type=jnp.float32,
    )
    for k in range(count):
        basis_ref[k] = basis[k * kept : (k + 1) * kept]


def f32(*shape):
    return jax.ShapeDtypeStruct(shape, jnp.float32)


VMEM = pl.BlockSpec(memory_space=pltpu.MemorySpace.VMEM)
ANY = pl.BlockSpec(memory_space=pl.ANY)
HBM = pl.BlockSpec(memory_space=pltpu.MemorySpace.HBM)


def call(kernel, outs, name, ins, specs=None, scratch=(), flops=0):
    size = sum(math.prod(x.shape) * 4 for x in (*ins, *outs))
    return pl.pallas_call(
        kernel,
        out_shape=outs,
        in_specs=specs or [VMEM] * len(ins),
        out_specs=[VMEM] * len(outs),
        scratch_shapes=list(scratch),
        compiler_params=pltpu.CompilerParams(vmem_limit_bytes=24 * 2**20),
        cost_estimate=pl.CostEstimate(flops=flops, bytes_accessed=size, transcendentals=0),
        name=name,
    )(*ins)


def butterfly(value, axis, last=False):
    count = lax.axis_size(axis)
    if count & (count - 1):
        total = lax.psum(value, axis)
        return (total, jnp.zeros_like(total)) if last else total
    bit = 1
    while bit < count:
        other = lax.ppermute(value, axis, [(i, i ^ bit) for i in range(count)])
        if last and 2 * bit == count:
            return value, other
        value = value + other
        bit *= 2
    return (value, jnp.zeros_like(value)) if last else value


def shards(displacement, velocity, slopes, stretch, moduli, buoyancy, probes):
    comps, layers, x_count, y_count = displacement.shape
    width = probes.shape[2]
    half = x_count // 2
    n_x, n_y = lax.axis_size("gx"), lax.axis_size("gy")
    sides = 1 if n_y == 2 else 2

    def flat(array):
        return array.reshape(array.shape[:-3] + (layers * x_count, y_count))

    def along_x(value, step):
        pairs = [(i, i + step) for i in range(n_x) if 0 <= i + step < n_x]
        return lax.ppermute(value, "gx", pairs)

    def along_y(value):
        if sides == 1:
            return [lax.ppermute(value, "gy", [(0, 1), (1, 0)])]
        return [
            lax.ppermute(value, "gy", [(i, i + s) for i in range(n_y) if 0 <= i + s < n_y])
            for s in (1, -1)
        ]

    def slabs(count):
        return f32(count, layers, y_count)

    u_flat = flat(displacement)
    fields = [u_flat, flat(slopes), flat(stretch), flat(moduli)]
    down, up, edge, metric = call(
        begin_kernel,
        [slabs(comps * half + 10), slabs(comps * half + 10), slabs(comps + 5), f32(5, x_count, layers, y_count)],
        "begin",
        fields,
        specs=[HBM] * 4,
        scratch=[pltpu.VMEM(field.shape, jnp.float32) for field in fields]
        + [pltpu.SemaphoreType.DMA((4,))],
    )
    before_low, before_high, push = call(
        rest_kernel,
        [slabs(comps * half), slabs(comps * half), slabs(x_count)],
        "rest",
        [u_flat, flat(velocity), flat(buoyancy)],
    )

    low, high = down, up
    sketch_rows = half * comps * (layers // 2)
    sketch = []
    for moment in range(STEPS):
        last = moment == STEPS - 1
        edge_in = along_y(edge)
        above = along_x(low, -1)
        below = along_x(high, 1)
        if moment == 0:
            first_edge, first_edge_in, first_below, first_above = edge, edge_in, below, above
        s_x, s_o, e_s = call(
            partial(tile_kernel, sides, comps),
            [f32(comps, x_count, layers, y_count), f32(3, x_count, layers, y_count), slabs(5)],
            f"tile_{moment}",
            [low, high, edge, *edge_in, metric, first_edge, *first_edge_in],
            flops=20_000_000,
        )
        (corner,) = call(
            partial(corner_kernel, half),
            [slabs(2)],
            f"corner_{moment}",
            [below, above, e_s, *(sketch or [push])],
            specs=[VMEM, VMEM, ANY, ANY],
        )
        corner_in = along_y(corner)
        next_low, next_high, edge = call(
            wide_kernel,
            [slabs(comps * half), slabs(comps * half), slabs(comps)],
            f"wide_{moment}",
            [
                low, high, below, above, before_low, before_high, metric, push, first_below,
                first_above, s_x, s_o, e_s,
            ],
            flops=20_000_000,
        )
        next_low, next_high, *edge = call(
            partial(fix_kernel, sides),
            [slabs(comps * half), slabs(comps * half)] + ([] if last else [slabs(comps)]),
            f"fix_{moment}",
            [*corner_in, first_below, first_above, e_s, push, next_low, next_high, edge],
        )
        sketch = call(
            partial(sketch_kernel, moment, last, (comps, half, layers, y_count)),
            [f32(sketch_rows, width)],
            f"sketch_{moment}",
            [next_low, next_high, before_low, before_high, probes, *sketch],
            scratch=[pltpu.VMEM((y_count, width), jnp.float32)],
        )
        before_low, before_high, low, high = low, high, next_low, next_high
        edge = None if last else edge[0]
    (final,) = call(
        partial(finish_kernel, half, layers),
        [f32(comps, layers * x_count, y_count)],
        "finish",
        [low, high],
    )
    final = final.reshape(displacement.shape)

    mine, theirs = butterfly(sketch[0], "gy", last=True)
    tall, packed = call(
        gram_kernel,
        [f32(sketch_rows, width), f32(width // 2 + SUB, width)],
        "gram",
        [mine, theirs],
    )
    first, second = butterfly(packed, "gx", last=True)
    depth = comps * (layers // 2)
    basis, factor = call(
        partial(factor_kernel, math.sqrt(sketch_rows * n_x)),
        [f32(half, depth // n_y, width), f32(width, width)],
        "factor",
        [first, second, tall.reshape(half, depth, width)],
    )
    return (final, basis, factor)


def solution(mesh):
    in_specs = (
        P(None, None, "gx", "gy"),
        P(None, None, "gx", "gy"),
        P(None, None, "gx", "gy"),
        P(None, "gx", "gy"),
        P(None, None, "gx", "gy"),
        P(None, "gx", "gy"),
        P(None, "gy", None),
    )
    out_specs = (P(None, None, "gx", "gy"), P("gx", "gy", None), P())
    return jax.shard_map(shards, mesh=mesh, in_specs=in_specs, out_specs=out_specs, check_vma=False)
```

time: 1000 us -> 101 us (0.10); the launches traced: 987 us -> 100 us
  matrix products: 478 us -> 0 us
  other arithmetic: 116 us -> 0.02 us
  loops' own time: 98.3 us -> 0 us
  waiting for transfers between devices: 139 us -> 47.7 us
  local copies, waits for them, and re-layouts: 81.5 us -> 3.8 us
  starting transfers between devices: 58 us -> 31.6 us
  Pallas kernels: 0 us -> 16.2 us
  between operations: 15.7 us -> 0.97 us
    dot_general x646 -> x0, matrix products: 478 us -> none  [the longest x128 124 us: column_step(): column = jnp.dot(gram, picker, precision=lax.Precision.HIGHEST)]
    psum x1 -> x0, waiting for transfers between devices: 124 us -> none  [shards(): gram_whole = lax.psum(gram_local, ('gx', 'gy'))]
    another operation x2 -> x0, loops' own time: 98.3 us -> none  [the longest x1 94 us: lower_factor(): return lax.fori_loop(0, order, column_step, jnp.zeros_like(gram))]
    add x264 -> x3, other arithmetic: 49.7 us -> 0.02 us  [butterfly(): value = value + other]
    slice x28 -> x0, local copies, waits for them, and re-layouts: 40.9 us -> none  [the longest x4 27.8 us: shards(): sampled = velocities[:, ::2, ::2, ::2]]
    div x12 -> x0, other arithmetic: 40.1 us -> none  [the longest x8 32.5 us: fourth(): return (segment(0) - segment(4) + 8.0 * (segment(3) - segment(1))) / 12.0]
    ppermute x20 -> x21, waiting for transfers between devices: 8.01 us -> 47.7 us  [the longest x8 33.9 us: along_x(): return lax.ppermute(value, 'gx', pairs)]
    ppermute x20 -> x21, starting transfers between devices: 57.9 us -> 31.6 us  [the longest x8 21.4 us: along_x(): return lax.ppermute(value, 'gx', pairs)]
  transfers between devices with their start and end apart: 22 -> 21, of which waited for: 5 -> 21; matrix products, arithmetic and copies ran while one was open for 6% -> 0% of each run, Pallas kernels for 0% -> 7%
where the time goes in v3:
time: 101 us; the launch traced here: 100 us
  waiting for transfers between devices  47.7 us (47%)
  starting transfers between devices  31.6 us (31%)
  Pallas kernels  16.2 us (16%)
  local copies, waits for them, and re-layouts  3.8 us (4%)
    ppermute x8, waiting for transfers between devices, along_x(): return lax.ppermute(value, 'gx', pairs)  33.9 us
    ppermute x8, starting transfers between devices, along_x(): return lax.ppermute(value, 'gx', pairs)  21.4 us
    pallas_call x25, Pallas kernels, call(): pl.pallas_call(kernel, out_shape=outs, in_specs=specs or [VMEM] * len(ins...  16.2 us
    ppermute x5, starting transfers between devices, butterfly(): other = lax.ppermute(value, axis, [(i, i ^ bit) for i in range(count)])  9.66 us
    ppermute x5, waiting for transfers between devices, butterfly(): other = lax.ppermute(value, axis, [(i, i ^ bit) for i in range(count)])  8.42 us
    ppermute x8, waiting for transfers between devices, along_y(): return [lax.ppermute(value, 'gy', [(0, 1), (1, 0)])]  5.39 us
    unnamed x14, local copies, waits for them, and re-layouts  3.8 us
  transfers between devices with their start and end apart: 21, of which 21 were waited for; matrix products, arithmetic and copies ran while one was open for 0% of the time, Pallas kernels for 7%

profile of v3, /device:TPU:0, one launch (start us, length us, event | category | flops | bytes accessed | tf_op | source)
XLA Modules:
  0.0 100.3 jit_solution(7028916773092125961)
XLA Ops:
  4.4 1.2 %begin.1 = (f32[22,32,128]{2,1,0:T(8,128)S(1)}, f32[22,32,128]{2,1,0:T(8,128)S(1)}, f32[8,32,128]{2,1,0:T(8,128)S(1)}, f32[5,8,32,128]{3,2,1,0:T(8,128)S(1)}) custom-call(f32[3,256,128]{2,1,0:T(8,128)S(1)} %bitcast.8, f32[2,256,128]{2,1,0:T(8,128)S(1)} %bitcast.11, f32[256,128]{1,0:T(8,128)S(1)} %bitcast.14, f32[2,256,128]{2,1,0:T(8,128)S(1)} %bitcast.12), custom_call_target="tpu_custom_call" | custom-call | bytes 2555904 | tf_op jit(solution)/shard_map/begin/pallas_call | solution.py:597
  5.6 4.9 %collective-permute-start = (f32[22,32,128]{2,1,0:T(8,128)S(1)}, f32[22,32,128]{2,1,0:T(8,128)S(1)}, u32[]{:S(2)}, u32[]{:S(2)}) collective-permute-start(f32[22,32,128]{2,1,0:T(8,128)S(1)} %get-tuple-element.49.refs_1_.high_ref.before_high.refs_3_), channel_id=1, source_target_pairs={{0,2},{2,4},{4,6},{6,8},{8,10},{10,12},{12,14},{14,16},{16,18},{18... | collective-permute-start | bytes 1081352 | tf_op jit(solution)/shard_map/ppermute | solution.py:636
  10.5 1.3 %collective-permute-start.1 = (f32[22,32,128]{2,1,0:T(8,128)S(1)}, f32[22,32,128]{2,1,0:T(8,128)S(1)}, u32[]{:S(2)}, u32[]{:S(2)}) collective-permute-start(f32[22,32,128]{2,1,0:T(8,128)S(1)} %get-tuple-element.50.refs_0_.low_ref.before_low.refs_2_), channel_id=1, source_target_pairs={{2,0},{4,2},{6,4},{8,6},{10,8},{12,10},{14,12},{16,14},{18,16},{20... | collective-permute-start | bytes 1081352 | tf_op jit(solution)/shard_map/ppermute | solution.py:636
  13.8 12.1 %collective-permute-done.below_ref.first_below.refs_1_ = f32[22,32,128]{2,1,0:T(8,128)S(1)} collective-permute-done((f32[22,32,128]{2,1,0:T(8,128)S(1)}, f32[22,32,128]{2,1,0:T(8,128)S(1)}, u32[]{:S(2)}, u32[]{:S(2)}) %collective-permute-start) | collective-permute-done | bytes 360480 | tf_op jit(solution)/shard_map/ppermute | solution.py:636
  25.9 1.9 %collective-permute-done.1.above_ref.first_above.refs_2_ = f32[22,32,128]{2,1,0:T(8,128)S(1)} collective-permute-done((f32[22,32,128]{2,1,0:T(8,128)S(1)}, f32[22,32,128]{2,1,0:T(8,128)S(1)}, u32[]{:S(2)}, u32[]{:S(2)}) %collective-permute-start.1) | collective-permute-done | bytes 360480 | tf_op jit(solution)/shard_map/ppermute | solution.py:636
  29.7 3.4 %collective-permute-start.4 = (f32[12,32,128]{2,1,0:T(8,128)S(1)}, f32[12,32,128]{2,1,0:T(8,128)S(1)}, u32[]{:S(2)}, u32[]{:S(2)}) collective-permute-start(f32[12,32,128]{2,1,0:T(8,128)S(1)} %get-tuple-element.62.refs_1_.high_ref.before_high.refs_3_), channel_id=1, source_target_pairs={{0,2},{2,4},{4,6},{6,8},{8,10},{10,12},{12,14},{14,16},{16,18},{18... | collective-permute-start | bytes 589832 | tf_op jit(solution)/shard_map/ppermute | solution.py:636
  33.1 1.3 %collective-permute-start.5 = (f32[12,32,128]{2,1,0:T(8,128)S(1)}, f32[12,32,128]{2,1,0:T(8,128)S(1)}, u32[]{:S(2)}, u32[]{:S(2)}) collective-permute-start(f32[12,32,128]{2,1,0:T(8,128)S(1)} %get-tuple-element.63.refs_0_.low_ref.before_low.refs_2_), channel_id=1, source_target_pairs={{2,0},{4,2},{6,4},{8,6},{10,8},{12,10},{14,12},{16,14},{18,16},{20... | collective-permute-start | bytes 589832 | tf_op jit(solution)/shard_map/ppermute | solution.py:636
  36.2 1.3 %collective-permute-done.4.below_ref = f32[12,32,128]{2,1,0:T(8,128)S(1)} collective-permute-done((f32[12,32,128]{2,1,0:T(8,128)S(1)}, f32[12,32,128]{2,1,0:T(8,128)S(1)}, u32[]{:S(2)}, u32[]{:S(2)}) %collective-permute-start.4) | collective-permute-done | bytes 196640 | tf_op jit(solution)/shard_map/ppermute | solution.py:636
  37.6 5.0 %collective-permute-done.5.above_ref = f32[12,32,128]{2,1,0:T(8,128)S(1)} collective-permute-done((f32[12,32,128]{2,1,0:T(8,128)S(1)}, f32[12,32,128]{2,1,0:T(8,128)S(1)}, u32[]{:S(2)}, u32[]{:S(2)}) %collective-permute-start.5) | collective-permute-done | bytes 196640 | tf_op jit(solution)/shard_map/ppermute | solution.py:636
  44.4 2.3 %collective-permute-start.8 = (f32[12,32,128]{2,1,0:T(8,128)S(1)}, f32[12,32,128]{2,1,0:T(8,128)S(1)}, u32[]{:S(2)}, u32[]{:S(2)}) collective-permute-start(f32[12,32,128]{2,1,0:T(8,128)S(1)} %get-tuple-element.71.refs_1_.high_ref.before_high.refs_3_), channel_id=1, source_target_pairs={{0,2},{2,4},{4,6},{6,8},{8,10},{10,12},{12,14},{14,16},{16,18},{18... | collective-permute-start | bytes 589832 | tf_op jit(solution)/shard_map/ppermute | solution.py:636
  46.6 1.3 %collective-permute-start.9 = (f32[12,32,128]{2,1,0:T(8,128)S(1)}, f32[12,32,128]{2,1,0:T(8,128)S(1)}, u32[]{:S(2)}, u32[]{:S(2)}) collective-permute-start(f32[12,32,128]{2,1,0:T(8,128)S(1)} %get-tuple-element.72.refs_0_.low_ref.before_low.refs_2_), channel_id=1, source_target_pairs={{2,0},{4,2},{6,4},{8,6},{10,8},{12,10},{14,12},{16,14},{18,16},{20... | collective-permute-start | bytes 589832 | tf_op jit(solution)/shard_map/ppermute | solution.py:636
  49.8 1.3 %collective-permute-done.8.below_ref = f32[12,32,128]{2,1,0:T(8,128)S(1)} collective-permute-done((f32[12,32,128]{2,1,0:T(8,128)S(1)}, f32[12,32,128]{2,1,0:T(8,128)S(1)}, u32[]{:S(2)}, u32[]{:S(2)}) %collective-permute-start.8) | collective-permute-done | bytes 196640 | tf_op jit(solution)/shard_map/ppermute | solution.py:636
  51.1 6.2 %collective-permute-done.9.above_ref = f32[12,32,128]{2,1,0:T(8,128)S(1)} collective-permute-done((f32[12,32,128]{2,1,0:T(8,128)S(1)}, f32[12,32,128]{2,1,0:T(8,128)S(1)}, u32[]{:S(2)}, u32[]{:S(2)}) %collective-permute-start.9) | collective-permute-done | bytes 196640 | tf_op jit(solution)/shard_map/ppermute | solution.py:636
  59.1 5.4 %collective-permute-start.12 = (f32[12,32,128]{2,1,0:T(8,128)S(1)}, f32[12,32,128]{2,1,0:T(8,128)S(1)}, u32[]{:S(2)}, u32[]{:S(2)}) collective-permute-start(f32[12,32,128]{2,1,0:T(8,128)S(1)} %get-tuple-element.80.refs_1_.high_ref), channel_id=1, source_target_pairs={{0,2},{2,4},{4,6},{6,8},{8,10},{10,12},{12,14},{14,16},{16,18},{18... | collective-permute-start | bytes 589832 | tf_op jit(solution)/shard_map/ppermute | solution.py:636
  64.6 1.5 %collective-permute-start.13 = (f32[12,32,128]{2,1,0:T(8,128)S(1)}, f32[12,32,128]{2,1,0:T(8,128)S(1)}, u32[]{:S(2)}, u32[]{:S(2)}) collective-permute-start(f32[12,32,128]{2,1,0:T(8,128)S(1)} %get-tuple-element.81.refs_0_.low_ref), channel_id=1, source_target_pairs={{2,0},{4,2},{6,4},{8,6},{10,8},{12,10},{14,12},{16,14},{18,16},{20... | collective-permute-start | bytes 589832 | tf_op jit(solution)/shard_map/ppermute | solution.py:636
  69.1 5.0 %collective-permute-done.13.above_ref = f32[12,32,128]{2,1,0:T(8,128)S(1)} collective-permute-done((f32[12,32,128]{2,1,0:T(8,128)S(1)}, f32[12,32,128]{2,1,0:T(8,128)S(1)}, u32[]{:S(2)}, u32[]{:S(2)}) %collective-permute-start.13) | collective-permute-done | bytes 196640 | tf_op jit(solution)/shard_map/ppermute | solution.py:636
  77.8 2.6 %collective-permute-start.17 = (f32[72,128]{1,0:T(8,128)S(1)}, f32[72,128]{1,0:T(8,128)S(1)}, u32[]{:S(2)}, u32[]{:S(2)}) collective-permute-start(f32[72,128]{1,0:T(8,128)S(1)} %get-tuple-element.91), channel_id=1, source_target_pairs={{0,2},{2,0},{4,6},{6,4},{8,10},{10,8},{12,14},{14,12},{16,18},{18,... | collective-permute-start | bytes 110600 | tf_op jit(solution)/shard_map/ppermute | solution.py:616
  80.4 1.9 %collective-permute-done.17 = f32[72,128]{1,0:T(8,128)S(1)} collective-permute-done((f32[72,128]{1,0:T(8,128)S(1)}, f32[72,128]{1,0:T(8,128)S(1)}, u32[]{:S(2)}, u32[]{:S(2)}) %collective-permute-start.17) | collective-permute-done | bytes 36896 | tf_op jit(solution)/shard_map/ppermute | solution.py:616
  82.4 1.5 %collective-permute-start.18 = (f32[72,128]{1,0:T(8,128)S(1)}, f32[72,128]{1,0:T(8,128)S(1)}, u32[]{:S(2)}, u32[]{:S(2)}) collective-permute-start(f32[72,128]{1,0:T(8,128)S(1)} %add.9), channel_id=1, source_target_pairs={{0,4},{2,6},{4,0},{6,2},{8,12},{10,14},{12,8},{14,10},{16,20},{18,... | collective-permute-start | bytes 110600 | tf_op jit(solution)/shard_map/ppermute | solution.py:616
  83.9 2.4 %collective-permute-done.18 = f32[72,128]{1,0:T(8,128)S(1)} collective-permute-done((f32[72,128]{1,0:T(8,128)S(1)}, f32[72,128]{1,0:T(8,128)S(1)}, u32[]{:S(2)}, u32[]{:S(2)}) %collective-permute-start.18) | collective-permute-done | bytes 36896 | tf_op jit(solution)/shard_map/ppermute | solution.py:616
  86.3 2.2 %collective-permute-start.19 = (f32[72,128]{1,0:T(8,128)S(1)}, f32[72,128]{1,0:T(8,128)S(1)}, u32[]{:S(2)}, u32[]{:S(2)}) collective-permute-start(f32[72,128]{1,0:T(8,128)S(1)} %add.10), channel_id=1, source_target_pairs={{0,8},{2,10},{4,12},{6,14},{8,0},{10,2},{12,4},{14,6},{16,24},{18,... | collective-permute-start | bytes 110600 | tf_op jit(solution)/shard_map/ppermute | solution.py:616
  88.6 1.9 %collective-permute-done.19 = f32[72,128]{1,0:T(8,128)S(1)} collective-permute-done((f32[72,128]{1,0:T(8,128)S(1)}, f32[72,128]{1,0:T(8,128)S(1)}, u32[]{:S(2)}, u32[]{:S(2)}) %collective-permute-start.19) | collective-permute-done | bytes 36896 | tf_op jit(solution)/shard_map/ppermute | solution.py:616
  90.5 3.0 %collective-permute-start.20 = (f32[72,128]{1,0:T(8,128)S(1)}, f32[72,128]{1,0:T(8,128)S(1)}, u32[]{:S(2)}, u32[]{:S(2)}) collective-permute-start(f32[72,128]{1,0:T(8,128)S(1)} %add.11.first_ref), channel_id=1, source_target_pairs={{0,16},{2,18},{4,20},{6,22},{8,24},{10,26},{12,28},{14,30},{16,0},... | collective-permute-start | bytes 110600 | tf_op jit(solution)/shard_map/ppermute | solution.py:616
  95.5 4.8 %factor.1 = (f32[4,24,128]{2,1,0:T(8,128)}, f32[128,128]{1,0:T(8,128)}) custom-call(f32[72,128]{1,0:T(8,128)S(1)} %add.11.first_ref, f32[72,128]{1,0:T(8,128)S(1)} %collective-permute-done.20.second_ref, f32[4,48,128]{2,1,0:T(8,128)S(1)} %bitcast.15), custom_call_target="tpu_custom_call" | custom-call | bytes 286720 | tf_op jit(solution)/shard_map/factor/pallas_call | solution.py:597
  (60 shorter events, 23.4 us)
Async XLA Ops:
  4.4 7.5 %copy-start.2 = (f32[3,32,8,128]{3,2,1,0:T(8,128)S(1)}, f32[3,32,8,128]{3,2,1,0:T(8,128)}, u32[]{:S(2)}) copy-start(f32[3,32,8,128]{3,2,1,0:T(8,128)} %param.8) | copy-start | bytes 1179652
  4.4 7.5 %copy-start.5 = (f32[32,8,128]{2,1,0:T(8,128)S(1)}, f32[32,8,128]{2,1,0:T(8,128)}, u32[]{:S(2)}) copy-start(f32[32,8,128]{2,1,0:T(8,128)} %param.12) | copy-start | bytes 393220
  5.6 20.3 %collective-permute-start = (f32[22,32,128]{2,1,0:T(8,128)S(1)}, f32[22,32,128]{2,1,0:T(8,128)S(1)}, u32[]{:S(2)}, u32[]{:S(2)}) collective-permute-start(f32[22,32,128]{2,1,0:T(8,128)S(1)} %get-tuple-element.49.refs_1_.high_ref.before_high.refs_3_), channel_id=1, source_target_pairs={{0,2},{2,4},{4,6},{6,8},{8,10},{10,12},{12,14},{14,16},{16,18},{18... | collective-permute-start | bytes 1081352 | tf_op jit(solution)/shard_map/ppermute | solution.py:636
  10.5 17.3 %collective-permute-start.1 = (f32[22,32,128]{2,1,0:T(8,128)S(1)}, f32[22,32,128]{2,1,0:T(8,128)S(1)}, u32[]{:S(2)}, u32[]{:S(2)}) collective-permute-start(f32[22,32,128]{2,1,0:T(8,128)S(1)} %get-tuple-element.50.refs_0_.low_ref.before_low.refs_2_), channel_id=1, source_target_pairs={{2,0},{4,2},{6,4},{8,6},{10,8},{12,10},{14,12},{16,14},{18,16},{20... | collective-permute-start | bytes 1081352 | tf_op jit(solution)/shard_map/ppermute | solution.py:636
  11.8 1.4 %collective-permute-start.2 = (f32[8,32,128]{2,1,0:T(8,128)S(1)}, f32[8,32,128]{2,1,0:T(8,128)S(1)}, u32[]{:S(2)}, u32[]{:S(2)}) collective-permute-start(f32[8,32,128]{2,1,0:T(8,128)S(1)} %get-tuple-element.51.refs_2_.refs_5_), channel_id=1, source_target_pairs={{0,1},{1,0},{2,3},{3,2},{4,5},{5,4},{6,7},{7,6},{8,9},{9,8},{10,11... | collective-permute-start | bytes 393224 | tf_op jit(solution)/shard_map/ppermute | solution.py:640
  27.9 1.3 %collective-permute-start.3 = (f32[2,32,128]{2,1,0:T(8,128)S(1)}, f32[2,32,128]{2,1,0:T(8,128)S(1)}, u32[]{:S(2)}, u32[]{:S(2)}) collective-permute-start(f32[2,32,128]{2,1,0:T(8,128)S(1)} %corner_0.1), channel_id=1, source_target_pairs={{0,1},{1,0},{2,3},{3,2},{4,5},{5,4},{6,7},{7,6},{8,9},{9,8},{10,11... | collective-permute-start | bytes 98312 | tf_op jit(solution)/shard_map/ppermute | solution.py:640
  29.2 5.3 %copy-start = (f32[4,64,128]{2,1,0:T(8,128)S(1)}, f32[4,64,128]{2,1,0:T(8,128)}, u32[]{:S(2)}) copy-start(f32[4,64,128]{2,1,0:T(8,128)} %refs_4_.7) | copy-start | bytes 393220
  29.7 7.9 %collective-permute-start.4 = (f32[12,32,128]{2,1,0:T(8,128)S(1)}, f32[12,32,128]{2,1,0:T(8,128)S(1)}, u32[]{:S(2)}, u32[]{:S(2)}) collective-permute-start(f32[12,32,128]{2,1,0:T(8,128)S(1)} %get-tuple-element.62.refs_1_.high_ref.before_high.refs_3_), channel_id=1, source_target_pairs={{0,2},{2,4},{4,6},{6,8},{8,10},{10,12},{12,14},{14,16},{16,18},{18... | collective-permute-start | bytes 589832 | tf_op jit(solution)/shard_map/ppermute | solution.py:636
  33.1 9.4 %collective-permute-start.5 = (f32[12,32,128]{2,1,0:T(8,128)S(1)}, f32[12,32,128]{2,1,0:T(8,128)S(1)}, u32[]{:S(2)}, u32[]{:S(2)}) collective-permute-start(f32[12,32,128]{2,1,0:T(8,128)S(1)} %get-tuple-element.63.refs_0_.low_ref.before_low.refs_2_), channel_id=1, source_target_pairs={{2,0},{4,2},{6,4},{8,6},{10,8},{12,10},{14,12},{16,14},{18,16},{20... | collective-permute-start | bytes 589832 | tf_op jit(solution)/shard_map/ppermute | solution.py:636
  34.4 1.3 %collective-permute-start.6 = (f32[3,32,128]{2,1,0:T(8,128)S(1)}, f32[3,32,128]{2,1,0:T(8,128)S(1)}, u32[]{:S(2)}, u32[]{:S(2)}) collective-permute-start(f32[3,32,128]{2,1,0:T(8,128)S(1)} %get-tuple-element.64.refs_2_), channel_id=1, source_target_pairs={{0,1},{1,0},{2,3},{3,2},{4,5},{5,4},{6,7},{7,6},{8,9},{9,8},{10,11... | collective-permute-start | bytes 147464 | tf_op jit(solution)/shard_map/ppermute | solution.py:640
  42.6 1.3 %collective-permute-start.7 = (f32[2,32,128]{2,1,0:T(8,128)S(1)}, f32[2,32,128]{2,1,0:T(8,128)S(1)}, u32[]{:S(2)}, u32[]{:S(2)}) collective-permute-start(f32[2,32,128]{2,1,0:T(8,128)S(1)} %corner_1.1), channel_id=1, source_target_pairs={{0,1},{1,0},{2,3},{3,2},{4,5},{5,4},{6,7},{7,6},{8,9},{9,8},{10,11... | collective-permute-start | bytes 98312 | tf_op jit(solution)/shard_map/ppermute | solution.py:640
  44.4 6.7 %collective-permute-start.8 = (f32[12,32,128]{2,1,0:T(8,128)S(1)}, f32[12,32,128]{2,1,0:T(8,128)S(1)}, u32[]{:S(2)}, u32[]{:S(2)}) collective-permute-start(f32[12,32,128]{2,1,0:T(8,128)S(1)} %get-tuple-element.71.refs_1_.high_ref.before_high.refs_3_), channel_id=1, source_target_pairs={{0,2},{2,4},{4,6},{6,8},{8,10},{10,12},{12,14},{14,16},{16,18},{18... | collective-permute-start | bytes 589832 | tf_op jit(solution)/shard_map/ppermute | solution.py:636
  46.6 10.7 %collective-permute-start.9 = (f32[12,32,128]{2,1,0:T(8,128)S(1)}, f32[12,32,128]{2,1,0:T(8,128)S(1)}, u32[]{:S(2)}, u32[]{:S(2)}) collective-permute-start(f32[12,32,128]{2,1,0:T(8,128)S(1)} %get-tuple-element.72.refs_0_.low_ref.before_low.refs_2_), channel_id=1, source_target_pairs={{2,0},{4,2},{6,4},{8,6},{10,8},{12,10},{14,12},{16,14},{18,16},{20... | collective-permute-start | bytes 589832 | tf_op jit(solution)/shard_map/ppermute | solution.py:636
  47.9 1.3 %collective-permute-start.10 = (f32[3,32,128]{2,1,0:T(8,128)S(1)}, f32[3,32,128]{2,1,0:T(8,128)S(1)}, u32[]{:S(2)}, u32[]{:S(2)}) collective-permute-start(f32[3,32,128]{2,1,0:T(8,128)S(1)} %get-tuple-element.73.refs_2_), channel_id=1, source_target_pairs={{0,1},{1,0},{2,3},{3,2},{4,5},{5,4},{6,7},{7,6},{8,9},{9,8},{10,11... | collective-permute-start | bytes 147464 | tf_op jit(solution)/shard_map/ppermute | solution.py:640
  57.4 1.3 %collective-permute-start.11 = (f32[2,32,128]{2,1,0:T(8,128)S(1)}, f32[2,32,128]{2,1,0:T(8,128)S(1)}, u32[]{:S(2)}, u32[]{:S(2)}) collective-permute-start(f32[2,32,128]{2,1,0:T(8,128)S(1)} %corner_2.1), channel_id=1, source_target_pairs={{0,1},{1,0},{2,3},{3,2},{4,5},{5,4},{6,7},{7,6},{8,9},{9,8},{10,11... | collective-permute-start | bytes 98312 | tf_op jit(solution)/shard_map/ppermute | solution.py:640
  59.1 9.9 %collective-permute-start.12 = (f32[12,32,128]{2,1,0:T(8,128)S(1)}, f32[12,32,128]{2,1,0:T(8,128)S(1)}, u32[]{:S(2)}, u32[]{:S(2)}) collective-permute-start(f32[12,32,128]{2,1,0:T(8,128)S(1)} %get-tuple-element.80.refs_1_.high_ref), channel_id=1, source_target_pairs={{0,2},{2,4},{4,6},{6,8},{8,10},{10,12},{12,14},{14,16},{16,18},{18... | collective-permute-start | bytes 589832 | tf_op jit(solution)/shard_map/ppermute | solution.py:636
  64.6 9.4 %collective-permute-start.13 = (f32[12,32,128]{2,1,0:T(8,128)S(1)}, f32[12,32,128]{2,1,0:T(8,128)S(1)}, u32[]{:S(2)}, u32[]{:S(2)}) collective-permute-start(f32[12,32,128]{2,1,0:T(8,128)S(1)} %get-tuple-element.81.refs_0_.low_ref), channel_id=1, source_target_pairs={{2,0},{4,2},{6,4},{8,6},{10,8},{12,10},{14,12},{16,14},{18,16},{20... | collective-permute-start | bytes 589832 | tf_op jit(solution)/shard_map/ppermute | solution.py:636
  66.1 1.3 %collective-permute-start.14 = (f32[3,32,128]{2,1,0:T(8,128)S(1)}, f32[3,32,128]{2,1,0:T(8,128)S(1)}, u32[]{:S(2)}, u32[]{:S(2)}) collective-permute-start(f32[3,32,128]{2,1,0:T(8,128)S(1)} %get-tuple-element.82.refs_2_), channel_id=1, source_target_pairs={{0,1},{1,0},{2,3},{3,2},{4,5},{5,4},{6,7},{7,6},{8,9},{9,8},{10,11... | collective-permute-start | bytes 147464 | tf_op jit(solution)/shard_map/ppermute | solution.py:640
  74.1 1.3 %collective-permute-start.15 = (f32[2,32,128]{2,1,0:T(8,128)S(1)}, f32[2,32,128]{2,1,0:T(8,128)S(1)}, u32[]{:S(2)}, u32[]{:S(2)}) collective-permute-start(f32[2,32,128]{2,1,0:T(8,128)S(1)} %corner_3.1), channel_id=1, source_target_pairs={{0,1},{1,0},{2,3},{3,2},{4,5},{5,4},{6,7},{7,6},{8,9},{9,8},{10,11... | collective-permute-start | bytes 98312 | tf_op jit(solution)/shard_map/ppermute | solution.py:640
  76.0 1.4 %collective-permute-start.16 = (f32[192,128]{1,0:T(8,128)S(1)}, f32[192,128]{1,0:T(8,128)S(1)}, u32[]{:S(2)}, u32[]{:S(2)}) collective-permute-start(f32[192,128]{1,0:T(8,128)S(1)} %sketch_3.1.first_ref), channel_id=1, source_target_pairs={{0,1},{1,0},{2,3},{3,2},{4,5},{5,4},{6,7},{7,6},{8,9},{9,8},{10,11... | collective-permute-start | bytes 294920 | tf_op jit(solution)/shard_map/ppermute | solution.py:616
  77.8 4.6 %collective-permute-start.17 = (f32[72,128]{1,0:T(8,128)S(1)}, f32[72,128]{1,0:T(8,128)S(1)}, u32[]{:S(2)}, u32[]{:S(2)}) collective-permute-start(f32[72,128]{1,0:T(8,128)S(1)} %get-tuple-element.91), channel_id=1, source_target_pairs={{0,2},{2,0},{4,6},{6,4},{8,10},{10,8},{12,14},{14,12},{16,18},{18,... | collective-permute-start | bytes 110600 | tf_op jit(solution)/shard_map/ppermute | solution.py:616
  82.4 4.0 %collective-permute-start.18 = (f32[72,128]{1,0:T(8,128)S(1)}, f32[72,128]{1,0:T(8,128)S(1)}, u32[]{:S(2)}, u32[]{:S(2)}) collective-permute-start(f32[72,128]{1,0:T(8,128)S(1)} %add.9), channel_id=1, source_target_pairs={{0,4},{2,6},{4,0},{6,2},{8,12},{10,14},{12,8},{14,10},{16,20},{18,... | collective-permute-start | bytes 110600 | tf_op jit(solution)/shard_map/ppermute | solution.py:616
  86.3 4.2 %collective-permute-start.19 = (f32[72,128]{1,0:T(8,128)S(1)}, f32[72,128]{1,0:T(8,128)S(1)}, u32[]{:S(2)}, u32[]{:S(2)}) collective-permute-start(f32[72,128]{1,0:T(8,128)S(1)} %add.10), channel_id=1, source_target_pairs={{0,8},{2,10},{4,12},{6,14},{8,0},{10,2},{12,4},{14,6},{16,24},{18,... | collective-permute-start | bytes 110600 | tf_op jit(solution)/shard_map/ppermute | solution.py:616
  90.5 5.0 %collective-permute-start.20 = (f32[72,128]{1,0:T(8,128)S(1)}, f32[72,128]{1,0:T(8,128)S(1)}, u32[]{:S(2)}, u32[]{:S(2)}) collective-permute-start(f32[72,128]{1,0:T(8,128)S(1)} %add.11.first_ref), channel_id=1, source_target_pairs={{0,16},{2,18},{4,20},{6,22},{8,24},{10,26},{12,28},{14,30},{16,0},... | collective-permute-start | bytes 110600 | tf_op jit(solution)/shard_map/ppermute | solution.py:616
  (4 other events, 3.8 us)

commit v4 on v3

--- a/solution.py
+++ b/solution.py
@@ -129,15 +129,44 @@
     return 8.0 * near if far is None else far + 8.0 * near
 
 
-def halves(low_ref, high_ref, half):
+def halves(far_ref, near_ref, half):
     def at(c, x):
-        return low_ref[c * half + x] if x < half else high_ref[c * half + x - half]
+        return far_ref[c * half + x] if x < half else near_ref[c * half + x - half]
 
     return at
 
 
+def is_odd():
+    return lax.axis_index("gx") % 2 == 1
+
+
+def mirrored(values, odd, flip=False):
+    other = [-value if flip else value for value in values[::-1]]
+    return [jnp.where(odd, second, first) for first, second in zip(values, other)]
+
+
+class Side:
+    def __init__(self, far, x_count):
+        self.far, self.half, self.x_count = far, x_count // 2, x_count
+        self.inside = range(self.half) if far else range(self.half, x_count)
+        self.outside = (-2, -1) if far else (x_count, x_count + 1)
+
+    def depth(self, x):
+        return -1 - x if self.far else x - self.x_count
+
+    def halo(self, ref, c, x):
+        place = self.depth(x) if self.far else self.half - 1 - self.depth(x)
+        value = ref[c * self.half + place]
+        return -value if c == 0 else value
+
+    def metric(self, ref, comps, m, x):
+        place = self.depth(x) if self.far else 1 - self.depth(x)
+        value = ref[comps * self.half + 2 * m + place]
+        return -value if m == 0 else value
+
+
 def begin_kernel(*refs):
-    sources, (down_ref, up_ref, edge_ref, metric_ref) = refs[:4], refs[4:8]
+    sources, (far_ref, near_ref, edge_ref, metric_ref) = refs[:4], refs[4:8]
     u_ref, slope_ref, stretch_ref, moduli_ref = refs[8:12]
     sems = refs[12]
     copies = [
@@ -150,12 +179,13 @@
     x_count, rows, y_count = metric_ref.shape[1:]
     half = x_count // 2
     comps = u_ref.shape[0]
+    odd = is_odd()
     for c in range(comps):
         at = strided(u_ref, x_count, rows, (c,))
-        slabs = [at(x) for x in range(x_count)]
+        slabs = mirrored([at(x) for x in range(x_count)], odd, c == 0)
         for k in range(half):
-            down_ref[c * half + k] = slabs[k]
-            up_ref[c * half + k] = slabs[half + k]
+            far_ref[c * half + k] = slabs[k]
+            near_ref[c * half + k] = slabs[half + k]
         edge_ref[c] = edge_message(lambda x: slabs[x], x_count, rows, y_count)
     for copy in copies[1:]:
         copy.wait()
@@ -167,39 +197,41 @@
         (strided(moduli_ref, x_count, rows, (1,)), 1.0 / 12.0),
     ]
     for m, (at, scale) in enumerate(fields):
-        slabs = [at(x) if scale is None else at(x) * scale for x in range(x_count)]
+        slabs = mirrored([at(x) for x in range(x_count)], odd, m == 0)
+        if scale is not None:
+            slabs = [slab * scale for slab in slabs]
         for x in range(x_count):
             metric_ref[m, x] = slabs[x]
         for k in range(2):
-            down_ref[comps * half + 2 * m + k] = slabs[k]
-            up_ref[comps * half + 2 * m + k] = slabs[x_count - 2 + k]
+            far_ref[comps * half + 2 * m + k] = slabs[k]
+            near_ref[comps * half + 2 * m + k] = slabs[x_count - 2 + k]
         edge_ref[comps + m] = edge_message(lambda x: slabs[x], x_count, rows, y_count)
 
 
-def rest_kernel(u_ref, v_ref, buoyancy_ref, before_low, before_high, push_ref):
+def rest_kernel(u_ref, v_ref, buoyancy_ref, before_far, before_near, push_ref):
     x_count, rows, _ = push_ref.shape
     half = x_count // 2
+    odd = is_odd()
     at = strided(buoyancy_ref, x_count, rows)
-    for x in range(x_count):
-        push_ref[x] = at(x) * (time_step**2 / 12.0)
+    for x, value in enumerate(mirrored([at(x) for x in range(x_count)], odd)):
+        push_ref[x] = value * (time_step**2 / 12.0)
     for c in range(u_ref.shape[0]):
         at, rate = strided(u_ref, x_count, rows, (c,)), strided(v_ref, x_count, rows, (c,))
-        for x in range(x_count):
-            (before_low if x < half else before_high)[c * half + x % half] = (
-                at(x) - time_step * rate(x)
-            )
-
-
-def corner_kernel(half, below_ref, above_ref, *refs):
+        before = [at(x) - time_step * rate(x) for x in range(x_count)]
+        for x, value in enumerate(mirrored(before, odd, c == 0)):
+            (before_far if x < half else before_near)[c * half + x % half] = value
+
+
+def corner_kernel(far, half, halo_ref, *refs):
     corner_ref = refs[-1]
-    rows, y_count = below_ref.shape[1:]
-    x_count = 2 * half
+    rows, y_count = halo_ref.shape[1:]
+    side = Side(far, 2 * half)
+    places = {x % side.x_count: x for x in side.outside}
     for c in range(corner_ref.shape[0]):
-
-        def load(x):
-            return below_ref[c * half + x - half] if x >= half else above_ref[c * half + x]
-
-        corner_ref[c] = edge_message(load, x_count, rows, y_count, (0, 1, x_count - 2, x_count - 1))
+        corner_ref[c] = edge_message(
+            lambda place: side.halo(halo_ref, c, places[place]),
+            side.x_count, rows, y_count, tuple(places),
+        )
 
 
 def all_stresses(grads, lame, shear):
@@ -286,29 +318,32 @@
 
 
 def wide_kernel(
-    low_ref, high_ref, below_ref, above_ref, before_low, before_high, metric_ref, push_ref,
-    first_below, first_above, s_x, s_o, e_s, out_low, out_high, out_edge,
+    far, far_ref, near_ref, halo_ref, before_ref, metric_ref, push_ref, first_halo, s_x, s_o, e_s,
+    out_ref, out_edge,
 ):
     x_count, rows, y_count = metric_ref.shape[1:]
     half, window = x_count // 2, y_count // x_count
     comps = s_x.shape[0]
-    inner = halves(low_ref, high_ref, half)
-    past = halves(before_low, before_high, half)
+    side = Side(far, x_count)
+    inner = halves(far_ref, near_ref, half)
     band = band_matrix(y_count)
+    steps = (-2, -1, 1, 2)
 
     def u(c, x):
-        if x < 0:
-            return below_ref[c * half + half + x]
-        return above_ref[c * half + x - x_count] if x >= x_count else inner(c, x)
+        return inner(c, x) if 0 <= x < x_count else side.halo(halo_ref, c, x)
+
+    def beyond(x):
+        return x < 0 if far else x >= x_count
 
     along_x, others = {}, {}
-    for x in range(x_count):
-        near = {k: x + k for k in (-2, -1, 1, 2) if not 0 <= x + k < x_count}
+    for x in range(side.inside[0] - 2, side.inside[-1] + 3):
+        if beyond(x):
+            continue
         values = [s_x[i, x] for i in range(3)]
-        rest = [s_o[i, x] for i in range(3)]
-        if near:
+        rest = [s_o[i, x] for i in range(3)] if x in side.inside else None
+        if any(beyond(x + k) for k in steps):
             add = [
-                central(*(u(c, near[k]) if k in near else None for k in (-2, -1, 1, 2)))
+                central(*(u(c, x + k) if beyond(x + k) else None for k in steps))
                 for c in range(comps)
             ]
             lame, shear = metric_ref[3, x], metric_ref[4, x]
@@ -320,17 +355,15 @@
             rest[2] = rest[2] + pressure
         along_x[x], others[x] = values, rest
 
-    outside = (-2, -1, x_count, x_count + 1)
     across = [
-        banded(jnp.concatenate([u(c, x) for x in outside], 0), band) for c in range(2)
+        banded(jnp.concatenate([u(c, x) for x in side.outside], 0), band) for c in range(2)
     ]
-    for place, x in enumerate(outside):
-        source, k = (first_below, place) if x < 0 else (first_above, place - 2)
+    for place, x in enumerate(side.outside):
         slope_x, slope_y, stretch, lame, shear = (
-            source[comps * half + 2 * m + k] for m in range(5)
+            side.metric(first_halo, comps, m, x) for m in range(5)
         )
         dr = [layer_derivative(u(c, x)) for c in range(comps)]
-        dx = [central(*(u(c, x + j) for j in (-2, -1, 1, 2))) for c in range(comps)]
+        dx = [central(*(u(c, x + k) for k in steps)) for c in range(comps)]
         dy = [across[c][place * rows : (place + 1) * rows] for c in range(2)]
         g11 = dx[0] + slope_x * dr[0]
         pressure = lame * (g11 + dy[1] + slope_y * dr[1] + stretch * dr[2])
@@ -345,45 +378,49 @@
 
     beside = []
     for i in range(comps):
-        result = banded(jnp.concatenate([across_of(i, x) for x in range(x_count)], 0), band)
+        result = banded(jnp.concatenate([across_of(i, x) for x in side.inside], 0), band)
         terms = edge_terms(e_s[i], window)
         beside.append(
-            [
-                result[x * rows : (x + 1) * rows] + edge_spread(terms, x, window)
-                for x in range(x_count)
-            ]
+            {
+                x: result[k * rows : (k + 1) * rows] + edge_spread(terms, x, window)
+                for k, x in enumerate(side.inside)
+            }
         )
 
     place = lanes_of((rows, y_count)) // window
     messages = [None] * comps
-    for x in range(x_count):
+    for k, x in enumerate(side.inside):
         slope_x, slope_y, stretch = (metric_ref[m, x] for m in range(3))
         r11, r12, r13 = (layer_derivative(value) for value in along_x[x])
         r22, r23, r33 = (layer_derivative(value) for value in others[x])
         layers = ((r11, r12, r13), (r12, r22, r23), (r13, r23, r33))
         for c in range(comps):
-            force = central(*(along_x[x + k][c] for k in (-2, -1, 1, 2))) + beside[c][x]
+            force = central(*(along_x[x + j][c] for j in steps)) + beside[c][x]
             force = force + slope_x * layers[c][0] + slope_y * layers[c][1]
             force = force + stretch * layers[c][2]
-            following = 2.0 * u(c, x) - past(c, x) + force * push_ref[x]
-            (out_low if x < half else out_high)[c * half + x % half] = following
+            at = c * half + k
+            following = 2.0 * inner(c, x) - before_ref[at] + force * push_ref[x]
+            out_ref[at] = following
             moved = roll(following, window * x + 4)
-            messages[c] = moved if x == 0 else jnp.where(place == x, moved, messages[c])
+            messages[c] = moved if k == 0 else jnp.where(place == x, moved, messages[c])
     for c in range(comps):
         out_edge[c] = messages[c]
 
 
-def fix_kernel(sides, *refs):
+def fix_kernel(far, sides, merge, *refs):
     corner_in = refs[:sides]
-    first_below, first_above, e_s, push_ref, low_ref, high_ref, edge_ref = refs[sides : 7 + sides]
-    out_low, out_high, *out_edge = refs[7 + sides :]
+    first_halo, e_s, push_ref, in_ref, edge_ref = refs[sides : 5 + sides]
+    far_edge = refs[5 + sides] if merge else None
+    out_ref, *out_edge = refs[5 + sides + bool(merge) :]
     x_count, rows, y_count = push_ref.shape
     half, window = x_count // 2, y_count // x_count
     comps = edge_ref.shape[0]
+    side = Side(far, x_count)
     has_left, has_right = neighbours()
     lane = lanes_of((rows, y_count))
     place, w = lane // window, lane % window
     lame, shear = 3, 4
+    steps = (-2, -1, 1, 2)
 
     corners = [
         jnp.where(w < 8, corner_in[-1][c] * has_right, roll(corner_in[0][c], 8) * has_left)
@@ -393,55 +430,60 @@
 
     def edge_change(corner):
         def near(k):
+            if (k < 0) != far:
+                return None
             inside = (place + k < x_count) if k > 0 else (place + k >= 0)
             return jnp.where(inside, 0.0, roll(corner, -window * k))
 
-        return central(*(near(k) for k in (-2, -1, 1, 2)))
+        return central(*(near(k) for k in steps))
 
     beside = [
         edge_terms(e_s[shear] * edge_change(corners[1]), window),
         edge_terms(e_s[lame] * edge_change(corners[0]), window),
     ]
 
-    def stress_change(c, x):
-        source, k = (first_below, x + 2) if x < 0 else (first_above, x - x_count)
-        modulus = source[comps * half + 2 * (lame if c == 0 else shear) + k]
-        return modulus * edge_spread(terms[1 - c], x % x_count, window)
-
     for c in range(comps):
         changes = {}
         if c < 2:
-            changes = {x: stress_change(c, x) for x in (-2, -1, x_count, x_count + 1)}
+            changes = {
+                x: side.metric(first_halo, comps, lame if c == 0 else shear, x)
+                * edge_spread(terms[1 - c], x % x_count, window)
+                for x in side.outside
+            }
         message = edge_ref[c]
-        for x in range(x_count):
-            at = c * half + x % half
-            value = (low_ref if x < half else high_ref)[at]
-            near = [changes.get(x + k) for k in (-2, -1, 1, 2)]
+        for k, x in enumerate(side.inside):
+            value = in_ref[c * half + k]
+            near = [changes.get(x + j) for j in steps]
             if any(item is not None for item in near):
                 change = central(*near) + edge_spread(beside[c], x, window)
                 value = value + change * push_ref[x]
                 message = jnp.where(place == x, roll(value, window * x + 4), message)
-            (out_low if x < half else out_high)[at] = value
+            out_ref[c * half + k] = value
         if out_edge:
+            if merge:
+                message = jnp.where(place < half, far_edge[c], message)
             out_edge[0][c] = message
 
 
 def sketch_kernel(moment, last, shape, *refs):
     comps, half, rows, y_count = shape
-    low_ref, high_ref, before_low, before_high, probe_ref = refs[:5]
+    far_ref, near_ref, before_far, before_near, probe_ref = refs[:5]
     sketch_in = None if moment == 0 else refs[5]
     sketch_ref, spread = refs[-2:]
     x_count = 2 * half
     groups = rows // SUB
     picked = groups // 2
-    now = halves(low_ref, high_ref, half)
-    past = halves(before_low, before_high, half)
+    now = halves(far_ref, near_ref, half)
+    past = halves(before_far, before_near, half)
+    odd = is_odd()
     spread[...] = jnp.zeros_like(spread)
     spread[pl.ds(0, y_count // 2, stride=2), :] = probe_ref[moment]
     rates = []
     for x in range(0, x_count, 2):
         for c in range(comps):
-            rate = (now(c, x) - past(c, x)) * (0.5 / time_step)
+            rate = now(c, x) - past(c, x)
+            other = now(c, x_count - 1 - x) - past(c, x_count - 1 - x)
+            rate = jnp.where(odd, -other if c == 0 else other, rate) * (0.5 / time_step)
             rates += [rate[SUB * v : SUB * (v + 1)] for v in range(0, groups, 2)]
     sketch = jnp.dot(
         jnp.concatenate(rates, 0),
@@ -462,12 +504,13 @@
         sketch_ref[...] = sketch
 
 
-def finish_kernel(half, rows, low_ref, high_ref, out_ref):
+def finish_kernel(half, rows, far_ref, near_ref, out_ref):
     x_count, groups = 2 * half, rows // SUB
-    now = halves(low_ref, high_ref, half)
+    now = halves(far_ref, near_ref, half)
+    odd = is_odd()
     for c in range(out_ref.shape[0]):
-        for x in range(x_count):
-            value = now(c, x)
+        values = mirrored([now(c, x) for x in range(x_count)], odd, c == 0)
+        for x, value in enumerate(values):
             for v in range(groups):
                 out_ref[c, pl.ds(x_count * v + x, SUB, stride=groups * x_count), :] = value[
                     SUB * v : SUB * (v + 1)
@@ -631,9 +674,9 @@
     def flat(array):
         return array.reshape(array.shape[:-3] + (layers * x_count, y_count))
 
-    def along_x(value, step):
-        pairs = [(i, i + step) for i in range(n_x) if 0 <= i + step < n_x]
-        return lax.ppermute(value, "gx", pairs)
+    def exchange(value, far):
+        pairs = [(i, i + 1) for i in range(1 if far else 0, n_x - 1, 2)]
+        return lax.ppermute(value, "gx", pairs + [(k, i) for i, k in pairs])
 
     def along_y(value):
         if sides == 1:
@@ -648,7 +691,7 @@
 
     u_flat = flat(displacement)
     fields = [u_flat, flat(slopes), flat(stretch), flat(moduli)]
-    down, up, edge, metric = call(
+    u_far, u_near, edge, metric = call(
         begin_kernel,
         [slabs(comps * half + 10), slabs(comps * half + 10), slabs(comps + 5), f32(5, x_count, layers, y_count)],
         "begin",
@@ -657,68 +700,81 @@
         scratch=[pltpu.VMEM(field.shape, jnp.float32) for field in fields]
         + [pltpu.SemaphoreType.DMA((4,))],
     )
-    before_low, before_high, push = call(
+    before_far, before_near, push = call(
         rest_kernel,
         [slabs(comps * half), slabs(comps * half), slabs(x_count)],
         "rest",
         [u_flat, flat(velocity), flat(buoyancy)],
     )
 
-    low, high = down, up
     sketch_rows = half * comps * (layers // 2)
     sketch = []
+
+    def half_step(far, moment, halo, first_halo, before, tokens, far_edge):
+        name = f"{'far' if far else 'near'}_{moment}"
+        last = moment == STEPS - 1
+        (corner,) = call(
+            partial(corner_kernel, far, half),
+            [slabs(2)],
+            f"corner_{name}",
+            [halo, *tokens],
+            specs=[VMEM] + [ANY] * len(tokens),
+        )
+        corner_in = along_y(corner)
+        value, own_edge = call(
+            partial(wide_kernel, far),
+            [slabs(comps * half), slabs(comps)],
+            f"wide_{name}",
+            [u_far, u_near, halo, before, metric, push, first_halo, s_x, s_o, e_s],
+            flops=10_000_000,
+        )
+        merge = [] if far_edge is None else [far_edge]
+        value, *own_edge = call(
+            partial(fix_kernel, far, sides, len(merge)),
+            [slabs(comps * half)] + ([] if last else [slabs(comps)]),
+            f"fix_{name}",
+            [*corner_in, first_halo, e_s, push, value, own_edge, *merge],
+        )
+        return value, (own_edge[0] if own_edge else None)
+
     for moment in range(STEPS):
         last = moment == STEPS - 1
+        if moment == 0:
+            far_halo = exchange(u_far, True)
+            near_halo = exchange(u_near, False)
         edge_in = along_y(edge)
-        above = along_x(low, -1)
-        below = along_x(high, 1)
         if moment == 0:
-            first_edge, first_edge_in, first_below, first_above = edge, edge_in, below, above
+            first_edge, first_edge_in, first_far, first_near = edge, edge_in, far_halo, near_halo
         s_x, s_o, e_s = call(
             partial(tile_kernel, sides, comps),
             [f32(comps, x_count, layers, y_count), f32(3, x_count, layers, y_count), slabs(5)],
             f"tile_{moment}",
-            [low, high, edge, *edge_in, metric, first_edge, *first_edge_in],
+            [u_far, u_near, edge, *edge_in, metric, first_edge, *first_edge_in],
             flops=20_000_000,
         )
-        (corner,) = call(
-            partial(corner_kernel, half),
-            [slabs(2)],
-            f"corner_{moment}",
-            [below, above, e_s, *(sketch or [push])],
-            specs=[VMEM, VMEM, ANY, ANY],
-        )
-        corner_in = along_y(corner)
-        next_low, next_high, edge = call(
-            wide_kernel,
-            [slabs(comps * half), slabs(comps * half), slabs(comps)],
-            f"wide_{moment}",
-            [
-                low, high, below, above, before_low, before_high, metric, push, first_below,
-                first_above, s_x, s_o, e_s,
-            ],
-            flops=20_000_000,
-        )
-        next_low, next_high, *edge = call(
-            partial(fix_kernel, sides),
-            [slabs(comps * half), slabs(comps * half)] + ([] if last else [slabs(comps)]),
-            f"fix_{moment}",
-            [*corner_in, first_below, first_above, e_s, push, next_low, next_high, edge],
-        )
+        next_far, far_edge = half_step(
+            True, moment, far_halo, first_far, before_far, [e_s, *(sketch or [push])], None
+        )
+        if not last:
+            far_halo = exchange(next_far, True)
+        next_near, edge = half_step(
+            False, moment, near_halo, first_near, before_near, [next_far], far_edge
+        )
+        if not last:
+            near_halo = exchange(next_near, False)
         sketch = call(
             partial(sketch_kernel, moment, last, (comps, half, layers, y_count)),
             [f32(sketch_rows, width)],
             f"sketch_{moment}",
-            [next_low, next_high, before_low, before_high, probes, *sketch],
+            [next_far, next_near, before_far, before_near, probes, *sketch],
             scratch=[pltpu.VMEM((y_count, width), jnp.float32)],
         )
-        before_low, before_high, low, high = low, high, next_low, next_high
-        edge = None if last else edge[0]
+        before_far, before_near, u_far, u_near = u_far, u_near, next_far, next_near
     (final,) = call(
         partial(finish_kernel, half, layers),
         [f32(comps, layers * x_count, y_count)],
         "finish",
-        [low, high],
+        [u_far, u_near],
     )
     final = final.reshape(displacement.shape)
 

time: 101 us -> 87.8 us (0.87)
  waiting for transfers between devices: 47.7 us -> 40.1 us
  starting transfers between devices: 31.6 us -> 24.3 us
  Pallas kernels: 16.2 us -> 18.3 us
    ppermute x8, waiting for transfers between devices: 33.9 us -> 20.7 us  [exchange(): return lax.ppermute(value, 'gx', pairs + [(k, i) for i, k in pairs])]
    ppermute x8, starting transfers between devices: 21.4 us -> 16.1 us  [exchange(): return lax.ppermute(value, 'gx', pairs + [(k, i) for i, k in pairs])]
    ppermute x8 -> x12, waiting for transfers between devices: 5.39 us -> 9.01 us  [along_y(): return [lax.ppermute(value, 'gy', [(0, 1), (1, 0)])]]
    ppermute x5, starting transfers between devices: 9.66 us -> 7.2 us  [butterfly(): other = lax.ppermute(value, axis, [(i, i ^ bit) for i in range(count)])]
    pallas_call x25 -> x37, Pallas kernels: 16.2 us -> 18.3 us  [call(): pl.pallas_call(kernel, out_shape=outs, in_specs=specs or [VMEM] * len(ins...]
    ppermute x5, waiting for transfers between devices: 8.42 us -> 10.4 us  [butterfly(): other = lax.ppermute(value, axis, [(i, i ^ bit) for i in range(count)])]
  transfers between devices with their start and end apart: 21 -> 25, of which waited for: 21 -> 21; matrix products, arithmetic and copies ran while one was open for 0% -> 0% of each run, Pallas kernels for 7% -> 13%
where the time goes in v4:
time: 87.8 us; the launch traced here: 87.5 us
  waiting for transfers between devices  40.1 us (46%)
  starting transfers between devices  24.3 us (28%)
  Pallas kernels  18.3 us (21%)
  local copies, waits for them, and re-layouts  3.8 us (4%)
  between operations  0.94 us (1%)
    ppermute x8, waiting for transfers between devices, exchange(): return lax.ppermute(value, 'gx', pairs + [(k, i) for i, k in pairs])  20.7 us
    pallas_call x37, Pallas kernels, call(): pl.pallas_call(kernel, out_shape=outs, in_specs=specs or [VMEM] * len(ins...  18.3 us
    ppermute x8, starting transfers between devices, exchange(): return lax.ppermute(value, 'gx', pairs + [(k, i) for i, k in pairs])  16.1 us
    ppermute x5, waiting for transfers between devices, butterfly(): other = lax.ppermute(value, axis, [(i, i ^ bit) for i in range(count)])  10.4 us
    ppermute x12, waiting for transfers between devices, along_y(): return [lax.ppermute(value, 'gy', [(0, 1), (1, 0)])]  9.01 us
    ppermute x5, starting transfers between devices, butterfly(): other = lax.ppermute(value, axis, [(i, i ^ bit) for i in range(count)])  7.2 us
    unnamed x14, local copies, waits for them, and re-layouts  3.8 us
  transfers between devices with their start and end apart: 25, of which 21 were waited for; matrix products, arithmetic and copies ran while one was open for 0% of the time, Pallas kernels for 13%

profile of v4, /device:TPU:0, one launch (start us, length us, event | category | flops | bytes accessed | tf_op | source)
XLA Modules:
  0.0 87.5 jit_solution(6424162184038444013)
XLA Ops:
  0.6 1.0 %copy-done.1 = f32[3,32,8,128]{3,2,1,0:T(8,128)S(1)} copy-done((f32[3,32,8,128]{3,2,1,0:T(8,128)S(1)}, f32[3,32,8,128]{3,2,1,0:T(8,128)}, u32[]{:S(2)}) %copy-start.1) | copy-done | bytes 393240
  1.6 0.9 %copy-done.3 = f32[2,32,8,128]{3,2,1,0:T(8,128)S(1)} copy-done((f32[2,32,8,128]{3,2,1,0:T(8,128)S(1)}, f32[2,32,8,128]{3,2,1,0:T(8,128)}, u32[]{:S(2)}) %copy-start.3) | copy-done | bytes 262168
  4.4 1.2 %begin.1 = (f32[22,32,128]{2,1,0:T(8,128)S(1)}, f32[22,32,128]{2,1,0:T(8,128)S(1)}, f32[8,32,128]{2,1,0:T(8,128)S(1)}, f32[5,8,32,128]{3,2,1,0:T(8,128)S(1)}) custom-call(f32[3,256,128]{2,1,0:T(8,128)S(1)} %bitcast.8, f32[2,256,128]{2,1,0:T(8,128)S(1)} %bitcast.11, f32[256,128]{1,0:T(8,128)S(1)} %bitcast.14, f32[2,256,128]{2,1,0:T(8,128)S(1)} %bitcast.12), custom_call_target="tpu_custom_call" | custom-call | bytes 2555904 | tf_op jit(solution)/shard_map/begin/pallas_call | solution.py:640
  6.4 5.7 %collective-permute-start.4 = (f32[22,32,128]{2,1,0:T(8,128)S(1)}, f32[22,32,128]{2,1,0:T(8,128)S(1)}, u32[]{:S(2)}, u32[]{:S(2)}) collective-permute-start(f32[22,32,128]{2,1,0:T(8,128)S(1)} %get-tuple-element.55.refs_1_.near_ref.before_ref.refs_3_), channel_id=1, source_target_pairs={{0,2},{4,6},{8,10},{12,14},{16,18},{20,22},{24,26},{28,30},{2,0},{... | collective-permute-start | bytes 1081352 | tf_op jit(solution)/shard_map/ppermute | solution.py:679
  16.4 11.5 %collective-permute-done.4.halo_ref.first_halo.refs_1_ = f32[22,32,128]{2,1,0:T(8,128)S(1)} collective-permute-done((f32[22,32,128]{2,1,0:T(8,128)S(1)}, f32[22,32,128]{2,1,0:T(8,128)S(1)}, u32[]{:S(2)}, u32[]{:S(2)}) %collective-permute-start.4) | collective-permute-done | bytes 360480 | tf_op jit(solution)/shard_map/ppermute | solution.py:679
  29.6 1.9 %collective-permute-start.9 = (f32[12,32,128]{2,1,0:T(8,128)S(1)}, f32[12,32,128]{2,1,0:T(8,128)S(1)}, u32[]{:S(2)}, u32[]{:S(2)}) collective-permute-start(f32[12,32,128]{2,1,0:T(8,128)S(1)} %get-tuple-element.70.refs_1_.near_ref.before_ref.refs_3_), channel_id=1, source_target_pairs={{0,2},{4,6},{8,10},{12,14},{16,18},{20,22},{24,26},{28,30},{2,0},{... | collective-permute-start | bytes 589832 | tf_op jit(solution)/shard_map/ppermute | solution.py:679
  31.8 1.0 %collective-permute-done.6.refs_3_ = f32[3,32,128]{2,1,0:T(8,128)S(1)} collective-permute-done((f32[3,32,128]{2,1,0:T(8,128)S(1)}, f32[3,32,128]{2,1,0:T(8,128)S(1)}, u32[]{:S(2)}, u32[]{:S(2)}) %collective-permute-start.6) | collective-permute-done | bytes 49184 | tf_op jit(solution)/shard_map/ppermute | solution.py:683
  35.7 1.3 %collective-permute-done.9.halo_ref = f32[12,32,128]{2,1,0:T(8,128)S(1)} collective-permute-done((f32[12,32,128]{2,1,0:T(8,128)S(1)}, f32[12,32,128]{2,1,0:T(8,128)S(1)}, u32[]{:S(2)}, u32[]{:S(2)}) %collective-permute-start.9) | collective-permute-done | bytes 196640 | tf_op jit(solution)/shard_map/ppermute | solution.py:679
  38.7 2.7 %collective-permute-start.14 = (f32[12,32,128]{2,1,0:T(8,128)S(1)}, f32[12,32,128]{2,1,0:T(8,128)S(1)}, u32[]{:S(2)}, u32[]{:S(2)}) collective-permute-start(f32[12,32,128]{2,1,0:T(8,128)S(1)} %get-tuple-element.81.refs_1_.near_ref.before_ref.refs_3_), channel_id=1, source_target_pairs={{0,2},{4,6},{8,10},{12,14},{16,18},{20,22},{24,26},{28,30},{2,0},{... | collective-permute-start | bytes 589832 | tf_op jit(solution)/shard_map/ppermute | solution.py:679
  41.6 1.0 %collective-permute-done.11.refs_3_ = f32[3,32,128]{2,1,0:T(8,128)S(1)} collective-permute-done((f32[3,32,128]{2,1,0:T(8,128)S(1)}, f32[3,32,128]{2,1,0:T(8,128)S(1)}, u32[]{:S(2)}, u32[]{:S(2)}) %collective-permute-start.11) | collective-permute-done | bytes 49184 | tf_op jit(solution)/shard_map/ppermute | solution.py:683
  45.7 3.5 %collective-permute-done.14.halo_ref = f32[12,32,128]{2,1,0:T(8,128)S(1)} collective-permute-done((f32[12,32,128]{2,1,0:T(8,128)S(1)}, f32[12,32,128]{2,1,0:T(8,128)S(1)}, u32[]{:S(2)}, u32[]{:S(2)}) %collective-permute-start.14) | collective-permute-done | bytes 196640 | tf_op jit(solution)/shard_map/ppermute | solution.py:679
  51.0 2.9 %collective-permute-start.18 = (f32[12,32,128]{2,1,0:T(8,128)S(1)}, f32[12,32,128]{2,1,0:T(8,128)S(1)}, u32[]{:S(2)}, u32[]{:S(2)}) collective-permute-start(f32[12,32,128]{2,1,0:T(8,128)S(1)} %get-tuple-element.92.refs_1_.near_ref), channel_id=1, source_target_pairs={{0,2},{4,6},{8,10},{12,14},{16,18},{20,22},{24,26},{28,30},{2,0},{... | collective-permute-start | bytes 589832 | tf_op jit(solution)/shard_map/ppermute | solution.py:679
  54.1 1.0 %collective-permute-done.16.refs_3_ = f32[3,32,128]{2,1,0:T(8,128)S(1)} collective-permute-done((f32[3,32,128]{2,1,0:T(8,128)S(1)}, f32[3,32,128]{2,1,0:T(8,128)S(1)}, u32[]{:S(2)}, u32[]{:S(2)}) %collective-permute-start.16) | collective-permute-done | bytes 49184 | tf_op jit(solution)/shard_map/ppermute | solution.py:683
  57.3 4.4 %collective-permute-done.18.halo_ref = f32[12,32,128]{2,1,0:T(8,128)S(1)} collective-permute-done((f32[12,32,128]{2,1,0:T(8,128)S(1)}, f32[12,32,128]{2,1,0:T(8,128)S(1)}, u32[]{:S(2)}, u32[]{:S(2)}) %collective-permute-start.18) | collective-permute-done | bytes 196640 | tf_op jit(solution)/shard_map/ppermute | solution.py:679
  63.9 1.1 %collective-permute-done.20.second_ref = f32[192,128]{1,0:T(8,128)S(1)} collective-permute-done((f32[192,128]{1,0:T(8,128)S(1)}, f32[192,128]{1,0:T(8,128)S(1)}, u32[]{:S(2)}, u32[]{:S(2)}) %collective-permute-start.20) | collective-permute-done | bytes 98336 | tf_op jit(solution)/shard_map/ppermute | solution.py:659
  65.4 2.5 %collective-permute-start.21 = (f32[72,128]{1,0:T(8,128)S(1)}, f32[72,128]{1,0:T(8,128)S(1)}, u32[]{:S(2)}, u32[]{:S(2)}) collective-permute-start(f32[72,128]{1,0:T(8,128)S(1)} %get-tuple-element.101), channel_id=1, source_target_pairs={{0,2},{2,0},{4,6},{6,4},{8,10},{10,8},{12,14},{14,12},{16,18},{18,... | collective-permute-start | bytes 110600 | tf_op jit(solution)/shard_map/ppermute | solution.py:659
  67.9 1.9 %collective-permute-done.21 = f32[72,128]{1,0:T(8,128)S(1)} collective-permute-done((f32[72,128]{1,0:T(8,128)S(1)}, f32[72,128]{1,0:T(8,128)S(1)}, u32[]{:S(2)}, u32[]{:S(2)}) %collective-permute-start.21) | collective-permute-done | bytes 36896 | tf_op jit(solution)/shard_map/ppermute | solution.py:659
  69.8 3.9 %collective-permute-done.22 = f32[72,128]{1,0:T(8,128)S(1)} collective-permute-done((f32[72,128]{1,0:T(8,128)S(1)}, f32[72,128]{1,0:T(8,128)S(1)}, u32[]{:S(2)}, u32[]{:S(2)}) %collective-permute-start.22) | collective-permute-done | bytes 36896 | tf_op jit(solution)/shard_map/ppermute | solution.py:659
  73.8 1.6 %collective-permute-start.23 = (f32[72,128]{1,0:T(8,128)S(1)}, f32[72,128]{1,0:T(8,128)S(1)}, u32[]{:S(2)}, u32[]{:S(2)}) collective-permute-start(f32[72,128]{1,0:T(8,128)S(1)} %add.10), channel_id=1, source_target_pairs={{0,8},{2,10},{4,12},{6,14},{8,0},{10,2},{12,4},{14,6},{16,24},{18,... | collective-permute-start | bytes 110600 | tf_op jit(solution)/shard_map/ppermute | solution.py:659
  75.4 2.4 %collective-permute-done.23 = f32[72,128]{1,0:T(8,128)S(1)} collective-permute-done((f32[72,128]{1,0:T(8,128)S(1)}, f32[72,128]{1,0:T(8,128)S(1)}, u32[]{:S(2)}, u32[]{:S(2)}) %collective-permute-start.23) | collective-permute-done | bytes 36896 | tf_op jit(solution)/shard_map/ppermute | solution.py:659
  77.8 2.9 %collective-permute-start.24 = (f32[72,128]{1,0:T(8,128)S(1)}, f32[72,128]{1,0:T(8,128)S(1)}, u32[]{:S(2)}, u32[]{:S(2)}) collective-permute-start(f32[72,128]{1,0:T(8,128)S(1)} %add.11.first_ref), channel_id=1, source_target_pairs={{0,16},{2,18},{4,20},{6,22},{8,24},{10,26},{12,28},{14,30},{16,0},... | collective-permute-start | bytes 110600 | tf_op jit(solution)/shard_map/ppermute | solution.py:659
  80.6 1.0 %finish.1 = f32[3,256,128]{2,1,0:T(8,128)} custom-call(f32[12,32,128]{2,1,0:T(8,128)S(1)} %fix_far_3.1.refs_0_.far_ref, f32[12,32,128]{2,1,0:T(8,128)S(1)} %fix_near_3.1.near_ref.refs_1_), custom_call_target="tpu_custom_call" | custom-call | bytes 786432 | tf_op jit(solution)/shard_map/finish/pallas_call | solution.py:640
  81.6 1.0 %collective-permute-done.24.second_ref = f32[72,128]{1,0:T(8,128)S(1)} collective-permute-done((f32[72,128]{1,0:T(8,128)S(1)}, f32[72,128]{1,0:T(8,128)S(1)}, u32[]{:S(2)}, u32[]{:S(2)}) %collective-permute-start.24) | collective-permute-done | bytes 36896 | tf_op jit(solution)/shard_map/ppermute | solution.py:659
  82.6 4.8 %factor.1 = (f32[4,24,128]{2,1,0:T(8,128)}, f32[128,128]{1,0:T(8,128)}) custom-call(f32[72,128]{1,0:T(8,128)S(1)} %add.11.first_ref, f32[72,128]{1,0:T(8,128)S(1)} %collective-permute-done.24.second_ref, f32[4,48,128]{2,1,0:T(8,128)S(1)} %bitcast.15), custom_call_target="tpu_custom_call" | custom-call | bytes 286720 | tf_op jit(solution)/shard_map/factor/pallas_call | solution.py:640
  (80 shorter events, 23.4 us)
Async XLA Ops:
  5.7 8.3 %collective-permute-start = (f32[22,32,128]{2,1,0:T(8,128)S(1)}, f32[22,32,128]{2,1,0:T(8,128)S(1)}, u32[]{:S(2)}, u32[]{:S(2)}) collective-permute-start(f32[22,32,128]{2,1,0:T(8,128)S(1)} %get-tuple-element.54.refs_0_.far_ref.before_ref.refs_2_), channel_id=1, source_target_pairs={{2,4},{6,8},{10,12},{14,16},{18,20},{22,24},{26,28},{4,2},{8,6},{1... | collective-permute-start | bytes 1081352 | tf_op jit(solution)/shard_map/ppermute | solution.py:679
  6.4 21.5 %collective-permute-start.4 = (f32[22,32,128]{2,1,0:T(8,128)S(1)}, f32[22,32,128]{2,1,0:T(8,128)S(1)}, u32[]{:S(2)}, u32[]{:S(2)}) collective-permute-start(f32[22,32,128]{2,1,0:T(8,128)S(1)} %get-tuple-element.55.refs_1_.near_ref.before_ref.refs_3_), channel_id=1, source_target_pairs={{0,2},{4,6},{8,10},{12,14},{16,18},{20,22},{24,26},{28,30},{2,0},{... | collective-permute-start | bytes 1081352 | tf_op jit(solution)/shard_map/ppermute | solution.py:679
  12.1 1.3 %collective-permute-start.1 = (f32[8,32,128]{2,1,0:T(8,128)S(1)}, f32[8,32,128]{2,1,0:T(8,128)S(1)}, u32[]{:S(2)}, u32[]{:S(2)}) collective-permute-start(f32[8,32,128]{2,1,0:T(8,128)S(1)} %get-tuple-element.56.refs_2_.refs_5_), channel_id=1, source_target_pairs={{0,1},{1,0},{2,3},{3,2},{4,5},{5,4},{6,7},{7,6},{8,9},{9,8},{10,11... | collective-permute-start | bytes 393224 | tf_op jit(solution)/shard_map/ppermute | solution.py:683
  14.1 1.3 %collective-permute-start.2 = (f32[2,32,128]{2,1,0:T(8,128)S(1)}, f32[2,32,128]{2,1,0:T(8,128)S(1)}, u32[]{:S(2)}, u32[]{:S(2)}) collective-permute-start(f32[2,32,128]{2,1,0:T(8,128)S(1)} %corner_far_0.1), channel_id=1, source_target_pairs={{0,1},{1,0},{2,3},{3,2},{4,5},{5,4},{6,7},{7,6},{8,9},{9,8},{10,11... | collective-permute-start | bytes 98312 | tf_op jit(solution)/shard_map/ppermute | solution.py:683
  15.7 17.5 %collective-permute-start.3 = (f32[12,32,128]{2,1,0:T(8,128)S(1)}, f32[12,32,128]{2,1,0:T(8,128)S(1)}, u32[]{:S(2)}, u32[]{:S(2)}) collective-permute-start(f32[12,32,128]{2,1,0:T(8,128)S(1)} %get-tuple-element.65.refs_0_.far_ref.before_ref.refs_2_), channel_id=1, source_target_pairs={{2,4},{6,8},{10,12},{14,16},{18,20},{22,24},{26,28},{4,2},{8,6},{1... | collective-permute-start | bytes 589832 | tf_op jit(solution)/shard_map/ppermute | solution.py:679
  28.0 1.3 %collective-permute-start.5 = (f32[2,32,128]{2,1,0:T(8,128)S(1)}, f32[2,32,128]{2,1,0:T(8,128)S(1)}, u32[]{:S(2)}, u32[]{:S(2)}) collective-permute-start(f32[2,32,128]{2,1,0:T(8,128)S(1)} %corner_near_0.1), channel_id=1, source_target_pairs={{0,1},{1,0},{2,3},{3,2},{4,5},{5,4},{6,7},{7,6},{8,9},{9,8},{10,11... | collective-permute-start | bytes 98312 | tf_op jit(solution)/shard_map/ppermute | solution.py:683
  29.6 7.4 %collective-permute-start.9 = (f32[12,32,128]{2,1,0:T(8,128)S(1)}, f32[12,32,128]{2,1,0:T(8,128)S(1)}, u32[]{:S(2)}, u32[]{:S(2)}) collective-permute-start(f32[12,32,128]{2,1,0:T(8,128)S(1)} %get-tuple-element.70.refs_1_.near_ref.before_ref.refs_3_), channel_id=1, source_target_pairs={{0,2},{4,6},{8,10},{12,14},{16,18},{20,22},{24,26},{28,30},{2,0},{... | collective-permute-start | bytes 589832 | tf_op jit(solution)/shard_map/ppermute | solution.py:679
  31.5 1.2 %collective-permute-start.6 = (f32[3,32,128]{2,1,0:T(8,128)S(1)}, f32[3,32,128]{2,1,0:T(8,128)S(1)}, u32[]{:S(2)}, u32[]{:S(2)}) collective-permute-start(f32[3,32,128]{2,1,0:T(8,128)S(1)} %get-tuple-element.71.refs_2_), channel_id=1, source_target_pairs={{0,1},{1,0},{2,3},{3,2},{4,5},{5,4},{6,7},{7,6},{8,9},{9,8},{10,11... | collective-permute-start | bytes 147464 | tf_op jit(solution)/shard_map/ppermute | solution.py:683
  33.4 1.3 %collective-permute-start.7 = (f32[2,32,128]{2,1,0:T(8,128)S(1)}, f32[2,32,128]{2,1,0:T(8,128)S(1)}, u32[]{:S(2)}, u32[]{:S(2)}) collective-permute-start(f32[2,32,128]{2,1,0:T(8,128)S(1)} %corner_far_1.1), channel_id=1, source_target_pairs={{0,1},{1,0},{2,3},{3,2},{4,5},{5,4},{6,7},{7,6},{8,9},{9,8},{10,11... | collective-permute-start | bytes 98312 | tf_op jit(solution)/shard_map/ppermute | solution.py:683
  35.0 8.1 %collective-permute-start.8 = (f32[12,32,128]{2,1,0:T(8,128)S(1)}, f32[12,32,128]{2,1,0:T(8,128)S(1)}, u32[]{:S(2)}, u32[]{:S(2)}) collective-permute-start(f32[12,32,128]{2,1,0:T(8,128)S(1)} %get-tuple-element.77.refs_0_.far_ref.before_ref.refs_2_), channel_id=1, source_target_pairs={{2,4},{6,8},{10,12},{14,16},{18,20},{22,24},{26,28},{4,2},{8,6},{1... | collective-permute-start | bytes 589832 | tf_op jit(solution)/shard_map/ppermute | solution.py:679
  37.1 1.3 %collective-permute-start.10 = (f32[2,32,128]{2,1,0:T(8,128)S(1)}, f32[2,32,128]{2,1,0:T(8,128)S(1)}, u32[]{:S(2)}, u32[]{:S(2)}) collective-permute-start(f32[2,32,128]{2,1,0:T(8,128)S(1)} %corner_near_1.1), channel_id=1, source_target_pairs={{0,1},{1,0},{2,3},{3,2},{4,5},{5,4},{6,7},{7,6},{8,9},{9,8},{10,11... | collective-permute-start | bytes 98312 | tf_op jit(solution)/shard_map/ppermute | solution.py:683
  38.7 10.5 %collective-permute-start.14 = (f32[12,32,128]{2,1,0:T(8,128)S(1)}, f32[12,32,128]{2,1,0:T(8,128)S(1)}, u32[]{:S(2)}, u32[]{:S(2)}) collective-permute-start(f32[12,32,128]{2,1,0:T(8,128)S(1)} %get-tuple-element.81.refs_1_.near_ref.before_ref.refs_3_), channel_id=1, source_target_pairs={{0,2},{4,6},{8,10},{12,14},{16,18},{20,22},{24,26},{28,30},{2,0},{... | collective-permute-start | bytes 589832 | tf_op jit(solution)/shard_map/ppermute | solution.py:679
  41.4 1.2 %collective-permute-start.11 = (f32[3,32,128]{2,1,0:T(8,128)S(1)}, f32[3,32,128]{2,1,0:T(8,128)S(1)}, u32[]{:S(2)}, u32[]{:S(2)}) collective-permute-start(f32[3,32,128]{2,1,0:T(8,128)S(1)} %get-tuple-element.82.refs_2_), channel_id=1, source_target_pairs={{0,1},{1,0},{2,3},{3,2},{4,5},{5,4},{6,7},{7,6},{8,9},{9,8},{10,11... | collective-permute-start | bytes 147464 | tf_op jit(solution)/shard_map/ppermute | solution.py:683
  43.2 1.3 %collective-permute-start.12 = (f32[2,32,128]{2,1,0:T(8,128)S(1)}, f32[2,32,128]{2,1,0:T(8,128)S(1)}, u32[]{:S(2)}, u32[]{:S(2)}) collective-permute-start(f32[2,32,128]{2,1,0:T(8,128)S(1)} %corner_far_2.1), channel_id=1, source_target_pairs={{0,1},{1,0},{2,3},{3,2},{4,5},{5,4},{6,7},{7,6},{8,9},{9,8},{10,11... | collective-permute-start | bytes 98312 | tf_op jit(solution)/shard_map/ppermute | solution.py:683
  44.9 10.7 %collective-permute-start.13 = (f32[12,32,128]{2,1,0:T(8,128)S(1)}, f32[12,32,128]{2,1,0:T(8,128)S(1)}, u32[]{:S(2)}, u32[]{:S(2)}) collective-permute-start(f32[12,32,128]{2,1,0:T(8,128)S(1)} %get-tuple-element.88.refs_0_.far_ref), channel_id=1, source_target_pairs={{2,4},{6,8},{10,12},{14,16},{18,20},{22,24},{26,28},{4,2},{8,6},{1... | collective-permute-start | bytes 589832 | tf_op jit(solution)/shard_map/ppermute | solution.py:679
  49.3 1.3 %collective-permute-start.15 = (f32[2,32,128]{2,1,0:T(8,128)S(1)}, f32[2,32,128]{2,1,0:T(8,128)S(1)}, u32[]{:S(2)}, u32[]{:S(2)}) collective-permute-start(f32[2,32,128]{2,1,0:T(8,128)S(1)} %corner_near_2.1), channel_id=1, source_target_pairs={{0,1},{1,0},{2,3},{3,2},{4,5},{5,4},{6,7},{7,6},{8,9},{9,8},{10,11... | collective-permute-start | bytes 98312 | tf_op jit(solution)/shard_map/ppermute | solution.py:683
  51.0 10.8 %collective-permute-start.18 = (f32[12,32,128]{2,1,0:T(8,128)S(1)}, f32[12,32,128]{2,1,0:T(8,128)S(1)}, u32[]{:S(2)}, u32[]{:S(2)}) collective-permute-start(f32[12,32,128]{2,1,0:T(8,128)S(1)} %get-tuple-element.92.refs_1_.near_ref), channel_id=1, source_target_pairs={{0,2},{4,6},{8,10},{12,14},{16,18},{20,22},{24,26},{28,30},{2,0},{... | collective-permute-start | bytes 589832 | tf_op jit(solution)/shard_map/ppermute | solution.py:679
  55.7 1.3 %collective-permute-start.17 = (f32[2,32,128]{2,1,0:T(8,128)S(1)}, f32[2,32,128]{2,1,0:T(8,128)S(1)}, u32[]{:S(2)}, u32[]{:S(2)}) collective-permute-start(f32[2,32,128]{2,1,0:T(8,128)S(1)} %corner_far_3.1), channel_id=1, source_target_pairs={{0,1},{1,0},{2,3},{3,2},{4,5},{5,4},{6,7},{7,6},{8,9},{9,8},{10,11... | collective-permute-start | bytes 98312 | tf_op jit(solution)/shard_map/ppermute | solution.py:683
  61.8 1.3 %collective-permute-start.19 = (f32[2,32,128]{2,1,0:T(8,128)S(1)}, f32[2,32,128]{2,1,0:T(8,128)S(1)}, u32[]{:S(2)}, u32[]{:S(2)}) collective-permute-start(f32[2,32,128]{2,1,0:T(8,128)S(1)} %corner_near_3.1), channel_id=1, source_target_pairs={{0,1},{1,0},{2,3},{3,2},{4,5},{5,4},{6,7},{7,6},{8,9},{9,8},{10,11... | collective-permute-start | bytes 98312 | tf_op jit(solution)/shard_map/ppermute | solution.py:683
  63.6 1.4 %collective-permute-start.20 = (f32[192,128]{1,0:T(8,128)S(1)}, f32[192,128]{1,0:T(8,128)S(1)}, u32[]{:S(2)}, u32[]{:S(2)}) collective-permute-start(f32[192,128]{1,0:T(8,128)S(1)} %sketch_3.1.first_ref), channel_id=1, source_target_pairs={{0,1},{1,0},{2,3},{3,2},{4,5},{5,4},{6,7},{7,6},{8,9},{9,8},{10,11... | collective-permute-start | bytes 294920 | tf_op jit(solution)/shard_map/ppermute | solution.py:659
  65.4 4.5 %collective-permute-start.21 = (f32[72,128]{1,0:T(8,128)S(1)}, f32[72,128]{1,0:T(8,128)S(1)}, u32[]{:S(2)}, u32[]{:S(2)}) collective-permute-start(f32[72,128]{1,0:T(8,128)S(1)} %get-tuple-element.101), channel_id=1, source_target_pairs={{0,2},{2,0},{4,6},{6,4},{8,10},{10,8},{12,14},{14,12},{16,18},{18,... | collective-permute-start | bytes 110600 | tf_op jit(solution)/shard_map/ppermute | solution.py:659
  69.8 4.0 %collective-permute-start.22 = (f32[72,128]{1,0:T(8,128)S(1)}, f32[72,128]{1,0:T(8,128)S(1)}, u32[]{:S(2)}, u32[]{:S(2)}) collective-permute-start(f32[72,128]{1,0:T(8,128)S(1)} %add.9), channel_id=1, source_target_pairs={{0,4},{2,6},{4,0},{6,2},{8,12},{10,14},{12,8},{14,10},{16,20},{18,... | collective-permute-start | bytes 110600 | tf_op jit(solution)/shard_map/ppermute | solution.py:659
  73.8 4.0 %collective-permute-start.23 = (f32[72,128]{1,0:T(8,128)S(1)}, f32[72,128]{1,0:T(8,128)S(1)}, u32[]{:S(2)}, u32[]{:S(2)}) collective-permute-start(f32[72,128]{1,0:T(8,128)S(1)} %add.10), channel_id=1, source_target_pairs={{0,8},{2,10},{4,12},{6,14},{8,0},{10,2},{12,4},{14,6},{16,24},{18,... | collective-permute-start | bytes 110600 | tf_op jit(solution)/shard_map/ppermute | solution.py:659
  77.8 4.9 %collective-permute-start.24 = (f32[72,128]{1,0:T(8,128)S(1)}, f32[72,128]{1,0:T(8,128)S(1)}, u32[]{:S(2)}, u32[]{:S(2)}) collective-permute-start(f32[72,128]{1,0:T(8,128)S(1)} %add.11.first_ref), channel_id=1, source_target_pairs={{0,16},{2,18},{4,20},{6,22},{8,24},{10,26},{12,28},{14,30},{16,0},... | collective-permute-start | bytes 110600 | tf_op jit(solution)/shard_map/ppermute | solution.py:659
  (8 other events, 22.7 us)

commit v5 on v4

--- a/solution.py
+++ b/solution.py
@@ -7,6 +7,7 @@
 from jax.experimental import pallas as pl
 from jax.experimental.pallas import tpu as pltpu
 from jax.sharding import PartitionSpec as P
+
 
 STEPS = 4
 SUB = 8
@@ -154,24 +155,62 @@
     def depth(self, x):
         return -1 - x if self.far else x - self.x_count
 
-    def halo(self, ref, c, x):
-        place = self.depth(x) if self.far else self.half - 1 - self.depth(x)
-        value = ref[c * self.half + place]
-        return -value if c == 0 else value
-
-    def metric(self, ref, comps, m, x):
+    def at(self, ref, first, index, x, negate, terms=None):
         place = self.depth(x) if self.far else 1 - self.depth(x)
-        value = ref[comps * self.half + 2 * m + place]
-        return -value if m == 0 else value
+        value = ref[first + 2 * index + place]
+        value = -value if negate else value
+        return value if terms is None else value + terms
+
+    def halo(self, ref, c, x, terms=None):
+        terms = None if terms is None or c > 1 else terms[self.slot(c, x)]
+        return self.at(ref, 0, c, x, c == 0, terms)
+
+    def own_part(self, ref, i, x, terms=None):
+        return self.at(ref, 6, i, x, i > 0, None if terms is None else terms[self.slot(2 + i, x)])
+
+    def modulus(self, ref, m, x):
+        return self.at(ref, 12, m, x, False)
+
+    def slot(self, index, x):
+        return 10 * (not self.far) + 2 * index + self.depth(x)
+
+    def packed(self, ref, f, x, window):
+        place = 2 * f + (self.depth(x) if self.far else 1 - self.depth(x))
+        value = roll(ref[16], ref.shape[2] - 4 - window * place)
+        return -value if f == 1 else value
+
+    def pack(self, messages, window):
+        place = lanes_of(messages[0].shape) // (2 * window)
+        packed = None
+        for f, message in enumerate(messages):
+            moved = roll(message, window * (2 * f - (0 if self.far else self.x_count - 2)))
+            packed = moved if packed is None else jnp.where(place == f, moved, packed)
+        return packed
+
+    def send(self, ref, u, metric):
+        for k, x in enumerate(self.inside[:2] if self.far else self.inside[-2:]):
+            slope_x, slope_y, stretch, lame, shear = (metric(m, x) for m in range(5))
+            dr = [layer_derivative(u(c, x)) for c in range(3)]
+            near = [x + j if x + j in self.inside else None for j in (-2, -1, 1, 2)]
+            dx = [central(*(None if j is None else u(c, j) for j in near)) for c in range(3)]
+            g11 = dx[0] + slope_x * dr[0]
+            parts = (
+                lame * (g11 + slope_y * dr[1] + stretch * dr[2]) + (shear + shear) * g11,
+                shear * (slope_y * dr[0] + dx[1] + slope_x * dr[1]),
+                shear * (stretch * dr[0] + dx[2] + slope_x * dr[2]),
+            )
+            for c in range(3):
+                ref[2 * c + k] = u(c, x)
+                ref[6 + 2 * c + k] = parts[c]
 
 
 def begin_kernel(*refs):
-    sources, (far_ref, near_ref, edge_ref, metric_ref) = refs[:4], refs[4:8]
-    u_ref, slope_ref, stretch_ref, moduli_ref = refs[8:12]
-    sems = refs[12]
+    sources, held, sems = refs[:5], refs[11:16], refs[16]
+    far_ref, near_ref, far_send, near_send, edge_ref, metric_ref = refs[5:11]
+    u_ref, slope_ref, stretch_ref, moduli_ref, buoyancy_ref = held
     copies = [
         pltpu.make_async_copy(source, target, sems.at[i])
-        for i, (source, target) in enumerate(zip(sources, refs[8:12]))
+        for i, (source, target) in enumerate(zip(sources, held))
     ]
     for copy in copies:
         copy.start()
@@ -203,9 +242,18 @@
         for x in range(x_count):
             metric_ref[m, x] = slabs[x]
         for k in range(2):
-            far_ref[comps * half + 2 * m + k] = slabs[k]
-            near_ref[comps * half + 2 * m + k] = slabs[x_count - 2 + k]
+            if m > 2:
+                far_send[6 + 2 * m + k] = slabs[k]
+                near_send[6 + 2 * m + k] = slabs[x_count - 2 + k]
         edge_ref[comps + m] = edge_message(lambda x: slabs[x], x_count, rows, y_count)
+    at = strided(buoyancy_ref, x_count, rows)
+    slabs = mirrored([at(x) for x in range(x_count)], odd)
+    push = edge_message(lambda x: slabs[x], x_count, rows, y_count) * (time_step**2 / 12.0)
+    u, window = halves(far_ref, near_ref, half), y_count // x_count
+    for far, ref in ((True, far_send), (False, near_send)):
+        side = Side(far, x_count)
+        side.send(ref, u, lambda m, x: metric_ref[m, x])
+        ref[16] = side.pack([push, *(edge_ref[comps + m] for m in range(3))], window)
 
 
 def rest_kernel(u_ref, v_ref, buoyancy_ref, before_far, before_near, push_ref):
@@ -222,16 +270,37 @@
             (before_far if x < half else before_near)[c * half + x % half] = value
 
 
-def corner_kernel(far, half, halo_ref, *refs):
-    corner_ref = refs[-1]
-    rows, y_count = halo_ref.shape[1:]
-    side = Side(far, 2 * half)
-    places = {x % side.x_count: x for x in side.outside}
+def corner_kernel(x_count, fixed, far_ref, near_ref, *refs):
+    corner_ref, terms = refs[-1], refs[0] if fixed else None
+    rows, y_count = far_ref.shape[1:]
+    places = {}
+    for far, ref in ((True, far_ref), (False, near_ref)):
+        side = Side(far, x_count)
+        places.update({x % x_count: (side, ref, x) for x in side.outside})
+
+    def load(c, place):
+        side, ref, x = places[place]
+        return side.halo(ref, c, x, terms) if c < 2 else side.modulus(ref, c - 2, x)
+
     for c in range(corner_ref.shape[0]):
         corner_ref[c] = edge_message(
-            lambda place: side.halo(halo_ref, c, places[place]),
-            side.x_count, rows, y_count, tuple(places),
-        )
+            lambda place: load(c, place), x_count, rows, y_count, tuple(places)
+        )
+
+
+def corner_tile(corner_in, c, window, has_left, has_right):
+    w = lanes_of(corner_in[0].shape[1:]) % window
+    return jnp.where(w < 8, corner_in[-1][c] * has_right, roll(corner_in[0][c], 8) * has_left)
+
+
+def beyond_change(value, window, x_count):
+    place = lanes_of(value.shape) // window
+
+    def near(k):
+        inside = (place + k < x_count) if k > 0 else (place + k >= 0)
+        return jnp.where(inside, 0.0, roll(value, -window * k))
+
+    return central(*(near(k) for k in (-2, -1, 1, 2)))
 
 
 def all_stresses(grads, lame, shear):
@@ -318,9 +387,11 @@
 
 
 def wide_kernel(
-    far, far_ref, near_ref, halo_ref, before_ref, metric_ref, push_ref, first_halo, s_x, s_o, e_s,
-    out_ref, out_edge,
+    far, fixed, send, far_ref, near_ref, halo_ref, before_ref, metric_ref, push_ref, first_halo, s_x,
+    s_o, e_s, *refs,
 ):
+    out_ref, send_ref, out_edge = refs[-3:]
+    terms = refs[0] if fixed else None
     x_count, rows, y_count = metric_ref.shape[1:]
     half, window = x_count // 2, y_count // x_count
     comps = s_x.shape[0]
@@ -330,7 +401,7 @@
     steps = (-2, -1, 1, 2)
 
     def u(c, x):
-        return inner(c, x) if 0 <= x < x_count else side.halo(halo_ref, c, x)
+        return inner(c, x) if 0 <= x < x_count else side.halo(halo_ref, c, x, terms)
 
     def beyond(x):
         return x < 0 if far else x >= x_count
@@ -359,19 +430,17 @@
         banded(jnp.concatenate([u(c, x) for x in side.outside], 0), band) for c in range(2)
     ]
     for place, x in enumerate(side.outside):
-        slope_x, slope_y, stretch, lame, shear = (
-            side.metric(first_halo, comps, m, x) for m in range(5)
-        )
-        dr = [layer_derivative(u(c, x)) for c in range(comps)]
-        dx = [central(*(u(c, x + k) for k in steps)) for c in range(comps)]
+        lame, shear = (side.modulus(first_halo, m, x) for m in range(2))
+        dx = [
+            central(*(u(c, x + k) if 0 <= x + k < x_count else None for k in steps))
+            for c in range(comps)
+        ]
         dy = [across[c][place * rows : (place + 1) * rows] for c in range(2)]
-        g11 = dx[0] + slope_x * dr[0]
-        pressure = lame * (g11 + dy[1] + slope_y * dr[1] + stretch * dr[2])
-        along_x[x] = [
-            pressure + (shear + shear) * g11,
-            shear * (dy[0] + slope_y * dr[0] + dx[1] + slope_x * dr[1]),
-            shear * (stretch * dr[0] + dx[2] + slope_x * dr[2]),
-        ]
+        values = [side.own_part(halo_ref, i, x, terms) for i in range(3)]
+        values[0] = values[0] + lame * (dx[0] + dy[1]) + (shear + shear) * dx[0]
+        values[1] = values[1] + shear * (dy[0] + dx[1])
+        values[2] = values[2] + shear * dx[2]
+        along_x[x] = values
 
     def across_of(i, x):
         return along_x[x][1] if i == 0 else others[x][i - 1]
@@ -379,10 +448,10 @@
     beside = []
     for i in range(comps):
         result = banded(jnp.concatenate([across_of(i, x) for x in side.inside], 0), band)
-        terms = edge_terms(e_s[i], window)
+        added = edge_terms(e_s[i], window)
         beside.append(
             {
-                x: result[k * rows : (k + 1) * rows] + edge_spread(terms, x, window)
+                x: result[k * rows : (k + 1) * rows] + edge_spread(added, x, window)
                 for k, x in enumerate(side.inside)
             }
         )
@@ -405,64 +474,102 @@
             messages[c] = moved if k == 0 else jnp.where(place == x, moved, messages[c])
     for c in range(comps):
         out_edge[c] = messages[c]
-
-
-def fix_kernel(far, sides, merge, *refs):
+    if send:
+        side.send(
+            send_ref,
+            lambda c, x: out_ref[c * half + x - side.inside[0]],
+            lambda m, x: metric_ref[m, x],
+        )
+
+
+def fix_kernel(sides, *refs):
     corner_in = refs[:sides]
-    first_halo, e_s, push_ref, in_ref, edge_ref = refs[sides : 5 + sides]
-    far_edge = refs[5 + sides] if merge else None
-    out_ref, *out_edge = refs[5 + sides + bool(merge) :]
+    first_far, first_near, e_s, push_ref = refs[sides : 4 + sides]
+    in_far, in_near, far_edge, near_edge = refs[4 + sides : 8 + sides]
+    out_far, out_near, *out_edge = refs[8 + sides :]
     x_count, rows, y_count = push_ref.shape
     half, window = x_count // 2, y_count // x_count
-    comps = edge_ref.shape[0]
-    side = Side(far, x_count)
+    comps = far_edge.shape[0]
     has_left, has_right = neighbours()
-    lane = lanes_of((rows, y_count))
-    place, w = lane // window, lane % window
+    place = lanes_of((rows, y_count)) // window
     lame, shear = 3, 4
     steps = (-2, -1, 1, 2)
 
-    corners = [
-        jnp.where(w < 8, corner_in[-1][c] * has_right, roll(corner_in[0][c], 8) * has_left)
+    corners = [corner_tile(corner_in, c, window, has_left, has_right) for c in range(2)]
+    terms = [edge_terms(corner, window) for corner in corners]
+    beside = [
+        edge_terms(e_s[shear] * beyond_change(corners[1], window, x_count), window),
+        edge_terms(e_s[lame] * beyond_change(corners[0], window, x_count), window),
+    ]
+    for c in range(comps):
+        message = jnp.where(place < half, far_edge[c], near_edge[c])
+        for far, first, in_ref, out_ref in (
+            (True, first_far, in_far, out_far),
+            (False, first_near, in_near, out_near),
+        ):
+            side = Side(far, x_count)
+            changes = {}
+            if c < 2:
+                changes = {
+                    x: side.modulus(first, c, x)
+                    * edge_spread(terms[1 - c], x % x_count, window)
+                    for x in side.outside
+                }
+            for k, x in enumerate(side.inside):
+                value = in_ref[c * half + k]
+                near = [changes.get(x + j) for j in steps]
+                if any(item is not None for item in near):
+                    change = central(*near) + edge_spread(beside[c], x, window)
+                    value = value + change * push_ref[x]
+                    message = jnp.where(place == x, roll(value, window * x + 4), message)
+                out_ref[c * half + k] = value
+        if out_edge:
+            out_edge[0][c] = message
+
+
+def partner_kernel(sides, edge_ref, *refs):
+    edge_in = refs[:sides]
+    metric_ref, first_far, first_near = refs[sides : 3 + sides]
+    moduli_in = refs[3 + sides : 3 + 2 * sides]
+    out_ref = refs[3 + 2 * sides]
+    x_count, _, y_count = metric_ref.shape[1:]
+    window = y_count // x_count
+    has_left, has_right = neighbours()
+    edges = [
+        edge_tile(edge_ref[c], edge_in[0][c], edge_in[-1][c], has_left, has_right, window)
         for c in range(2)
     ]
-    terms = [edge_terms(corner, window) for corner in corners]
-
-    def edge_change(corner):
-        def near(k):
-            if (k < 0) != far:
-                return None
-            inside = (place + k < x_count) if k > 0 else (place + k >= 0)
-            return jnp.where(inside, 0.0, roll(corner, -window * k))
-
-        return central(*(near(k) for k in steps))
-
+    lame, shear = (corner_tile(moduli_in, 2 + m, window, has_left, has_right) for m in range(2))
+    terms = [edge_terms(edge, window) for edge in edges]
     beside = [
-        edge_terms(e_s[shear] * edge_change(corners[1]), window),
-        edge_terms(e_s[lame] * edge_change(corners[0]), window),
+        edge_terms(shear * beyond_change(edges[1], window, x_count), window),
+        edge_terms(lame * beyond_change(edges[0], window, x_count), window),
     ]
-
-    for c in range(comps):
-        changes = {}
-        if c < 2:
+    for far, first in ((True, first_far), (False, first_near)):
+        side = Side(far, x_count)
+        added = {}
+        for c in range(2):
             changes = {
-                x: side.metric(first_halo, comps, lame if c == 0 else shear, x)
-                * edge_spread(terms[1 - c], x % x_count, window)
-                for x in side.outside
+                x: metric_ref[3 + c, x] * edge_spread(terms[1 - c], x, window)
+                for x in (side.inside[:2] if far else side.inside[-2:])
             }
-        message = edge_ref[c]
-        for k, x in enumerate(side.inside):
-            value = in_ref[c * half + k]
-            near = [changes.get(x + j) for j in steps]
-            if any(item is not None for item in near):
-                change = central(*near) + edge_spread(beside[c], x, window)
-                value = value + change * push_ref[x]
-                message = jnp.where(place == x, roll(value, window * x + 4), message)
-            out_ref[c * half + k] = value
-        if out_edge:
-            if merge:
-                message = jnp.where(place < half, far_edge[c], message)
-            out_edge[0][c] = message
+            for x in side.outside:
+                near = [changes.get(x + k) for k in (-2, -1, 1, 2)]
+                change = central(*near) + edge_spread(beside[c], x % x_count, window)
+                change = change * side.packed(first, 0, x, window)
+                added[c, x] = out_ref[side.slot(c, x)] = change
+        for x in side.outside:
+            slope_x, slope_y, stretch = (side.packed(first, 1 + m, x, window) for m in range(3))
+            own_lame, own_shear = (side.modulus(first, m, x) for m in range(2))
+            dr = [layer_derivative(added[c, x]) for c in range(2)]
+            near = [added.get((c, x + k)) for c in range(2) for k in (-2, -1, 1, 2)]
+            dx = [central(*near[:4]), central(*near[4:])]
+            g11 = dx[0] + slope_x * dr[0]
+            out_ref[side.slot(2, x)] = (
+                own_lame * (g11 + slope_y * dr[1]) + (own_shear + own_shear) * g11
+            )
+            out_ref[side.slot(3, x)] = own_shear * (slope_y * dr[0] + dx[1] + slope_x * dr[1])
+            out_ref[side.slot(4, x)] = own_shear * (stretch * dr[0])
 
 
 def sketch_kernel(moment, last, shape, *refs):
@@ -635,7 +742,7 @@
 HBM = pl.BlockSpec(memory_space=pltpu.MemorySpace.HBM)
 
 
-def call(kernel, outs, name, ins, specs=None, scratch=(), flops=0):
+def call(kernel, outs, ins, specs=None, scratch=(), flops=0):
     size = sum(math.prod(x.shape) * 4 for x in (*ins, *outs))
     return pl.pallas_call(
         kernel,
@@ -645,7 +752,6 @@
         scratch_shapes=list(scratch),
         compiler_params=pltpu.CompilerParams(vmem_limit_bytes=24 * 2**20),
         cost_estimate=pl.CostEstimate(flops=flops, bytes_accessed=size, transcendentals=0),
-        name=name,
     )(*ins)
 
 
@@ -690,82 +796,90 @@
         return f32(count, layers, y_count)
 
     u_flat = flat(displacement)
-    fields = [u_flat, flat(slopes), flat(stretch), flat(moduli)]
-    u_far, u_near, edge, metric = call(
+    fields = [
+        pltpu.with_memory_space_constraint(field, pltpu.MemorySpace.HBM)
+        for field in (u_flat, flat(slopes), flat(stretch), flat(moduli), flat(buoyancy))
+    ]
+    u_far, u_near, far_send, near_send, edge, metric = call(
         begin_kernel,
-        [slabs(comps * half + 10), slabs(comps * half + 10), slabs(comps + 5), f32(5, x_count, layers, y_count)],
-        "begin",
+        [
+            slabs(comps * half), slabs(comps * half), slabs(17), slabs(17), slabs(comps + 5),
+            f32(5, x_count, layers, y_count),
+        ],
         fields,
-        specs=[HBM] * 4,
+        specs=[HBM] * 5,
         scratch=[pltpu.VMEM(field.shape, jnp.float32) for field in fields]
-        + [pltpu.SemaphoreType.DMA((4,))],
+        + [pltpu.SemaphoreType.DMA((5,))],
     )
     before_far, before_near, push = call(
         rest_kernel,
         [slabs(comps * half), slabs(comps * half), slabs(x_count)],
-        "rest",
         [u_flat, flat(velocity), flat(buoyancy)],
     )
 
     sketch_rows = half * comps * (layers // 2)
     sketch = []
 
-    def half_step(far, moment, halo, first_halo, before, tokens, far_edge):
-        name = f"{'far' if far else 'near'}_{moment}"
-        last = moment == STEPS - 1
-        (corner,) = call(
-            partial(corner_kernel, far, half),
-            [slabs(2)],
-            f"corner_{name}",
-            [halo, *tokens],
-            specs=[VMEM] + [ANY] * len(tokens),
-        )
-        corner_in = along_y(corner)
-        value, own_edge = call(
-            partial(wide_kernel, far),
-            [slabs(comps * half), slabs(comps)],
-            f"wide_{name}",
-            [u_far, u_near, halo, before, metric, push, first_halo, s_x, s_o, e_s],
+    def half_step(far, moment, halo, first_halo, before, terms, token):
+        return call(
+            partial(wide_kernel, far, len(terms), moment < STEPS - 1),
+            [slabs(comps * half), slabs(12), slabs(comps)],
+            [
+                u_far, u_near, halo, before, metric, push, first_halo, s_x, s_o, e_s, *terms, *token,
+            ],
+            specs=[VMEM] * (10 + len(terms)) + [ANY] * len(token),
             flops=10_000_000,
         )
-        merge = [] if far_edge is None else [far_edge]
-        value, *own_edge = call(
-            partial(fix_kernel, far, sides, len(merge)),
-            [slabs(comps * half)] + ([] if last else [slabs(comps)]),
-            f"fix_{name}",
-            [*corner_in, first_halo, e_s, push, value, own_edge, *merge],
-        )
-        return value, (own_edge[0] if own_edge else None)
-
+
+    terms = []
     for moment in range(STEPS):
         last = moment == STEPS - 1
         if moment == 0:
-            far_halo = exchange(u_far, True)
-            near_halo = exchange(u_near, False)
+            far_halo = exchange(far_send, True)
+            near_halo = exchange(near_send, False)
         edge_in = along_y(edge)
         if moment == 0:
             first_edge, first_edge_in, first_far, first_near = edge, edge_in, far_halo, near_halo
         s_x, s_o, e_s = call(
             partial(tile_kernel, sides, comps),
             [f32(comps, x_count, layers, y_count), f32(3, x_count, layers, y_count), slabs(5)],
-            f"tile_{moment}",
             [u_far, u_near, edge, *edge_in, metric, first_edge, *first_edge_in],
             flops=20_000_000,
         )
-        next_far, far_edge = half_step(
-            True, moment, far_halo, first_far, before_far, [e_s, *(sketch or [push])], None
+        raw_far, far_send, far_edge = half_step(
+            True, moment, far_halo, first_far, before_far, terms, sketch or [push]
+        )
+        (corner,) = call(
+            partial(corner_kernel, x_count, len(terms)),
+            [slabs(2 if moment else 4)],
+            [far_halo, near_halo, *terms, raw_far],
+            specs=[VMEM] * (2 + len(terms)) + [ANY],
+        )
+        corner_in = along_y(corner)
+        if moment == 0:
+            moduli_in = corner_in
+        raw_near, near_send, near_edge = half_step(
+            False, moment, near_halo, first_near, before_near, terms, [raw_far]
         )
         if not last:
-            far_halo = exchange(next_far, True)
-        next_near, edge = half_step(
-            False, moment, near_halo, first_near, before_near, [next_far], far_edge
-        )
-        if not last:
-            near_halo = exchange(next_near, False)
+            far_halo = exchange(far_send, True)
+            near_halo = exchange(near_send, False)
+            terms = call(
+                partial(partner_kernel, sides),
+                [slabs(20)],
+                [edge, *edge_in, metric, first_far, first_near, *moduli_in],
+            )
+        next_far, next_near, *edge = call(
+            partial(fix_kernel, sides),
+            [slabs(comps * half), slabs(comps * half)] + ([] if last else [slabs(comps)]),
+            [
+                *corner_in, first_far, first_near, e_s, push, raw_far, raw_near, far_edge, near_edge,
+            ],
+        )
+        edge = None if last else edge[0]
         sketch = call(
             partial(sketch_kernel, moment, last, (comps, half, layers, y_count)),
             [f32(sketch_rows, width)],
-            f"sketch_{moment}",
             [next_far, next_near, before_far, before_near, probes, *sketch],
             scratch=[pltpu.VMEM((y_count, width), jnp.float32)],
         )
@@ -773,24 +887,19 @@
     (final,) = call(
         partial(finish_kernel, half, layers),
         [f32(comps, layers * x_count, y_count)],
-        "finish",
         [u_far, u_near],
     )
     final = final.reshape(displacement.shape)
 
     mine, theirs = butterfly(sketch[0], "gy", last=True)
     tall, packed = call(
-        gram_kernel,
-        [f32(sketch_rows, width), f32(width // 2 + SUB, width)],
-        "gram",
-        [mine, theirs],
+        gram_kernel, [f32(sketch_rows, width), f32(width // 2 + SUB, width)], [mine, theirs]
     )
     first, second = butterfly(packed, "gx", last=True)
     depth = comps * (layers // 2)
     basis, factor = call(
         partial(factor_kernel, math.sqrt(sketch_rows * n_x)),
         [f32(half, depth // n_y, width), f32(width, width)],
-        "factor",
         [first, second, tall.reshape(half, depth, width)],
     )
     return (final, basis, factor)
@@ -807,4 +916,5 @@
         P(None, "gy", None),
     )
     out_specs = (P(None, None, "gx", "gy"), P("gx", "gy", None), P())
+
     return jax.shard_map(shards, mesh=mesh, in_specs=in_specs, out_specs=out_specs, check_vma=False)

time: 87.8 us -> 81.1 us (0.924)
  waiting for transfers between devices: 40.1 us -> 33 us
  local copies, waits for them, and re-layouts: 3.8 us -> 0.23 us
  starting transfers between devices: 24.3 us -> 26.4 us
  Pallas kernels: 18.3 us -> 20.3 us
    ppermute x5, starting transfers between devices: 7.2 us -> 11 us  [butterfly(): other = lax.ppermute(value, axis, [(i, i ^ bit) for i in range(count)])]
    unnamed x14 -> x8, local copies, waits for them, and re-layouts: 3.8 us -> 0.23 us
    ppermute x12 -> x8, waiting for transfers between devices: 9.01 us -> 5.48 us  [along_y(): return [lax.ppermute(value, 'gy', [(0, 1), (1, 0)])]]
    ppermute x8, waiting for transfers between devices: 20.7 us -> 17.7 us  [exchange(): return lax.ppermute(value, 'gx', pairs + [(k, i) for i, k in pairs])]
    pallas_call x37 -> x32, Pallas kernels: 18.3 us -> 20.3 us  [call(): pl.pallas_call(kernel, out_shape=outs, in_specs=specs or [VMEM] * len(ins...]
    ppermute x8, starting transfers between devices: 16.1 us -> 14.5 us  [exchange(): return lax.ppermute(value, 'gx', pairs + [(k, i) for i, k in pairs])]
  transfers between devices with their start and end apart: 25 -> 21, of which waited for: 21 -> 17; matrix products, arithmetic and copies ran while one was open for 0% -> 0% of each run, Pallas kernels for 13% -> 15%
where the time goes in v5:
time: 81.1 us; the launch traced here: 80.9 us
  waiting for transfers between devices  33 us (41%)
  starting transfers between devices  26.4 us (33%)
  Pallas kernels  20.3 us (25%)
  between operations  0.97 us (1%)
    pallas_call x32, Pallas kernels, call(): pl.pallas_call(kernel, out_shape=outs, in_specs=specs or [VMEM] * len(ins...  20.3 us
    ppermute x8, waiting for transfers between devices, exchange(): return lax.ppermute(value, 'gx', pairs + [(k, i) for i, k in pairs])  17.7 us
    ppermute x8, starting transfers between devices, exchange(): return lax.ppermute(value, 'gx', pairs + [(k, i) for i, k in pairs])  14.5 us
    ppermute x5, starting transfers between devices, butterfly(): other = lax.ppermute(value, axis, [(i, i ^ bit) for i in range(count)])  11 us
    ppermute x5, waiting for transfers between devices, butterfly(): other = lax.ppermute(value, axis, [(i, i ^ bit) for i in range(count)])  9.8 us
    ppermute x8, waiting for transfers between devices, along_y(): return [lax.ppermute(value, 'gy', [(0, 1), (1, 0)])]  5.48 us
  transfers between devices with their start and end apart: 21, of which 17 were waited for; matrix products, arithmetic and copies ran while one was open for 0% of the time, Pallas kernels for 15%

profile of v5, /device:TPU:0, one launch (start us, length us, event | category | flops | bytes accessed | tf_op | source)
XLA Modules:
  0.0 80.9 jit_solution(16004717052018271875)
XLA Ops:
  0.7 2.2 %shard_map.94 = (f32[12,32,128]{2,1,0:T(8,128)S(1)}, f32[12,32,128]{2,1,0:T(8,128)S(1)}, f32[17,32,128]{2,1,0:T(8,128)S(1)}, f32[17,32,128]{2,1,0:T(8,128)S(1)},...) custom-call(f32[3,256,128]{2,1,0:T(8,128)} %bitcast.8, f32[2,256,128]{2,1,0:T(8,128)} %bitcast.15, ...), custom_call_target="tpu_custom_call" | custom-call | bytes 2916352 | tf_op jit(solution)/shard_map/pallas_call | solution.py:747
  3.5 5.8 %collective-permute-start.3 = (f32[17,32,128]{2,1,0:T(8,128)S(1)}, f32[17,32,128]{2,1,0:T(8,128)S(1)}, u32[]{:S(2)}, u32[]{:S(2)}) collective-permute-start(f32[17,32,128]{2,1,0:T(8,128)S(1)} %get-tuple-element.72), channel_id=1, source_target_pairs={{0,2},{4,6},{8,10},{12,14},{16,18},{20,22},{24,26},{28,30},{2,0},{... | collective-permute-start | bytes 835592 | tf_op jit(solution)/shard_map/ppermute | solution.py:785
  12.3 10.3 %collective-permute-done.3.halo_ref.first_halo.near_ref.refs_3_.refs_2_ = f32[17,32,128]{2,1,0:T(8,128)S(1)} collective-permute-done((f32[17,32,128]{2,1,0:T(8,128)S(1)}, f32[17,32,128]{2,1,0:T(8,128)S(1)}, u32[]{:S(2)}, u32[]{:S(2)}) %collective-permute-start.3) | collective-permute-done | bytes 278560 | tf_op jit(solution)/shard_map/ppermute | solution.py:785
  24.1 1.2 %collective-permute-done.5.refs_4_.refs_0_ = f32[4,32,128]{2,1,0:T(8,128)S(1)} collective-permute-done((f32[4,32,128]{2,1,0:T(8,128)S(1)}, f32[4,32,128]{2,1,0:T(8,128)S(1)}, u32[]{:S(2)}, u32[]{:S(2)}) %collective-permute-start.5) | collective-permute-done | bytes 65568 | tf_op jit(solution)/shard_map/ppermute | solution.py:789
  28.8 1.2 %collective-permute-done.4.near_ref.halo_ref = f32[12,32,128]{2,1,0:T(8,128)S(1)} collective-permute-done((f32[12,32,128]{2,1,0:T(8,128)S(1)}, f32[12,32,128]{2,1,0:T(8,128)S(1)}, u32[]{:S(2)}, u32[]{:S(2)}) %collective-permute-start.4) | collective-permute-done | bytes 196640 | tf_op jit(solution)/shard_map/ppermute | solution.py:785
  30.4 2.9 %collective-permute-start.11 = (f32[12,32,128]{2,1,0:T(8,128)S(1)}, f32[12,32,128]{2,1,0:T(8,128)S(1)}, u32[]{:S(2)}, u32[]{:S(2)}) collective-permute-start(f32[12,32,128]{2,1,0:T(8,128)S(1)} %get-tuple-element.97), channel_id=1, source_target_pairs={{0,2},{4,6},{8,10},{12,14},{16,18},{20,22},{24,26},{28,30},{2,0},{... | collective-permute-start | bytes 589832 | tf_op jit(solution)/shard_map/ppermute | solution.py:785
  33.5 1.2 %collective-permute-done.7.refs_0_ = f32[2,32,128]{2,1,0:T(8,128)S(1)} collective-permute-done((f32[2,32,128]{2,1,0:T(8,128)S(1)}, f32[2,32,128]{2,1,0:T(8,128)S(1)}, u32[]{:S(2)}, u32[]{:S(2)}) %collective-permute-start.7) | collective-permute-done | bytes 32800 | tf_op jit(solution)/shard_map/ppermute | solution.py:789
  37.5 0.9 %collective-permute-start.10 = (f32[12,32,128]{2,1,0:T(8,128)S(1)}, f32[12,32,128]{2,1,0:T(8,128)S(1)}, u32[]{:S(2)}, u32[]{:S(2)}) collective-permute-start(f32[12,32,128]{2,1,0:T(8,128)S(1)} %get-tuple-element.96), channel_id=1, source_target_pairs={{2,4},{6,8},{10,12},{14,16},{18,20},{22,24},{26,28},{4,2},{8,6},{1... | collective-permute-start | bytes 589832 | tf_op jit(solution)/shard_map/ppermute | solution.py:785
  38.3 3.6 %collective-permute-done.11.halo_ref.near_ref = f32[12,32,128]{2,1,0:T(8,128)S(1)} collective-permute-done((f32[12,32,128]{2,1,0:T(8,128)S(1)}, f32[12,32,128]{2,1,0:T(8,128)S(1)}, u32[]{:S(2)}, u32[]{:S(2)}) %collective-permute-start.11) | collective-permute-done | bytes 196640 | tf_op jit(solution)/shard_map/ppermute | solution.py:785
  42.4 2.2 %collective-permute-start.12 = (f32[12,32,128]{2,1,0:T(8,128)S(1)}, f32[12,32,128]{2,1,0:T(8,128)S(1)}, u32[]{:S(2)}, u32[]{:S(2)}) collective-permute-start(f32[12,32,128]{2,1,0:T(8,128)S(1)} %get-tuple-element.99), channel_id=1, source_target_pairs={{0,2},{4,6},{8,10},{12,14},{16,18},{20,22},{24,26},{28,30},{2,0},{... | collective-permute-start | bytes 589832 | tf_op jit(solution)/shard_map/ppermute | solution.py:785
  44.7 1.2 %collective-permute-done.13.refs_0_ = f32[2,32,128]{2,1,0:T(8,128)S(1)} collective-permute-done((f32[2,32,128]{2,1,0:T(8,128)S(1)}, f32[2,32,128]{2,1,0:T(8,128)S(1)}, u32[]{:S(2)}, u32[]{:S(2)}) %collective-permute-start.13) | collective-permute-done | bytes 32800 | tf_op jit(solution)/shard_map/ppermute | solution.py:789
  48.2 1.0 %shard_map.118 = (f32[12,32,128]{2,1,0:T(8,128)S(1)}, f32[12,32,128]{2,1,0:T(8,128)}, f32[3,32,128]{2,1,0:T(8,128)S(1)}) custom-call(f32[12,32,128]{2,1,0:T(8,128)S(1)} %get-tuple-element.103.refs_0_.far_ref, f32[12,32,128]{2,1,0:T(8,128)S(1)} %get-tuple-element.104.refs_1_.near_ref, f32[12,32,128]{2,1,0:T(8,128)S(1)} %collective-permute-done.10.halo_ref.far_ref, ...), custom_call_target="tpu_custom_call" | custom-call | flops 10000000 | bytes 3588096 | tf_op jit(solution)/shard_map/pallas_call | solution.py:747
  49.3 2.6 %collective-permute-done.12.near_ref.halo_ref = f32[12,32,128]{2,1,0:T(8,128)S(1)} collective-permute-done((f32[12,32,128]{2,1,0:T(8,128)S(1)}, f32[12,32,128]{2,1,0:T(8,128)S(1)}, u32[]{:S(2)}, u32[]{:S(2)}) %collective-permute-start.12) | collective-permute-done | bytes 196640 | tf_op jit(solution)/shard_map/ppermute | solution.py:785
  52.1 1.0 %shard_map.120 = (f32[12,32,128]{2,1,0:T(8,128)S(1)}, f32[12,32,128]{2,1,0:T(8,128)}, f32[3,32,128]{2,1,0:T(8,128)S(1)}) custom-call(f32[12,32,128]{2,1,0:T(8,128)S(1)} %get-tuple-element.103.refs_0_.far_ref, f32[12,32,128]{2,1,0:T(8,128)S(1)} %get-tuple-element.104.refs_1_.near_ref, f32[12,32,128]{2,1,0:T(8,128)S(1)} %collective-permute-done.12.near_ref.halo_ref, ...), custom_call_target="tpu_custom_call" | custom-call | flops 10000000 | bytes 3686400 | tf_op jit(solution)/shard_map/pallas_call | solution.py:747
  54.3 1.0 %collective-permute-done.16.second_ref = f32[192,128]{1,0:T(8,128)S(1)} collective-permute-done((f32[192,128]{1,0:T(8,128)S(1)}, f32[192,128]{1,0:T(8,128)S(1)}, u32[]{:S(2)}, u32[]{:S(2)}) %collective-permute-start.16) | collective-permute-done | bytes 98336 | tf_op jit(solution)/shard_map/ppermute | solution.py:765
  55.7 2.5 %collective-permute-start.17 = (f32[72,128]{1,0:T(8,128)S(1)}, f32[72,128]{1,0:T(8,128)S(1)}, u32[]{:S(2)}, u32[]{:S(2)}) collective-permute-start(f32[72,128]{1,0:T(8,128)S(1)} %get-tuple-element.115), channel_id=1, source_target_pairs={{0,2},{2,0},{4,6},{6,4},{8,10},{10,8},{12,14},{14,12},{16,18},{18,... | collective-permute-start | bytes 110600 | tf_op jit(solution)/shard_map/ppermute | solution.py:765
  58.2 2.0 %collective-permute-done.17 = f32[72,128]{1,0:T(8,128)S(1)} collective-permute-done((f32[72,128]{1,0:T(8,128)S(1)}, f32[72,128]{1,0:T(8,128)S(1)}, u32[]{:S(2)}, u32[]{:S(2)}) %collective-permute-start.17) | collective-permute-done | bytes 36896 | tf_op jit(solution)/shard_map/ppermute | solution.py:765
  60.2 3.9 %collective-permute-done.18 = f32[72,128]{1,0:T(8,128)S(1)} collective-permute-done((f32[72,128]{1,0:T(8,128)S(1)}, f32[72,128]{1,0:T(8,128)S(1)}, u32[]{:S(2)}, u32[]{:S(2)}) %collective-permute-start.18) | collective-permute-done | bytes 36896 | tf_op jit(solution)/shard_map/ppermute | solution.py:765
  64.1 4.9 %collective-permute-start.19 = (f32[72,128]{1,0:T(8,128)S(1)}, f32[72,128]{1,0:T(8,128)S(1)}, u32[]{:S(2)}, u32[]{:S(2)}) collective-permute-start(f32[72,128]{1,0:T(8,128)S(1)} %add.10), channel_id=1, source_target_pairs={{0,8},{2,10},{4,12},{6,14},{8,0},{10,2},{12,4},{14,6},{16,24},{18,... | collective-permute-start | bytes 110600 | tf_op jit(solution)/shard_map/ppermute | solution.py:765
  69.1 1.9 %collective-permute-done.19 = f32[72,128]{1,0:T(8,128)S(1)} collective-permute-done((f32[72,128]{1,0:T(8,128)S(1)}, f32[72,128]{1,0:T(8,128)S(1)}, u32[]{:S(2)}, u32[]{:S(2)}) %collective-permute-start.19) | collective-permute-done | bytes 36896 | tf_op jit(solution)/shard_map/ppermute | solution.py:765
  71.0 3.1 %collective-permute-start.20 = (f32[72,128]{1,0:T(8,128)S(1)}, f32[72,128]{1,0:T(8,128)S(1)}, u32[]{:S(2)}, u32[]{:S(2)}) collective-permute-start(f32[72,128]{1,0:T(8,128)S(1)} %add.11.first_ref), channel_id=1, source_target_pairs={{0,16},{2,18},{4,20},{6,22},{8,24},{10,26},{12,28},{14,30},{16,0},... | collective-permute-start | bytes 110600 | tf_op jit(solution)/shard_map/ppermute | solution.py:765
  74.1 1.0 %shard_map.122 = f32[3,256,128]{2,1,0:T(8,128)} custom-call(f32[12,32,128]{2,1,0:T(8,128)S(1)} %get-tuple-element.113.far_ref.refs_0_, f32[12,32,128]{2,1,0:T(8,128)S(1)} %get-tuple-element.114.near_ref.refs_1_), custom_call_target="tpu_custom_call" | custom-call | bytes 786432 | tf_op jit(solution)/shard_map/pallas_call | solution.py:747
  75.1 1.0 %collective-permute-done.20.second_ref = f32[72,128]{1,0:T(8,128)S(1)} collective-permute-done((f32[72,128]{1,0:T(8,128)S(1)}, f32[72,128]{1,0:T(8,128)S(1)}, u32[]{:S(2)}, u32[]{:S(2)}) %collective-permute-start.20) | collective-permute-done | bytes 36896 | tf_op jit(solution)/shard_map/ppermute | solution.py:765
  76.1 4.8 %shard_map.125 = (f32[4,24,128]{2,1,0:T(8,128)}, f32[128,128]{1,0:T(8,128)}) custom-call(f32[72,128]{1,0:T(8,128)S(1)} %add.11.first_ref, f32[72,128]{1,0:T(8,128)S(1)} %collective-permute-done.20.second_ref, f32[4,48,128]{2,1,0:T(8,128)S(1)} %bitcast.13), custom_call_target="tpu_custom_call" | custom-call | bytes 286720 | tf_op jit(solution)/shard_map/pallas_call | solution.py:747
  (61 shorter events, 16.5 us)
Async XLA Ops:
  0.6 8.6 %copy-start.1 = (f32[3,32,8,128]{3,2,1,0:T(8,128)S(1)}, f32[3,32,8,128]{3,2,1,0:T(8,128)}, u32[]{:S(2)}) copy-start(f32[3,32,8,128]{3,2,1,0:T(8,128)} %param.7) | copy-start | bytes 1179652
  0.6 8.6 %copy-start.2 = (f32[32,8,128]{2,1,0:T(8,128)S(1)}, f32[32,8,128]{2,1,0:T(8,128)}, u32[]{:S(2)}) copy-start(f32[32,8,128]{2,1,0:T(8,128)} %param.12) | copy-start | bytes 393220
  0.7 8.6 %copy-start.3 = (f32[3,32,8,128]{3,2,1,0:T(8,128)S(1)}, f32[3,32,8,128]{3,2,1,0:T(8,128)}, u32[]{:S(2)}) copy-start(f32[3,32,8,128]{3,2,1,0:T(8,128)} %param.8) | copy-start | bytes 1179652
  2.8 8.3 %collective-permute-start = (f32[17,32,128]{2,1,0:T(8,128)S(1)}, f32[17,32,128]{2,1,0:T(8,128)S(1)}, u32[]{:S(2)}, u32[]{:S(2)}) collective-permute-start(f32[17,32,128]{2,1,0:T(8,128)S(1)} %get-tuple-element.63), channel_id=1, source_target_pairs={{2,4},{6,8},{10,12},{14,16},{18,20},{22,24},{26,28},{4,2},{8,6},{1... | collective-permute-start | bytes 835592 | tf_op jit(solution)/shard_map/ppermute | solution.py:785
  3.5 19.1 %collective-permute-start.3 = (f32[17,32,128]{2,1,0:T(8,128)S(1)}, f32[17,32,128]{2,1,0:T(8,128)S(1)}, u32[]{:S(2)}, u32[]{:S(2)}) collective-permute-start(f32[17,32,128]{2,1,0:T(8,128)S(1)} %get-tuple-element.72), channel_id=1, source_target_pairs={{0,2},{4,6},{8,10},{12,14},{16,18},{20,22},{24,26},{28,30},{2,0},{... | collective-permute-start | bytes 835592 | tf_op jit(solution)/shard_map/ppermute | solution.py:785
  9.3 1.3 %collective-permute-start.1 = (f32[8,32,128]{2,1,0:T(8,128)S(1)}, f32[8,32,128]{2,1,0:T(8,128)S(1)}, u32[]{:S(2)}, u32[]{:S(2)}) collective-permute-start(f32[8,32,128]{2,1,0:T(8,128)S(1)} %get-tuple-element.67.refs_2_.refs_5_.edge_ref), channel_id=1, source_target_pairs={{0,1},{1,0},{2,3},{3,2},{4,5},{5,4},{6,7},{7,6},{8,9},{9,8},{10,11... | collective-permute-start | bytes 393224 | tf_op jit(solution)/shard_map/ppermute | solution.py:789
  11.7 16.0 %collective-permute-start.2 = (f32[12,32,128]{2,1,0:T(8,128)S(1)}, f32[12,32,128]{2,1,0:T(8,128)S(1)}, u32[]{:S(2)}, u32[]{:S(2)}) collective-permute-start(f32[12,32,128]{2,1,0:T(8,128)S(1)} %get-tuple-element.71), channel_id=1, source_target_pairs={{2,4},{6,8},{10,12},{14,16},{18,20},{22,24},{26,28},{4,2},{8,6},{1... | collective-permute-start | bytes 589832 | tf_op jit(solution)/shard_map/ppermute | solution.py:785
  23.1 6.9 %collective-permute-start.4 = (f32[12,32,128]{2,1,0:T(8,128)S(1)}, f32[12,32,128]{2,1,0:T(8,128)S(1)}, u32[]{:S(2)}, u32[]{:S(2)}) collective-permute-start(f32[12,32,128]{2,1,0:T(8,128)S(1)} %get-tuple-element.75), channel_id=1, source_target_pairs={{0,2},{4,6},{8,10},{12,14},{16,18},{20,22},{24,26},{28,30},{2,0},{... | collective-permute-start | bytes 589832 | tf_op jit(solution)/shard_map/ppermute | solution.py:785
  24.0 1.3 %collective-permute-start.5 = (f32[4,32,128]{2,1,0:T(8,128)S(1)}, f32[4,32,128]{2,1,0:T(8,128)S(1)}, u32[]{:S(2)}, u32[]{:S(2)}) collective-permute-start(f32[4,32,128]{2,1,0:T(8,128)S(1)} %shard_map.99), channel_id=1, source_target_pairs={{0,1},{1,0},{2,3},{3,2},{4,5},{5,4},{6,7},{7,6},{8,9},{9,8},{10,11... | collective-permute-start | bytes 196616 | tf_op jit(solution)/shard_map/ppermute | solution.py:789
  25.8 1.3 %collective-permute-start.6 = (f32[3,32,128]{2,1,0:T(8,128)S(1)}, f32[3,32,128]{2,1,0:T(8,128)S(1)}, u32[]{:S(2)}, u32[]{:S(2)}) collective-permute-start(f32[3,32,128]{2,1,0:T(8,128)S(1)} %get-tuple-element.81.refs_2_.edge_ref), channel_id=1, source_target_pairs={{0,1},{1,0},{2,3},{3,2},{4,5},{5,4},{6,7},{7,6},{8,9},{9,8},{10,11... | collective-permute-start | bytes 147464 | tf_op jit(solution)/shard_map/ppermute | solution.py:789
  28.1 8.9 %collective-permute-start.8 = (f32[12,32,128]{2,1,0:T(8,128)S(1)}, f32[12,32,128]{2,1,0:T(8,128)S(1)}, u32[]{:S(2)}, u32[]{:S(2)}) collective-permute-start(f32[12,32,128]{2,1,0:T(8,128)S(1)} %get-tuple-element.91), channel_id=1, source_target_pairs={{2,4},{6,8},{10,12},{14,16},{18,20},{22,24},{26,28},{4,2},{8,6},{1... | collective-permute-start | bytes 589832 | tf_op jit(solution)/shard_map/ppermute | solution.py:785
  30.4 11.5 %collective-permute-start.11 = (f32[12,32,128]{2,1,0:T(8,128)S(1)}, f32[12,32,128]{2,1,0:T(8,128)S(1)}, u32[]{:S(2)}, u32[]{:S(2)}) collective-permute-start(f32[12,32,128]{2,1,0:T(8,128)S(1)} %get-tuple-element.97), channel_id=1, source_target_pairs={{0,2},{4,6},{8,10},{12,14},{16,18},{20,22},{24,26},{28,30},{2,0},{... | collective-permute-start | bytes 589832 | tf_op jit(solution)/shard_map/ppermute | solution.py:785
  33.4 1.3 %collective-permute-start.7 = (f32[2,32,128]{2,1,0:T(8,128)S(1)}, f32[2,32,128]{2,1,0:T(8,128)S(1)}, u32[]{:S(2)}, u32[]{:S(2)}) collective-permute-start(f32[2,32,128]{2,1,0:T(8,128)S(1)} %shard_map.105), channel_id=1, source_target_pairs={{0,1},{1,0},{2,3},{3,2},{4,5},{5,4},{6,7},{7,6},{8,9},{9,8},{10,11... | collective-permute-start | bytes 98312 | tf_op jit(solution)/shard_map/ppermute | solution.py:789
  35.1 1.3 %collective-permute-start.9 = (f32[3,32,128]{2,1,0:T(8,128)S(1)}, f32[3,32,128]{2,1,0:T(8,128)S(1)}, u32[]{:S(2)}, u32[]{:S(2)}) collective-permute-start(f32[3,32,128]{2,1,0:T(8,128)S(1)} %get-tuple-element.92.refs_2_.edge_ref), channel_id=1, source_target_pairs={{0,1},{1,0},{2,3},{3,2},{4,5},{5,4},{6,7},{7,6},{8,9},{9,8},{10,11... | collective-permute-start | bytes 147464 | tf_op jit(solution)/shard_map/ppermute | solution.py:789
  37.5 10.7 %collective-permute-start.10 = (f32[12,32,128]{2,1,0:T(8,128)S(1)}, f32[12,32,128]{2,1,0:T(8,128)S(1)}, u32[]{:S(2)}, u32[]{:S(2)}) collective-permute-start(f32[12,32,128]{2,1,0:T(8,128)S(1)} %get-tuple-element.96), channel_id=1, source_target_pairs={{2,4},{6,8},{10,12},{14,16},{18,20},{22,24},{26,28},{4,2},{8,6},{1... | collective-permute-start | bytes 589832 | tf_op jit(solution)/shard_map/ppermute | solution.py:785
  42.4 9.5 %collective-permute-start.12 = (f32[12,32,128]{2,1,0:T(8,128)S(1)}, f32[12,32,128]{2,1,0:T(8,128)S(1)}, u32[]{:S(2)}, u32[]{:S(2)}) collective-permute-start(f32[12,32,128]{2,1,0:T(8,128)S(1)} %get-tuple-element.99), channel_id=1, source_target_pairs={{0,2},{4,6},{8,10},{12,14},{16,18},{20,22},{24,26},{28,30},{2,0},{... | collective-permute-start | bytes 589832 | tf_op jit(solution)/shard_map/ppermute | solution.py:785
  44.6 1.3 %collective-permute-start.13 = (f32[2,32,128]{2,1,0:T(8,128)S(1)}, f32[2,32,128]{2,1,0:T(8,128)S(1)}, u32[]{:S(2)}, u32[]{:S(2)}) collective-permute-start(f32[2,32,128]{2,1,0:T(8,128)S(1)} %shard_map.114), channel_id=1, source_target_pairs={{0,1},{1,0},{2,3},{3,2},{4,5},{5,4},{6,7},{7,6},{8,9},{9,8},{10,11... | collective-permute-start | bytes 98312 | tf_op jit(solution)/shard_map/ppermute | solution.py:789
  46.4 1.3 %collective-permute-start.14 = (f32[3,32,128]{2,1,0:T(8,128)S(1)}, f32[3,32,128]{2,1,0:T(8,128)S(1)}, u32[]{:S(2)}, u32[]{:S(2)}) collective-permute-start(f32[3,32,128]{2,1,0:T(8,128)S(1)} %get-tuple-element.105.refs_2_), channel_id=1, source_target_pairs={{0,1},{1,0},{2,3},{3,2},{4,5},{5,4},{6,7},{7,6},{8,9},{9,8},{10,11... | collective-permute-start | bytes 147464 | tf_op jit(solution)/shard_map/ppermute | solution.py:789
  52.0 1.3 %collective-permute-start.15 = (f32[2,32,128]{2,1,0:T(8,128)S(1)}, f32[2,32,128]{2,1,0:T(8,128)S(1)}, u32[]{:S(2)}, u32[]{:S(2)}) collective-permute-start(f32[2,32,128]{2,1,0:T(8,128)S(1)} %shard_map.119), channel_id=1, source_target_pairs={{0,1},{1,0},{2,3},{3,2},{4,5},{5,4},{6,7},{7,6},{8,9},{9,8},{10,11... | collective-permute-start | bytes 98312 | tf_op jit(solution)/shard_map/ppermute | solution.py:789
  53.9 1.4 %collective-permute-start.16 = (f32[192,128]{1,0:T(8,128)S(1)}, f32[192,128]{1,0:T(8,128)S(1)}, u32[]{:S(2)}, u32[]{:S(2)}) collective-permute-start(f32[192,128]{1,0:T(8,128)S(1)} %shard_map.123.first_ref), channel_id=1, source_target_pairs={{0,1},{1,0},{2,3},{3,2},{4,5},{5,4},{6,7},{7,6},{8,9},{9,8},{10,11... | collective-permute-start | bytes 294920 | tf_op jit(solution)/shard_map/ppermute | solution.py:765
  55.7 4.5 %collective-permute-start.17 = (f32[72,128]{1,0:T(8,128)S(1)}, f32[72,128]{1,0:T(8,128)S(1)}, u32[]{:S(2)}, u32[]{:S(2)}) collective-permute-start(f32[72,128]{1,0:T(8,128)S(1)} %get-tuple-element.115), channel_id=1, source_target_pairs={{0,2},{2,0},{4,6},{6,4},{8,10},{10,8},{12,14},{14,12},{16,18},{18,... | collective-permute-start | bytes 110600 | tf_op jit(solution)/shard_map/ppermute | solution.py:765
  60.2 4.0 %collective-permute-start.18 = (f32[72,128]{1,0:T(8,128)S(1)}, f32[72,128]{1,0:T(8,128)S(1)}, u32[]{:S(2)}, u32[]{:S(2)}) collective-permute-start(f32[72,128]{1,0:T(8,128)S(1)} %add.9), channel_id=1, source_target_pairs={{0,4},{2,6},{4,0},{6,2},{8,12},{10,14},{12,8},{14,10},{16,20},{18,... | collective-permute-start | bytes 110600 | tf_op jit(solution)/shard_map/ppermute | solution.py:765
  64.1 6.9 %collective-permute-start.19 = (f32[72,128]{1,0:T(8,128)S(1)}, f32[72,128]{1,0:T(8,128)S(1)}, u32[]{:S(2)}, u32[]{:S(2)}) collective-permute-start(f32[72,128]{1,0:T(8,128)S(1)} %add.10), channel_id=1, source_target_pairs={{0,8},{2,10},{4,12},{6,14},{8,0},{10,2},{12,4},{14,6},{16,24},{18,... | collective-permute-start | bytes 110600 | tf_op jit(solution)/shard_map/ppermute | solution.py:765
  71.0 5.1 %collective-permute-start.20 = (f32[72,128]{1,0:T(8,128)S(1)}, f32[72,128]{1,0:T(8,128)S(1)}, u32[]{:S(2)}, u32[]{:S(2)}) collective-permute-start(f32[72,128]{1,0:T(8,128)S(1)} %add.11.first_ref), channel_id=1, source_target_pairs={{0,16},{2,18},{4,20},{6,22},{8,24},{10,26},{12,28},{14,30},{16,0},... | collective-permute-start | bytes 110600 | tf_op jit(solution)/shard_map/ppermute | solution.py:765
  (1 other events, 0.9 us)
